TPU v7x, 256 devices: a whole 4x4x8 slice. The times are simulated.
256 devices in a mesh: ta: 4 (over y), ha: 16 (over x, z_hi, core), wa: 4 (over z_lo).
Axes of the slice: x: 4, y: 4, z: 8 (z_hi: 2, z_lo: 4; z = z_hi * 4 + z_lo), core: 2. Of those that a mesh axis runs over, the one named last changes fastest.
Arguments:
- latents: bfloat16 [8, 256, 128, 256], P('ta', 'ha', 'wa'), may hold values from -6 to 6
- norm_gain: float32 [256], replicated, may hold values from 0.1 to 1.9
- conv_weight: bfloat16 [3, 3, 3, 256, 256], replicated, may hold values from -0.078125 to 0.078125
- qkv_weight: bfloat16 [1024, 16, 3, 128], P(None, ('ta', 'wa')), may hold values from -2.7 to 2.7
Outputs:
- block_out: bfloat16 [8, 256, 128, 256], P('ta', 'ha', 'wa')
- attended: bfloat16 [8, 128, 64, 16, 128], P(None, 'ha', None, ('ta', 'wa'))
All inputs are finite; a program needn't handle non-finite values.
Results may differ from a plain program's by a relative error of at most 0.0062.
Values may be sent and summed in bfloat16 or wider, within the bound.
No kernel may reach another device: no remote copies, remote signals or barrier semaphores. Data moves between devices by JAX's collectives and lax.ppermute only.
A program may use at most 128 MiB of HBM per device.

v0:
```python
import jax
import jax.numpy as jnp
from jax import lax
from jax.sharding import PartitionSpec as P

WIN = 4


def extended(cells, sides, width):
    for axis, dim in sides:
        count = lax.axis_size(axis)
        ends = count - 1
        head = lax.slice_in_dim(cells, 0, width, axis=dim)
        tail = lax.slice_in_dim(cells, cells.shape[dim] - width, cells.shape[dim], axis=dim)
        cells = jnp.concatenate(
            [
                lax.ppermute(tail, axis, [(i, (i + 1) % count) for i in range(ends)]),
                cells,
                lax.ppermute(head, axis, [((i + 1) % count, i) for i in range(ends)]),
            ],
            axis=dim,
        )
    return cells


def local(latents, norm_gain, conv_weight, qkv_weight):
    t_dev, h_dev, w_dev, channels = latents.shape
    rows_dev = h_dev // 2
    cols_dev = w_dev // 2
    latent_f32 = latents.astype(jnp.float32)
    scale_rms = lax.rsqrt(jnp.mean(latent_f32 * latent_f32, axis=-1, keepdims=True) + 1e-06)
    normed = jax.nn.silu(latent_f32 * scale_rms * norm_gain).astype(jnp.bfloat16)
    padded = extended(normed, (("ta", 0), ("ha", 1), ("wa", 2)), 1)
    conv_out = lax.conv_general_dilated(
        padded[None],
        conv_weight,
        (1, 1, 1),
        "VALID",
        dimension_numbers=("NDHWC", "DHWIO", "NDHWC"),
        preferred_element_type=jnp.float32,
    )[0]
    block_out = (latent_f32 + conv_out).astype(jnp.bfloat16)
    patches = (
        block_out.reshape(t_dev, rows_dev, 2, cols_dev, 2, channels)
        .transpose(0, 1, 3, 2, 4, 5)
        .reshape(t_dev * rows_dev * cols_dev, 4 * channels)
    )
    width_in, head_dev, qkv_count, head_size = qkv_weight.shape
    every_head = lax.all_gather(qkv_weight, ("ta", "wa"), axis=1, tiled=True)
    projected = jnp.dot(
        patches, every_head.reshape(width_in, -1), preferred_element_type=jnp.float32
    ).astype(jnp.bfloat16)
    gathered = lax.all_to_all(projected, ("ta", "wa"), split_axis=1, concat_axis=0, tiled=True)
    n_time = lax.axis_size("ta")
    n_width = lax.axis_size("wa")
    frames = n_time * t_dev
    patch_cols = n_width * cols_dev
    qkv_rows = gathered.reshape(
        n_time, n_width, t_dev, rows_dev, cols_dev, head_dev, qkv_count, head_size
    )
    qkv_rows = qkv_rows.transpose(0, 2, 3, 1, 4, 5, 6, 7).reshape(
        frames, rows_dev, patch_cols, head_dev, qkv_count, head_size
    )
    queries = qkv_rows[:, :, :, :, 0, :]
    key_value = qkv_rows[:, :, :, :, 1:, :].reshape(
        frames, rows_dev, patch_cols, head_dev, 2 * head_size
    )
    kv_rim = extended(key_value, (("ha", 1),), WIN)
    row_base = lax.axis_index("ha") * rows_dev
    total_rows = rows_dev * lax.axis_size("ha")

    def attend(block_idx):
        q_block = lax.dynamic_slice_in_dim(queries, block_idx * WIN, WIN, 1)
        kv_block = lax.dynamic_slice_in_dim(kv_rim, block_idx * WIN, 3 * WIN, 1)
        key_part = kv_block[..., :head_size]
        value_part = kv_block[..., head_size:]
        scores = jnp.einsum(
            "tiahd,tjbhd->thiajb", q_block, key_part, preferred_element_type=jnp.float32
        ) * head_size ** (-0.5)
        q_row = jnp.arange(WIN, dtype=jnp.int32)[:, None]
        k_row = jnp.arange(3 * WIN, dtype=jnp.int32)[None, :] - WIN
        k_global = row_base + block_idx * WIN + k_row
        allowed = (jnp.abs(q_row - k_row) <= WIN) & (k_global >= 0) & (k_global < total_rows)
        scores = jnp.where(allowed[None, None, :, None, :, None], scores, -1e30)
        row_max = jnp.max(scores, axis=(4, 5), keepdims=True)
        exp_scores = jnp.exp(scores - row_max)
        probs = (exp_scores / jnp.sum(exp_scores, axis=(4, 5), keepdims=True)).astype(jnp.bfloat16)
        result = jnp.einsum(
            "thiajb,tjbhd->tiahd", probs, value_part, preferred_element_type=jnp.float32
        )
        return result.astype(jnp.bfloat16)

    blocks = lax.map(attend, jnp.arange(rows_dev // WIN, dtype=jnp.int32))
    attended = blocks.transpose(1, 0, 2, 3, 4, 5).reshape(
        frames, rows_dev, patch_cols, head_dev, head_size
    )
    return (block_out, attended)


def solution(mesh):
    return jax.shard_map(
        local,
        mesh=mesh,
        in_specs=(P("ta", "ha", "wa", None), P(), P(), P(None, ("ta", "wa"), None, None)),
        out_specs=(P("ta", "ha", "wa", None), P(None, "ha", None, ("ta", "wa"), None)),
        check_vma=False,
    )
```

profile of v0, /device:TPU:3, one launch (start us, length us, event | category | flops | bytes accessed | tf_op | source)
XLA Modules:
  0.0 499.1 jit_solution(14405158100643521824)
XLA Ops:
  7.9 1.7 fusion.27
  9.7 1.5 fusion.34
  11.2 3.2 collective-permute-start
  15.8 3.7 collective-permute-done
  19.4 3.8 collective-permute-done.1
  23.5 10.5 %collective-permute-start.2 = (bf16[4,1,32,256]{3,1,2,0:T(2,128)(2,1)S(1)}, bf16[4,1,32,256]{3,1,2,0:T(2,128)(2,1)S(1)}, u32[]{:S(2)}, u32[]{:S(2)}) collective-permute-start(bf16[4,1,32,256]{3,1,2,0:T(2,128)(2,1)S(1)} %get-tuple-element.106), channel_id=1, source_target_pairs={{0,4},{4,8},{8,12},{12,16},{16,20},{20,24},{24,28},{28,32},{32,36}... | collective-permute-start | bytes 196616 | tf_op jit(solution)/shard_map/ppermute | solution.py:17
  34.0 1.9 collective-permute-start.3
  35.9 4.1 collective-permute-done.2
  40.0 9.0 %collective-permute-done.3 = bf16[4,1,32,256]{3,1,2,0:T(2,128)(2,1)S(1)} collective-permute-done((bf16[4,1,32,256]{3,1,2,0:T(2,128)(2,1)S(1)}, bf16[4,1,32,256]{3,1,2,0:T(2,128)(2,1)S(1)}, u32[]{:S(2)}, u32[]{:S(2)}) %collective-permute-start.3) | collective-permute-done | bytes 65568 | tf_op jit(solution)/shard_map/ppermute | solution.py:19
  49.0 4.6 collective-permute-start.4
  55.9 6.5 %collective-permute-done.5 = bf16[4,18,1,256]{3,1,2,0:T(8,128)(2,1)S(1)} collective-permute-done((bf16[4,18,1,256]{3,1,2,0:T(8,128)(2,1)S(1)}, bf16[4,18,1,256]{3,1,2,0:T(8,128)(2,1)S(1)}, u32[]{:S(2)}, u32[]{:S(2)}) %collective-permute-start.5) | collective-permute-done | bytes 36896 | tf_op jit(solution)/shard_map/ppermute | solution.py:19
  65.2 5.0 %fusion.24 = f32[2,16,8,5,256]{4,2,3,1,0:T(8,128)S(1)} fusion(bf16[3,3,3,256,256]{4,3,2,1,0:T(8,128)(2,1)S(1)} %copy-done, bf16[4,18,1,7,2,256]{5,3,4,1,0,2:T(8,128)(2,1)S(1)} %slice.56, bf16[4,18,1,8,5,256]{5,3,4,1,0,2:T(8,128)(2,1)S(1)} %copy.38, pred[8,5]{0,1:T(8,128)(4,1)S(1)} %copy-done.8), kind=kOutput, calls=%fused_computation.42 | convolution fusion | flops 4536369152 | bytes 6840360 | tf_op jit(solution)/shard_map/conv_general_dilated | solution.py:34
  73.0 217.5 %all-gather.2.cloned.1.call-done = bf16[1024,16,3,128]{3,0,2,1:T(8,128)(2,1)} async-done(((bf16[1024,1,3,128]{3,0,2,1:T(8,128)(2,1)}), bf16[1024,16,3,128]{3,0,2,1:T(8,128)(2,1)}) %all-gather.2.cloned.1.call-update) | async-done | bytes 12582928 | tf_op jit(solution)/shard_map/all_gather | solution.py:49
  290.5 15.7 %copy.41 = bf16[1024,16,3,128]{0,3,2,1:T(8,128)(2,1)} copy(bf16[1024,16,3,128]{3,0,2,1:T(8,128)(2,1)} %all-gather.2.cloned.1.call-done) | data formatting | bytes 25165824 | tf_op jit(solution)/shard_map/all_gather | solution.py:49
  306.3 8.2 %convolution_convert_fusion = bf16[256,6144]{1,0:T(8,128)(2,1)S(1)} fusion(bf16[256,1024]{1,0:T(8,128)(2,1)} %reshape.155, bf16[1024,6144]{0,1:T(8,128)(2,1)} %bitcast.102), kind=kOutput, calls=%fused_computation.25 | convolution fusion | flops 3222798336 | bytes 16252928 | tf_op jit(solution)/shard_map/dot_general | solution.py:50
  315.0 76.1 %all_to_all.16 = bf16[256,16,384]{2,0,1:T(8,128)(2,1)S(1)} all-to-all(bf16[256,16,384]{2,0,1:T(8,128)(2,1)S(1)} %bitcast.105), channel_id=1, replica_groups=mesh['ta'=4,'ha'=16,'wa'=4] {'ta','wa'}, dimensions={1} | all-to-all | bytes 6291456 | tf_op jit(solution)/shard_map/all_to_all | solution.py:53
  391.1 3.9 reshape.157
  395.0 3.1 copy.43
  398.5 1.9 fusion.40
  400.4 8.9 %collective-permute-start.6 = (bf16[8,4,64,1,256]{4,2,1,0,3:T(8,128)(2,1)}, bf16[8,4,64,1,256]{4,2,1,0,3:T(8,128)(2,1)}, u32[]{:S(2)}, u32[]{:S(2)}) collective-permute-start(bf16[8,4,64,1,256]{4,2,1,0,3:T(8,128)(2,1)} %get-tuple-element.102), channel_id=1, source_target_pairs={{0,4},{4,8},{8,12},{12,16},{16,20},{20,24},{24,28},{28,32},{32,36}... | collective-permute-start | bytes 3145736 | tf_op jit(solution)/shard_map/ppermute | solution.py:17
  409.3 1.9 collective-permute-start.7
  413.5 37.9 %collective-permute-done.6 = bf16[8,4,64,1,256]{4,2,1,0,3:T(8,128)(2,1)} collective-permute-done((bf16[8,4,64,1,256]{4,2,1,0,3:T(8,128)(2,1)}, bf16[8,4,64,1,256]{4,2,1,0,3:T(8,128)(2,1)}, u32[]{:S(2)}, u32[]{:S(2)}) %collective-permute-start.6) | collective-permute-done | bytes 1048608 | tf_op jit(solution)/shard_map/ppermute | solution.py:17
  451.4 5.2 %collective-permute-done.7 = bf16[8,4,64,1,256]{4,2,1,0,3:T(8,128)(2,1)} collective-permute-done((bf16[8,4,64,1,256]{4,2,1,0,3:T(8,128)(2,1)}, bf16[8,4,64,1,256]{4,2,1,0,3:T(8,128)(2,1)}, u32[]{:S(2)}, u32[]{:S(2)}) %collective-permute-start.7) | collective-permute-done | bytes 1048608 | tf_op jit(solution)/shard_map/ppermute | solution.py:19
  456.7 3.4 pad_maximum_fusion
  460.1 29.8 %while.12 = (s32[]{:T(128)}, bf16[2,8,4,64,1,128]{5,3,2,1,4,0:T(8,128)(2,1)}, s32[2]{0:T(128)S(1)}, bf16[8,16,64,1,256]{4,2,1,0,3:T(8,128)(2,1)}, s32[]{:T(128)}...) while((s32[]{:T(128)}, ...), condition=%wide.region_4.5_spmd, body=%wide.region_1.4_spmd.sunk | while | flops 824439104 | bytes 37807656 | solution.py:93
  461.4 3.7 fusion.50
  465.1 3.4 fusion.51
  468.5 5.5 %fusion.52 = bf16[2,8,4,64,1,128]{5,3,2,1,4,0:T(8,128)(2,1)S(1)} fusion(bf16[2,8,4,64,1,128]{5,3,2,1,4,0:T(8,128)(2,1)S(1)} %copy-done.6, s32[]{:T(128)S(6)} %copy.66, f32[8,4,64,12,64]{2,4,3,1,0:T(8,128)S(1)} %get-tuple-element.153, f32[8,4,64]{2,1,0:T(4,128)S(1)} %fusion.51, f32[8,4,64]{2,1,0:T(4,128)S(1)} %get-tuple-element.154, ...), kind=kOutput, calls=%fused_computation.12.clone.1 | convolution fusion | flops 410779648 | bytes 14713356 | tf_op jit(solution)/shard_map/while/body/eval_jaxpr/thiajb,tjbhd->tiahd/dot_general | solution.py:88
  476.3 3.7 fusion.50
  480.0 3.4 fusion.51
  483.4 5.5 %fusion.52 = bf16[2,8,4,64,1,128]{5,3,2,1,4,0:T(8,128)(2,1)S(1)} fusion(bf16[2,8,4,64,1,128]{5,3,2,1,4,0:T(8,128)(2,1)S(1)} %copy-done.6, s32[]{:T(128)S(6)} %copy.66, f32[8,4,64,12,64]{2,4,3,1,0:T(8,128)S(1)} %get-tuple-element.153, f32[8,4,64]{2,1,0:T(4,128)S(1)} %fusion.51, f32[8,4,64]{2,1,0:T(4,128)S(1)} %get-tuple-element.154, ...), kind=kOutput, calls=%fused_computation.12.clone.1 | convolution fusion | flops 410779648 | bytes 14713356 | tf_op jit(solution)/shard_map/while/body/eval_jaxpr/thiajb,tjbhd->tiahd/dot_general | solution.py:88
  489.9 2.4 copy.45
  (55 shorter events, 16.3 us)
Async XLA Ops:
  7.2 58.0 %copy-start = (bf16[3,3,3,256,256]{4,3,2,1,0:T(8,128)(2,1)S(1)}, bf16[3,3,3,256,256]{4,3,2,1,0:T(8,128)(2,1)}, u32[]{:S(2)}) copy-start(bf16[3,3,3,256,256]{4,3,2,1,0:T(8,128)(2,1)} %param.8) | copy-start | bytes 10616836
  7.2 283.3 %all-gather.2.cloned.1.call-start = ((), (), s32[]{:S(2)}) async-start(), calls=%async_computation.1 | async-start | bytes 13369344 | tf_op jit(solution)/shard_map/all_gather | solution.py:49
  11.2 8.2 %collective-permute-start = (bf16[1,16,32,256]{3,1,2,0:T(8,128)(2,1)S(1)}, bf16[1,16,32,256]{3,1,2,0:T(8,128)(2,1)S(1)}, u32[]{:S(2)}, u32[]{:S(2)}) collective-permute-start(bf16[1,16,32,256]{3,1,2,0:T(8,128)(2,1)S(1)} %get-tuple-element.108), channel_id=1, source_target_pairs={{0,64},{64,128},{128,192},{1,65},{65,129},{129,193},{2,66},{66,130... | collective-permute-start | bytes 786440 | tf_op jit(solution)/shard_map/ppermute | solution.py:17
  14.5 8.8 %collective-permute-start.1 = (bf16[1,16,32,256]{3,1,2,0:T(8,128)(2,1)S(1)}, bf16[1,16,32,256]{3,1,2,0:T(8,128)(2,1)S(1)}, u32[]{:S(2)}, u32[]{:S(2)}) collective-permute-start(bf16[1,16,32,256]{3,1,2,0:T(8,128)(2,1)S(1)} %get-tuple-element.109), channel_id=1, source_target_pairs={{64,0},{128,64},{192,128},{65,1},{129,65},{193,129},{66,2},{130,66... | collective-permute-start | bytes 786440 | tf_op jit(solution)/shard_map/ppermute | solution.py:19
  23.5 16.5 %collective-permute-start.2 = (bf16[4,1,32,256]{3,1,2,0:T(2,128)(2,1)S(1)}, bf16[4,1,32,256]{3,1,2,0:T(2,128)(2,1)S(1)}, u32[]{:S(2)}, u32[]{:S(2)}) collective-permute-start(bf16[4,1,32,256]{3,1,2,0:T(2,128)(2,1)S(1)} %get-tuple-element.106), channel_id=1, source_target_pairs={{0,4},{4,8},{8,12},{12,16},{16,20},{20,24},{24,28},{28,32},{32,36}... | collective-permute-start | bytes 196616 | tf_op jit(solution)/shard_map/ppermute | solution.py:17
  34.0 15.0 %collective-permute-start.3 = (bf16[4,1,32,256]{3,1,2,0:T(2,128)(2,1)S(1)}, bf16[4,1,32,256]{3,1,2,0:T(2,128)(2,1)S(1)}, u32[]{:S(2)}, u32[]{:S(2)}) collective-permute-start(bf16[4,1,32,256]{3,1,2,0:T(2,128)(2,1)S(1)} %get-tuple-element.107), channel_id=1, source_target_pairs={{4,0},{8,4},{12,8},{16,12},{20,16},{24,20},{28,24},{32,28},{36,32}... | collective-permute-start | bytes 196616 | tf_op jit(solution)/shard_map/ppermute | solution.py:19
  49.0 6.8 %collective-permute-start.4 = (bf16[4,18,1,256]{3,1,2,0:T(8,128)(2,1)S(1)}, bf16[4,18,1,256]{3,1,2,0:T(8,128)(2,1)S(1)}, u32[]{:S(2)}, u32[]{:S(2)}) collective-permute-start(bf16[4,18,1,256]{3,1,2,0:T(8,128)(2,1)S(1)} %get-tuple-element.104), channel_id=1, source_target_pairs={{0,1},{1,2},{2,3},{4,5},{5,6},{6,7},{8,9},{9,10},{10,11},{12,13},{... | collective-permute-start | bytes 110600 | tf_op jit(solution)/shard_map/ppermute | solution.py:17
  53.7 8.7 %collective-permute-start.5 = (bf16[4,18,1,256]{3,1,2,0:T(8,128)(2,1)S(1)}, bf16[4,18,1,256]{3,1,2,0:T(8,128)(2,1)S(1)}, u32[]{:S(2)}, u32[]{:S(2)}) collective-permute-start(bf16[4,18,1,256]{3,1,2,0:T(8,128)(2,1)S(1)} %get-tuple-element.105), channel_id=1, source_target_pairs={{1,0},{2,1},{3,2},{5,4},{6,5},{7,6},{9,8},{10,9},{11,10},{13,12},{... | collective-permute-start | bytes 110600 | tf_op jit(solution)/shard_map/ppermute | solution.py:19
  64.1 1.1 copy-start.8
  65.2 5.4 %copy-start.3 = (bf16[2,16,32,256]{3,2,1,0:T(8,128)(2,1)S(1)}, bf16[2,16,32,256]{3,2,1,0:T(8,128)(2,1)}, u32[]{:S(2)}) copy-start(bf16[2,16,32,256]{3,2,1,0:T(8,128)(2,1)} %param.6) | copy-start | bytes 1572868
  71.1 235.2 %copy-start.4 = (bf16[2,16,32,256]{3,1,2,0:T(8,128)(2,1)}, bf16[2,16,32,256]{3,1,2,0:T(8,128)(2,1)S(1)}, u32[]{:S(2)}) copy-start(bf16[2,16,32,256]{3,1,2,0:T(8,128)(2,1)S(1)} %fusion.35) | copy-start | bytes 1572868
  398.0 2.4 copy-start.2
  398.1 13.2 %copy-start.5 = (bf16[2,16,32,256]{3,1,2,0:T(8,128)(2,1)S(1)}, bf16[2,16,32,256]{3,1,2,0:T(8,128)(2,1)}, u32[]{:S(2)}) copy-start(bf16[2,16,32,256]{3,1,2,0:T(8,128)(2,1)} %copy-done.4) | copy-start | bytes 1572868
  400.4 51.0 %collective-permute-start.6 = (bf16[8,4,64,1,256]{4,2,1,0,3:T(8,128)(2,1)}, bf16[8,4,64,1,256]{4,2,1,0,3:T(8,128)(2,1)}, u32[]{:S(2)}, u32[]{:S(2)}) collective-permute-start(bf16[8,4,64,1,256]{4,2,1,0,3:T(8,128)(2,1)} %get-tuple-element.102), channel_id=1, source_target_pairs={{0,4},{4,8},{8,12},{12,16},{16,20},{20,24},{24,28},{28,32},{32,36}... | collective-permute-start | bytes 3145736 | tf_op jit(solution)/shard_map/ppermute | solution.py:17
  409.3 47.4 %collective-permute-start.7 = (bf16[8,4,64,1,256]{4,2,1,0,3:T(8,128)(2,1)}, bf16[8,4,64,1,256]{4,2,1,0,3:T(8,128)(2,1)}, u32[]{:S(2)}, u32[]{:S(2)}) collective-permute-start(bf16[8,4,64,1,256]{4,2,1,0,3:T(8,128)(2,1)} %get-tuple-element.103), channel_id=1, source_target_pairs={{4,0},{8,4},{12,8},{16,12},{20,16},{24,20},{28,24},{32,28},{36,32}... | collective-permute-start | bytes 3145736 | tf_op jit(solution)/shard_map/ppermute | solution.py:19
  465.1 3.5 copy-start.6
  474.0 1.0 copy-start.7
  479.9 3.5 copy-start.6
  488.9 1.0 copy-start.7
  489.9 2.4 copy-start.1
Sparse Core Ops, SparseCore 0:
  9.8 280.7 all-gather.1
where the time goes:
time: 500 us; the launch traced here: 499 us
  waiting for transfers between devices  289 us (58%)
  blocking collectives  76.1 us (15%)
  local copies, waits for them, and re-layouts  37.4 us (7%)
  starting transfers between devices  33.7 us (7%)
  matrix products  31.5 us (6%)
  other arithmetic  15.3 us (3%)
  between operations  14.3 us (3%)
    all_gather x1, waiting for transfers between devices, local(): every_head = lax.all_gather(qkv_weight, ('ta', 'wa'), axis=1, tiled=True)  218 us
    all_to_all x1, blocking collectives, local(): lax.all_to_all(projected, ('ta', 'wa'), split_axis=1, concat_axis=0, tile...  76.1 us
    ppermute x4, waiting for transfers between devices, extended(): lax.ppermute(tail, axis, [(i, (i + 1) % count) for i in range(ends)])  46.5 us
    ppermute x4, starting transfers between devices, extended(): lax.ppermute(tail, axis, [(i, (i + 1) % count) for i in range(ends)])  27.3 us
    ppermute x4, waiting for transfers between devices, extended(): lax.ppermute(head, axis, [((i + 1) % count, i) for i in range(ends)])  24.6 us
    all_gather x1, local copies, waits for them, and re-layouts, local(): every_head = lax.all_gather(qkv_weight, ('ta', 'wa'), axis=1, tiled=True)  15.7 us
    dot_general x2, matrix products, attend(): jnp.einsum('thiajb,tjbhd->tiahd', probs, value_part, preferred_element_ty...  10.9 us
  transfers between devices with their start and end apart: 9, of which 9 were waited for; matrix products, arithmetic and copies ran while one was open for 3% of the time, Pallas kernels for 0%

commit v1 on v0

--- a/solution.py
+++ b/solution.py
@@ -40,30 +40,23 @@
         preferred_element_type=jnp.float32,
     )[0]
     block_out = (latent_f32 + conv_out).astype(jnp.bfloat16)
+    width_in, head_dev, qkv_count, head_size = qkv_weight.shape
+    col_heads = lax.all_gather(qkv_weight, "ta", axis=1, tiled=True)
+    heads = col_heads.shape[1]
+    wide = lax.all_gather(block_out, "wa", axis=2, tiled=True)
+    patch_cols = wide.shape[2] // 2
     patches = (
-        block_out.reshape(t_dev, rows_dev, 2, cols_dev, 2, channels)
+        wide.reshape(t_dev, rows_dev, 2, patch_cols, 2, channels)
         .transpose(0, 1, 3, 2, 4, 5)
-        .reshape(t_dev * rows_dev * cols_dev, 4 * channels)
+        .reshape(t_dev * rows_dev * patch_cols, 4 * channels)
     )
-    width_in, head_dev, qkv_count, head_size = qkv_weight.shape
-    every_head = lax.all_gather(qkv_weight, ("ta", "wa"), axis=1, tiled=True)
     projected = jnp.dot(
-        patches, every_head.reshape(width_in, -1), preferred_element_type=jnp.float32
+        patches, col_heads.reshape(width_in, -1), preferred_element_type=jnp.float32
     ).astype(jnp.bfloat16)
-    gathered = lax.all_to_all(projected, ("ta", "wa"), split_axis=1, concat_axis=0, tiled=True)
-    n_time = lax.axis_size("ta")
-    n_width = lax.axis_size("wa")
-    frames = n_time * t_dev
-    patch_cols = n_width * cols_dev
-    qkv_rows = gathered.reshape(
-        n_time, n_width, t_dev, rows_dev, cols_dev, head_dev, qkv_count, head_size
-    )
-    qkv_rows = qkv_rows.transpose(0, 2, 3, 1, 4, 5, 6, 7).reshape(
-        frames, rows_dev, patch_cols, head_dev, qkv_count, head_size
-    )
+    qkv_rows = projected.reshape(t_dev, rows_dev, patch_cols, heads, qkv_count, head_size)
     queries = qkv_rows[:, :, :, :, 0, :]
     key_value = qkv_rows[:, :, :, :, 1:, :].reshape(
-        frames, rows_dev, patch_cols, head_dev, 2 * head_size
+        t_dev, rows_dev, patch_cols, heads, 2 * head_size
     )
     kv_rim = extended(key_value, (("ha", 1),), WIN)
     row_base = lax.axis_index("ha") * rows_dev
@@ -92,8 +85,9 @@
 
     blocks = lax.map(attend, jnp.arange(rows_dev // WIN, dtype=jnp.int32))
     attended = blocks.transpose(1, 0, 2, 3, 4, 5).reshape(
-        frames, rows_dev, patch_cols, head_dev, head_size
+        t_dev, rows_dev, patch_cols, heads, head_size
     )
+    attended = lax.all_to_all(attended, "ta", split_axis=3, concat_axis=0, tiled=True)
     return (block_out, attended)
 
 

time: 500 us -> 311 us (0.62)
  the two profiles are of different devices: /device:TPU:3 before, /device:TPU:67 now
where the time goes in v1:
time: 311 us; the launch traced here: 310 us
  waiting for transfers between devices  154 us (50%)
  local copies, waits for them, and re-layouts  56 us (18%)
  matrix products  35.1 us (11%)
  starting transfers between devices  33.3 us (11%)
  other arithmetic  15.9 us (5%)
  between operations  14.3 us (5%)
    all_gather x1, waiting for transfers between devices, local(): wide = lax.all_gather(block_out, 'wa', axis=2, tiled=True)  46.3 us
    ppermute x4, waiting for transfers between devices, extended(): lax.ppermute(tail, axis, [(i, (i + 1) % count) for i in range(ends)])  42 us
    all_gather x1, waiting for transfers between devices, local(): col_heads = lax.all_gather(qkv_weight, 'ta', axis=1, tiled=True)  33.7 us
    ppermute x4, starting transfers between devices, extended(): lax.ppermute(tail, axis, [(i, (i + 1) % count) for i in range(ends)])  20.1 us
    ppermute x4, waiting for transfers between devices, extended(): lax.ppermute(head, axis, [((i + 1) % count, i) for i in range(ends)])  19 us
    dot_general x2, matrix products, attend(): jnp.einsum('thiajb,tjbhd->tiahd', probs, value_part, preferred_element_ty...  16.7 us
    all_to_all x1, waiting for transfers between devices, local(): lax.all_to_all(attended, 'ta', split_axis=3, concat_axis=0, tiled=True)  12.7 us
    while x12, local copies, waits for them, and re-layouts  11 us
  transfers between devices with their start and end apart: 11, of which 10 were waited for; matrix products, arithmetic and copies ran while one was open for 5% of the time, Pallas kernels for 0%

profile of v1, /device:TPU:67, one launch (start us, length us, event | category | flops | bytes accessed | tf_op | source)
XLA Modules:
  0.0 310.4 jit_solution(17546351096016199151)
XLA Ops:
  10.4 3.2 %collective-permute-start = (bf16[1,16,32,256]{3,1,2,0:T(8,128)(2,1)S(1)}, bf16[1,16,32,256]{3,1,2,0:T(8,128)(2,1)S(1)}, u32[]{:S(2)}, u32[]{:S(2)}) collective-permute-start(bf16[1,16,32,256]{3,1,2,0:T(8,128)(2,1)S(1)} %get-tuple-element.126), channel_id=1, source_target_pairs={{0,64},{64,128},{128,192},{1,65},{65,129},{129,193},{2,66},{66,130... | collective-permute-start | bytes 786440 | tf_op jit(solution)/shard_map/ppermute | solution.py:17
  14.9 3.7 %collective-permute-done = bf16[1,16,32,256]{3,1,2,0:T(8,128)(2,1)S(1)} collective-permute-done((bf16[1,16,32,256]{3,1,2,0:T(8,128)(2,1)S(1)}, bf16[1,16,32,256]{3,1,2,0:T(8,128)(2,1)S(1)}, u32[]{:S(2)}, u32[]{:S(2)}) %collective-permute-start) | collective-permute-done | bytes 262176 | tf_op jit(solution)/shard_map/ppermute | solution.py:17
  18.6 3.8 %collective-permute-done.1 = bf16[1,16,32,256]{3,1,2,0:T(8,128)(2,1)S(1)} collective-permute-done((bf16[1,16,32,256]{3,1,2,0:T(8,128)(2,1)S(1)}, bf16[1,16,32,256]{3,1,2,0:T(8,128)(2,1)S(1)}, u32[]{:S(2)}, u32[]{:S(2)}) %collective-permute-start.1) | collective-permute-done | bytes 262176 | tf_op jit(solution)/shard_map/ppermute | solution.py:19
  22.6 8.7 %collective-permute-start.2 = (bf16[4,1,32,256]{3,1,2,0:T(2,128)(2,1)S(1)}, bf16[4,1,32,256]{3,1,2,0:T(2,128)(2,1)S(1)}, u32[]{:S(2)}, u32[]{:S(2)}) collective-permute-start(bf16[4,1,32,256]{3,1,2,0:T(2,128)(2,1)S(1)} %get-tuple-element.124), channel_id=1, source_target_pairs={{0,4},{4,8},{8,12},{12,16},{16,20},{20,24},{24,28},{28,32},{32,36}... | collective-permute-start | bytes 196616 | tf_op jit(solution)/shard_map/ppermute | solution.py:17
  33.9 9.1 %collective-permute-done.3 = bf16[4,1,32,256]{3,1,2,0:T(2,128)(2,1)S(1)} collective-permute-done((bf16[4,1,32,256]{3,1,2,0:T(2,128)(2,1)S(1)}, bf16[4,1,32,256]{3,1,2,0:T(2,128)(2,1)S(1)}, u32[]{:S(2)}, u32[]{:S(2)}) %collective-permute-start.3) | collective-permute-done | bytes 65568 | tf_op jit(solution)/shard_map/ppermute | solution.py:19
  44.9 3.4 %collective-permute-start.5 = (bf16[4,18,1,256]{3,1,2,0:T(8,128)(2,1)S(1)}, bf16[4,18,1,256]{3,1,2,0:T(8,128)(2,1)S(1)}, u32[]{:S(2)}, u32[]{:S(2)}) collective-permute-start(bf16[4,18,1,256]{3,1,2,0:T(8,128)(2,1)S(1)} %get-tuple-element.123), channel_id=1, source_target_pairs={{1,0},{2,1},{3,2},{5,4},{6,5},{7,6},{9,8},{10,9},{11,10},{13,12},{... | collective-permute-start | bytes 110600 | tf_op jit(solution)/shard_map/ppermute | solution.py:19
  52.6 5.0 %fusion.23 = f32[2,16,8,5,256]{4,2,3,1,0:T(8,128)S(1)} fusion(bf16[3,3,3,256,256]{4,3,2,1,0:T(8,128)(2,1)S(1)} %copy-done, bf16[4,18,1,7,2,256]{5,3,4,1,0,2:T(8,128)(2,1)S(1)} %slice.56, bf16[4,18,1,8,5,256]{5,3,4,1,0,2:T(8,128)(2,1)S(1)} %copy.44, pred[8,5]{0,1:T(8,128)(4,1)S(1)} %copy-done.6), kind=kOutput, calls=%fused_computation.40 | convolution fusion | flops 4536369152 | bytes 6840360 | tf_op jit(solution)/shard_map/conv_general_dilated | solution.py:34
  60.0 46.3 %all-gather.3.cloned.1.call-done = bf16[2,16,128,256]{3,1,2,0:T(8,128)(2,1)} async-done(((bf16[2,16,32,256]{3,1,2,0:T(8,128)(2,1)}), bf16[2,16,128,256]{3,1,2,0:T(8,128)(2,1)}) %all-gather.3.cloned.1.call-update) | async-done | bytes 2097168 | tf_op jit(solution)/shard_map/all_gather | solution.py:46
  106.3 2.7 reshape.104
  109.0 3.5 %copy.74 = bf16[2,8,2,64,2,256]{5,4,2,3,1,0:T(2,128)(2,1)} copy(bf16[2,8,2,64,2,256]{5,2,1,4,3,0:T(2,128)(2,1)S(1)} %reshape.104) | data formatting | bytes 4194304 | tf_op jit(solution)/shard_map/reshape | solution.py:49
  112.6 4.5 %reshape.105 = bf16[1024,1024]{1,0:T(8,128)(2,1)} reshape(bf16[2,8,64,2,2,256]{5,4,3,2,1,0:T(2,128)(2,1)} %bitcast.88) | data formatting | bytes 4194304 | tf_op jit(solution)/shard_map/reshape | solution.py:51
  117.0 33.7 %all-gather.5.cloned.1.call-done = bf16[1024,4,3,128]{3,0,2,1:T(8,128)(2,1)} async-done(((bf16[1024,1,3,128]{3,0,2,1:T(8,128)(2,1)}), bf16[1024,4,3,128]{3,0,2,1:T(8,128)(2,1)}) %all-gather.5.cloned.1.call-update) | async-done | bytes 3145744 | tf_op jit(solution)/shard_map/all_gather | solution.py:44
  150.7 4.6 %copy.47 = bf16[1024,4,3,128]{0,3,2,1:T(8,128)(2,1)} copy(bf16[1024,4,3,128]{3,0,2,1:T(8,128)(2,1)} %all-gather.5.cloned.1.call-done) | data formatting | bytes 6291456 | tf_op jit(solution)/shard_map/all_gather | solution.py:44
  155.4 6.0 %convolution_convert_fusion = bf16[1024,1536]{1,0:T(8,128)(2,1)S(1)} fusion(bf16[1024,1024]{1,0:T(8,128)(2,1)} %reshape.105, bf16[1024,1536]{0,1:T(8,128)(2,1)} %bitcast.91), kind=kOutput, calls=%fused_computation.28 | convolution fusion | flops 3222798336 | bytes 8388608 | tf_op jit(solution)/shard_map/dot_general | solution.py:53
  161.3 4.5 %reshape.107 = bf16[2,8,64,4,3,128]{5,4,3,2,1,0:T(4,128)(2,1)} reshape(bf16[1024,1536]{1,0:T(8,128)(2,1)S(1)} %convolution_convert_fusion) | data formatting | bytes 6291456 | tf_op jit(solution)/shard_map/reshape | solution.py:56
  165.9 4.6 %slice.58 = bf16[2,8,64,4,2,128]{5,4,3,2,1,0:T(2,128)(2,1)S(1)} slice(bf16[2,8,64,4,3,128]{5,4,3,2,1,0:T(4,128)(2,1)} %reshape.107), slice={[0:2], [0:8], [0:64], [0:4], [1:3], [0:128]} | slice | bytes 4194304 | tf_op jit(solution)/shard_map/slice | solution.py:58
  176.7 6.3 %collective-permute-start.6 = (bf16[2,4,64,4,256]{4,2,1,3,0:T(8,128)(2,1)}, bf16[2,4,64,4,256]{4,2,1,3,0:T(8,128)(2,1)}, u32[]{:S(2)}, u32[]{:S(2)}) collective-permute-start(bf16[2,4,64,4,256]{4,2,1,3,0:T(8,128)(2,1)} %get-tuple-element.120), channel_id=1, source_target_pairs={{0,4},{4,8},{8,12},{12,16},{16,20},{20,24},{24,28},{28,32},{32,36}... | collective-permute-start | bytes 3145736 | tf_op jit(solution)/shard_map/ppermute | solution.py:17
  185.2 3.8 %slice.61 = bf16[2,8,64,4,1,128]{5,4,3,2,1,0:T(2,128)(2,1)S(1)} slice(bf16[2,8,64,4,3,128]{5,4,3,2,1,0:T(4,128)(2,1)} %reshape.107), slice={[0:2], [0:8], [0:64], [0:4], [0:1], [0:128]} | slice | bytes 2097152 | tf_op jit(solution)/shard_map/slice | solution.py:57
  189.3 37.8 %collective-permute-done.6 = bf16[2,4,64,4,256]{4,2,1,3,0:T(8,128)(2,1)} collective-permute-done((bf16[2,4,64,4,256]{4,2,1,3,0:T(8,128)(2,1)}, bf16[2,4,64,4,256]{4,2,1,3,0:T(8,128)(2,1)}, u32[]{:S(2)}, u32[]{:S(2)}) %collective-permute-start.6) | collective-permute-done | bytes 1048608 | tf_op jit(solution)/shard_map/ppermute | solution.py:17
  227.0 4.6 %collective-permute-done.7 = bf16[2,4,64,4,256]{4,2,1,3,0:T(8,128)(2,1)} collective-permute-done((bf16[2,4,64,4,256]{4,2,1,3,0:T(8,128)(2,1)}, bf16[2,4,64,4,256]{4,2,1,3,0:T(8,128)(2,1)}, u32[]{:S(2)}, u32[]{:S(2)}) %collective-permute-start.7) | collective-permute-done | bytes 1048608 | tf_op jit(solution)/shard_map/ppermute | solution.py:19
  231.7 3.4 %pad_maximum_fusion = bf16[2,16,64,4,256]{4,2,1,3,0:T(8,128)(2,1)} fusion(bf16[2,4,64,4,256]{4,2,1,3,0:T(8,128)(2,1)} %collective-permute-done.7, bf16[2,8,64,4,256]{4,2,1,3,0:T(8,128)(2,1)S(1)} %copy.48, bf16[2,4,64,4,256]{4,2,1,3,0:T(8,128)(2,1)} %collective-permute-done.6), kind=kLoop, calls=%fused_computation.25 | loop fusion | flops 4194304 | bytes 8388608 | tf_op jit(solution)/shard_map/concatenate | solution.py:15
  235.0 44.8 %while.12 = (s32[]{:T(128)}, bf16[2,2,4,64,4,128]{5,3,4,2,0,1:T(8,128)(2,1)}, s32[2]{0:T(128)S(1)}, bf16[2,16,64,4,256]{4,2,1,3,0:T(8,128)(2,1)}, s32[]{:T(128)}...) while((s32[]{:T(128)}, ...), condition=%wide.region_4.5_spmd, body=%wide.region_1.4_spmd.sunk | while | flops 824439104 | bytes 64005228 | solution.py:86
  236.3 3.7 %fusion.49 = (f32[2,4,4,64]{3,2,1,0:T(4,128)S(1)}, f32[2,4,4,64,12,64]{3,5,4,2,1,0:T(8,128)S(1)}) fusion(pred[4,12]{1,0:T(4,128)(4,1)S(1)} %fusion.48, bf16[2,16,64,4,256]{4,2,1,3,0:T(8,128)(2,1)} %get-tuple-element.200, s32[]{:T(128)S(6)} %select_n.43, bf16[2,8,64,4,128]{4,2,1,3,0:T(8,128)(2,1)S(1)} %get-tuple-element.202, s32[]{:T(128)S(6)} %select_n.44), kind=kOutput, calls=%fused_computation.3.clone.1 | convolution fusion | flops 407369728 | bytes 8397320 | tf_op jit(solution)/shard_map/while/body/eval_jaxpr/tiahd,tjbhd->thiajb/dot_general | solution.py:70
  240.0 4.5 %copy-done.2 = f32[2,4,4,64,12,64]{3,5,4,2,1,0:T(8,128)} copy-done((f32[2,4,4,64,12,64]{3,5,4,2,1,0:T(8,128)}, f32[2,4,4,64,12,64]{3,5,4,2,1,0:T(8,128)S(1)}, u32[]{:S(2)}) %copy-start.2) | copy-done | bytes 6291480 | tf_op jit(solution)/shard_map/while
  244.6 3.4 %fusion.50 = f32[2,4,4,64]{3,2,1,0:T(4,128)S(1)} fusion(f32[2,4,4,64,12,64]{3,5,4,2,1,0:T(8,128)S(1)} %get-tuple-element.171, f32[2,4,4,64]{3,2,1,0:T(4,128)S(1)} %get-tuple-element.172, pred[4,12]{1,0:T(4,128)(4,1)S(1)} %fusion.48), kind=kLoop, calls=%fused_computation.4.clone.1 | loop fusion | flops 6289408 | bytes 6307888 | tf_op jit(solution)/shard_map/while/body/eval_jaxpr/reduce_sum | solution.py:80
  248.0 8.4 %fusion.51 = bf16[1,2,4,64,4,128]{5,3,2,4,1,0:T(8,128)(2,1)S(1)} fusion(f32[2,4,4,64,12,64]{3,5,4,2,1,0:T(8,128)} %copy-done.2, f32[2,4,4,64]{3,2,1,0:T(4,128)S(1)} %fusion.50, f32[2,4,4,64]{3,2,1,0:T(4,128)S(1)} %get-tuple-element.172, pred[4,12]{1,0:T(4,128)(4,1)S(1)} %fusion.48, bf16[2,16,64,4,256]{4,2,1,3,0:T(8,128)(2,1)} %get-tuple-element.200, ...), kind=kOutput, calls=%fused_computation.11.clone.1 | convolution fusion | flops 410779648 | bytes 14696504 | tf_op jit(solution)/shard_map/while/body/eval_jaxpr/thiajb,tjbhd->tiahd/dot_general | solution.py:81
  258.7 3.7 %fusion.49 = (f32[2,4,4,64]{3,2,1,0:T(4,128)S(1)}, f32[2,4,4,64,12,64]{3,5,4,2,1,0:T(8,128)S(1)}) fusion(pred[4,12]{1,0:T(4,128)(4,1)S(1)} %fusion.48, bf16[2,16,64,4,256]{4,2,1,3,0:T(8,128)(2,1)} %get-tuple-element.200, s32[]{:T(128)S(6)} %select_n.43, bf16[2,8,64,4,128]{4,2,1,3,0:T(8,128)(2,1)S(1)} %get-tuple-element.202, s32[]{:T(128)S(6)} %select_n.44), kind=kOutput, calls=%fused_computation.3.clone.1 | convolution fusion | flops 407369728 | bytes 8397320 | tf_op jit(solution)/shard_map/while/body/eval_jaxpr/tiahd,tjbhd->thiajb/dot_general | solution.py:70
  262.4 4.5 %copy-done.2 = f32[2,4,4,64,12,64]{3,5,4,2,1,0:T(8,128)} copy-done((f32[2,4,4,64,12,64]{3,5,4,2,1,0:T(8,128)}, f32[2,4,4,64,12,64]{3,5,4,2,1,0:T(8,128)S(1)}, u32[]{:S(2)}) %copy-start.2) | copy-done | bytes 6291480 | tf_op jit(solution)/shard_map/while
  267.0 3.4 %fusion.50 = f32[2,4,4,64]{3,2,1,0:T(4,128)S(1)} fusion(f32[2,4,4,64,12,64]{3,5,4,2,1,0:T(8,128)S(1)} %get-tuple-element.171, f32[2,4,4,64]{3,2,1,0:T(4,128)S(1)} %get-tuple-element.172, pred[4,12]{1,0:T(4,128)(4,1)S(1)} %fusion.48), kind=kLoop, calls=%fused_computation.4.clone.1 | loop fusion | flops 6289408 | bytes 6307888 | tf_op jit(solution)/shard_map/while/body/eval_jaxpr/reduce_sum | solution.py:80
  270.4 8.4 %fusion.51 = bf16[1,2,4,64,4,128]{5,3,2,4,1,0:T(8,128)(2,1)S(1)} fusion(f32[2,4,4,64,12,64]{3,5,4,2,1,0:T(8,128)} %copy-done.2, f32[2,4,4,64]{3,2,1,0:T(4,128)S(1)} %fusion.50, f32[2,4,4,64]{3,2,1,0:T(4,128)S(1)} %get-tuple-element.172, pred[4,12]{1,0:T(4,128)(4,1)S(1)} %fusion.48, bf16[2,16,64,4,256]{4,2,1,3,0:T(8,128)(2,1)} %get-tuple-element.200, ...), kind=kOutput, calls=%fused_computation.11.clone.1 | convolution fusion | flops 410779648 | bytes 14696504 | tf_op jit(solution)/shard_map/while/body/eval_jaxpr/thiajb,tjbhd->tiahd/dot_general | solution.py:81
  282.3 4.2 %all-to-all-start = ((bf16[2,8,64,4,128]{4,2,1,0,3:T(8,128)(2,1)}), bf16[2,8,64,4,128]{4,2,1,0,3:T(8,128)(2,1)}, u32[]{:S(2)}, u32[]{:S(2)}) async-start(bf16[2,8,64,4,128]{4,2,1,0,3:T(8,128)(2,1)} %copy.54), calls=%async_computation | async-start | bytes 2097152 | tf_op jit(solution)/shard_map/all_to_all | solution.py:90
  288.5 12.7 %all-to-all-done = bf16[2,8,64,4,128]{4,2,1,0,3:T(8,128)(2,1)} async-done(((bf16[2,8,64,4,128]{4,2,1,0,3:T(8,128)(2,1)}), bf16[2,8,64,4,128]{4,2,1,0,3:T(8,128)(2,1)}, u32[]{:S(2)}, u32[]{:S(2)}) %all-to-all-start) | async-done | bytes 1048608 | tf_op jit(solution)/shard_map/all_to_all | solution.py:90
  (61 shorter events, 34.4 us)
Async XLA Ops:
  7.2 45.4 %copy-start = (bf16[3,3,3,256,256]{4,3,2,1,0:T(8,128)(2,1)S(1)}, bf16[3,3,3,256,256]{4,3,2,1,0:T(8,128)(2,1)}, u32[]{:S(2)}) copy-start(bf16[3,3,3,256,256]{4,3,2,1,0:T(8,128)(2,1)} %param.8) | copy-start | bytes 10616836
  7.2 99.1 %all-gather.3.cloned.1.call-start = ((), (), s32[]{:S(2)}) async-start(), calls=%async_computation.1 | async-start | bytes 2621440 | tf_op jit(solution)/shard_map/all_gather | solution.py:46
  10.4 8.2 %collective-permute-start = (bf16[1,16,32,256]{3,1,2,0:T(8,128)(2,1)S(1)}, bf16[1,16,32,256]{3,1,2,0:T(8,128)(2,1)S(1)}, u32[]{:S(2)}, u32[]{:S(2)}) collective-permute-start(bf16[1,16,32,256]{3,1,2,0:T(8,128)(2,1)S(1)} %get-tuple-element.126), channel_id=1, source_target_pairs={{0,64},{64,128},{128,192},{1,65},{65,129},{129,193},{2,66},{66,130... | collective-permute-start | bytes 786440 | tf_op jit(solution)/shard_map/ppermute | solution.py:17
  13.6 8.8 %collective-permute-start.1 = (bf16[1,16,32,256]{3,1,2,0:T(8,128)(2,1)S(1)}, bf16[1,16,32,256]{3,1,2,0:T(8,128)(2,1)S(1)}, u32[]{:S(2)}, u32[]{:S(2)}) collective-permute-start(bf16[1,16,32,256]{3,1,2,0:T(8,128)(2,1)S(1)} %get-tuple-element.127), channel_id=1, source_target_pairs={{64,0},{128,64},{192,128},{65,1},{129,65},{193,129},{66,2},{130,66... | collective-permute-start | bytes 786440 | tf_op jit(solution)/shard_map/ppermute | solution.py:19
  22.6 11.2 %collective-permute-start.2 = (bf16[4,1,32,256]{3,1,2,0:T(2,128)(2,1)S(1)}, bf16[4,1,32,256]{3,1,2,0:T(2,128)(2,1)S(1)}, u32[]{:S(2)}, u32[]{:S(2)}) collective-permute-start(bf16[4,1,32,256]{3,1,2,0:T(2,128)(2,1)S(1)} %get-tuple-element.124), channel_id=1, source_target_pairs={{0,4},{4,8},{8,12},{12,16},{16,20},{20,24},{24,28},{28,32},{32,36}... | collective-permute-start | bytes 196616 | tf_op jit(solution)/shard_map/ppermute | solution.py:17
  31.4 11.6 %collective-permute-start.3 = (bf16[4,1,32,256]{3,1,2,0:T(2,128)(2,1)S(1)}, bf16[4,1,32,256]{3,1,2,0:T(2,128)(2,1)S(1)}, u32[]{:S(2)}, u32[]{:S(2)}) collective-permute-start(bf16[4,1,32,256]{3,1,2,0:T(2,128)(2,1)S(1)} %get-tuple-element.125), channel_id=1, source_target_pairs={{4,0},{8,4},{12,8},{16,12},{20,16},{24,20},{28,24},{32,28},{36,32}... | collective-permute-start | bytes 196616 | tf_op jit(solution)/shard_map/ppermute | solution.py:19
  43.0 5.3 %collective-permute-start.4 = (bf16[4,18,1,256]{3,1,2,0:T(8,128)(2,1)S(1)}, bf16[4,18,1,256]{3,1,2,0:T(8,128)(2,1)S(1)}, u32[]{:S(2)}, u32[]{:S(2)}) collective-permute-start(bf16[4,18,1,256]{3,1,2,0:T(8,128)(2,1)S(1)} %get-tuple-element.122), channel_id=1, source_target_pairs={{0,1},{1,2},{2,3},{4,5},{5,6},{6,7},{8,9},{9,10},{10,11},{12,13},{... | collective-permute-start | bytes 110600 | tf_op jit(solution)/shard_map/ppermute | solution.py:17
  44.9 4.8 %collective-permute-start.5 = (bf16[4,18,1,256]{3,1,2,0:T(8,128)(2,1)S(1)}, bf16[4,18,1,256]{3,1,2,0:T(8,128)(2,1)S(1)}, u32[]{:S(2)}, u32[]{:S(2)}) collective-permute-start(bf16[4,18,1,256]{3,1,2,0:T(8,128)(2,1)S(1)} %get-tuple-element.123), channel_id=1, source_target_pairs={{1,0},{2,1},{3,2},{5,4},{6,5},{7,6},{9,8},{10,9},{11,10},{13,12},{... | collective-permute-start | bytes 110600 | tf_op jit(solution)/shard_map/ppermute | solution.py:19
  51.5 1.1 copy-start.6
  52.6 5.4 %copy-start.3 = (bf16[2,16,32,256]{3,2,1,0:T(8,128)(2,1)S(1)}, bf16[2,16,32,256]{3,2,1,0:T(8,128)(2,1)}, u32[]{:S(2)}) copy-start(bf16[2,16,32,256]{3,2,1,0:T(8,128)(2,1)} %param.6) | copy-start | bytes 1572868
  59.2 91.5 %all-gather.5.cloned.1.call-start = ((), (), s32[]{:S(2)}) async-start(), calls=%async_computation.2 | async-start | bytes 3932160 | tf_op jit(solution)/shard_map/all_gather | solution.py:44
  176.7 50.3 %collective-permute-start.6 = (bf16[2,4,64,4,256]{4,2,1,3,0:T(8,128)(2,1)}, bf16[2,4,64,4,256]{4,2,1,3,0:T(8,128)(2,1)}, u32[]{:S(2)}, u32[]{:S(2)}) collective-permute-start(bf16[2,4,64,4,256]{4,2,1,3,0:T(8,128)(2,1)} %get-tuple-element.120), channel_id=1, source_target_pairs={{0,4},{4,8},{8,12},{12,16},{16,20},{20,24},{24,28},{28,32},{32,36}... | collective-permute-start | bytes 3145736 | tf_op jit(solution)/shard_map/ppermute | solution.py:17
  183.0 48.6 %collective-permute-start.7 = (bf16[2,4,64,4,256]{4,2,1,3,0:T(8,128)(2,1)}, bf16[2,4,64,4,256]{4,2,1,3,0:T(8,128)(2,1)}, u32[]{:S(2)}, u32[]{:S(2)}) collective-permute-start(bf16[2,4,64,4,256]{4,2,1,3,0:T(8,128)(2,1)} %get-tuple-element.121), channel_id=1, source_target_pairs={{4,0},{8,4},{12,8},{16,12},{20,16},{24,20},{28,24},{32,28},{36,32}... | collective-permute-start | bytes 3145736 | tf_op jit(solution)/shard_map/ppermute | solution.py:19
  240.0 4.5 %copy-start.2 = (f32[2,4,4,64,12,64]{3,5,4,2,1,0:T(8,128)}, f32[2,4,4,64,12,64]{3,5,4,2,1,0:T(8,128)S(1)}, u32[]{:S(2)}) copy-start(f32[2,4,4,64,12,64]{3,5,4,2,1,0:T(8,128)S(1)} %get-tuple-element.171) | copy-start | bytes 18874372 | tf_op jit(solution)/shard_map/while
  248.0 8.4 %copy-start.4 = (bf16[2,2,4,64,4,128]{5,3,4,2,0,1:T(8,128)(2,1)S(1)}, bf16[2,2,4,64,4,128]{5,3,4,2,0,1:T(8,128)(2,1)}, u32[]{:S(2)}) copy-start(bf16[2,2,4,64,4,128]{5,3,4,2,0,1:T(8,128)(2,1)} %get-tuple-element.186) | copy-start | bytes 3145732 | tf_op jit(solution)/shard_map/while
  256.5 1.0 copy-start.5
  262.4 4.5 %copy-start.2 = (f32[2,4,4,64,12,64]{3,5,4,2,1,0:T(8,128)}, f32[2,4,4,64,12,64]{3,5,4,2,1,0:T(8,128)S(1)}, u32[]{:S(2)}) copy-start(f32[2,4,4,64,12,64]{3,5,4,2,1,0:T(8,128)S(1)} %get-tuple-element.171) | copy-start | bytes 18874372 | tf_op jit(solution)/shard_map/while
  270.4 8.4 %copy-start.4 = (bf16[2,2,4,64,4,128]{5,3,4,2,0,1:T(8,128)(2,1)S(1)}, bf16[2,2,4,64,4,128]{5,3,4,2,0,1:T(8,128)(2,1)}, u32[]{:S(2)}) copy-start(bf16[2,2,4,64,4,128]{5,3,4,2,0,1:T(8,128)(2,1)} %get-tuple-element.186) | copy-start | bytes 3145732 | tf_op jit(solution)/shard_map/while
  278.9 1.0 copy-start.5
  279.9 23.7 %copy-start.1 = (bf16[3,3,3,256,256]{4,3,2,1,0:T(8,128)(2,1)S(1)}, bf16[3,3,3,256,256]{4,3,2,1,0:T(8,128)(2,1)}, u32[]{:S(2)}) copy-start(bf16[3,3,3,256,256]{4,3,2,1,0:T(8,128)(2,1)} %param.8) | copy-start | bytes 10616836
  282.3 19.0 %all-to-all-start = ((bf16[2,8,64,4,128]{4,2,1,0,3:T(8,128)(2,1)}), bf16[2,8,64,4,128]{4,2,1,0,3:T(8,128)(2,1)}, u32[]{:S(2)}, u32[]{:S(2)}) async-start(bf16[2,8,64,4,128]{4,2,1,0,3:T(8,128)(2,1)} %copy.54), calls=%async_computation | async-start | bytes 2097152 | tf_op jit(solution)/shard_map/all_to_all | solution.py:90
Sparse Core Ops, SparseCore 0:
  59.3 46.8 all-gather.2
  108.1 42.5 all-gather.4

commit v2 on v1

v2 whole, which is shorter than its diff:
```python
import functools
import math

import jax
import jax.numpy as jnp
from jax import lax
from jax.experimental import pallas as pl
from jax.experimental.pallas import tpu as pltpu
from jax.sharding import PartitionSpec as P


WIN = 4
NEG = -1e30
LANES = 128


def project_body(place, own, other, w0, w1, w2, w3, out):
    core = place[0]
    rows, cols, depth = own.shape
    cells = jnp.concatenate(
        [own[...].reshape(rows * cols, depth), other[...].reshape(rows * cols, depth)], axis=0
    )
    for d, w_ref in enumerate((w0, w1, w2, w3)):
        wide = 3 * w_ref.shape[2]
        weight = jnp.concatenate([w_ref[0], w_ref[1], w_ref[2]], axis=1)
        got = jnp.dot(cells, weight, preferred_element_type=jnp.float32).astype(jnp.bfloat16)
        got = got.reshape(2, rows, cols, wide)
        lanes = slice(d * wide, (d + 1) * wide)
        out[pl.ds(core * rows, rows), :, lanes] = got[0]
        out[pl.ds((1 - core) * rows, rows), :, lanes] = got[1]


def project(place, own, other, weights):
    rows, cols, depth = own.shape
    wide = 3 * weights[0].shape[2] * len(weights)
    vmem = pl.BlockSpec(memory_space=pltpu.VMEM)
    return pl.pallas_call(
        project_body,
        out_shape=jax.ShapeDtypeStruct((2 * rows, cols, wide), jnp.bfloat16),
        in_specs=[pl.BlockSpec(memory_space=pltpu.SMEM)] + [vmem] * 6,
        out_specs=vmem,
        compiler_params=pltpu.CompilerParams(vmem_limit_bytes=16 * 2**20),
        cost_estimate=pl.CostEstimate(
            flops=4 * rows * cols * depth * wide, bytes_accessed=4 * 2**20, transcendentals=0
        ),
        name="project",
    )(place, own, other, *weights)


def head_body(d, scale, place, bias, p0, p1, p2, p3, out_ref):
    slots = (p0, p1, p2, p3)
    col, flip = place[1], place[2]
    rows, cols, _ = p0.shape
    size = out_ref.shape[3]
    span = WIN * 4 * cols

    def load(at, which):
        lane = (3 * d + which) * size
        return jnp.concatenate(
            [p[at : at + WIN, :, lane : lane + size].reshape(WIN * cols, size) for p in slots],
            axis=0,
        )

    def row_of(dim):
        return (lax.broadcasted_iota(jnp.int32, (span, span), dim) // cols) % WIN

    q_row, k_row = row_of(0), row_of(1)
    above = jnp.where(k_row >= q_row, 0.0, NEG)
    below = jnp.where(k_row <= q_row, 0.0, NEG)
    ones = jnp.ones((span, size), jnp.bfloat16)
    steps = (rows - 2 * WIN) // WIN
    half = steps // 2
    for r in range(steps):
        query = load(WIN + r * WIN, 0)
        parts = []
        for part in range(3):
            score = lax.dot_general(
                query,
                load((r + part) * WIN, 1),
                (((1,), (1,)), ((), ())),
                preferred_element_type=jnp.float32,
            ) * scale
            if part == 0:
                score = score + above
                if r == 0:
                    score = score + bias[0]
            if part == 2:
                score = score + below
                if r == steps - 1:
                    score = score + bias[1]
            parts.append(score)
        peak = jnp.max(jnp.maximum(jnp.maximum(parts[0], parts[1]), parts[2]), axis=1, keepdims=True)
        total = None
        for part in range(3):
            prob = jnp.exp2(parts[part] - peak).astype(jnp.bfloat16)
            value = jnp.concatenate([load((r + part) * WIN, 2), ones], axis=1)
            term = jnp.dot(prob, value, preferred_element_type=jnp.float32)
            total = term if total is None else total + term
        result = (total[:, :size] / total[:, size:]).astype(jnp.bfloat16)
        result = result.reshape(4, WIN, cols, size)
        at = (r % half) * WIN
        for slot in range(4):
            out_ref[(r // half) ^ flip, at : at + WIN, pl.ds((col ^ slot) * cols, cols), :] = result[slot]


def one_head(d, size, place, bias, slots):
    rows, cols, _ = slots[0].shape
    vmem = pl.BlockSpec(memory_space=pltpu.VMEM)
    queries = (rows - 2 * WIN) * 4 * cols
    return pl.pallas_call(
        functools.partial(head_body, d, math.log2(math.e) * size**-0.5),
        out_shape=jax.ShapeDtypeStruct((2, rows // 2 - WIN, 4 * cols, size), jnp.bfloat16),
        in_specs=[pl.BlockSpec(memory_space=pltpu.SMEM)] * 2 + [vmem] * 4,
        out_specs=vmem,
        compiler_params=pltpu.CompilerParams(vmem_limit_bytes=16 * 2**20),
        cost_estimate=pl.CostEstimate(
            flops=6 * queries * 12 * 4 * cols * size,
            bytes_accessed=2**20,
            transcendentals=queries * 12 * 4 * cols,
        ),
        name="head",
    )(place, bias, *slots)


def activated(cells, gain):
    cells = cells.astype(jnp.float32)
    rms = lax.rsqrt(jnp.mean(cells * cells, axis=-1, keepdims=True) + 1e-06)
    scaled = cells * rms * gain
    return scaled / (1.0 + jnp.exp(-scaled))


def conv_body(
    place_ref, own, before, after, rim, rim_before, rim_after, left, right, gain, w_ref,
    block_ref, keep_ref, give_ref, taps, raw, left_n, right_n, sums,
):
    core, frame = place_ref[0], place_ref[2]
    frames, h_dev, w_dev, channels = own.shape
    rim_rows = rim.shape[1]
    far = rim_rows - 1
    rows = h_dev + far - 1
    own_at = jnp.where(core == 0, far, 1)
    far_at = jnp.where(core == 0, 0, h_dev + 1)
    near_at = jnp.where(core == 0, h_dev + far, 0)
    scale = gain[...].reshape(1, 1, channels)

    for side_ref, to in ((left, left_n), (right, right_n)):
        to[...] = activated(side_ref[...], scale)
    col = lax.broadcasted_iota(jnp.int32, (1, w_dev, channels), 1)

    def put(source, lead, t, start, count, at, skip, keep_raw):
        raw_cells = source[lead, start : start + count]
        if keep_raw:
            raw[t - 1, pl.ds(at, count)] = raw_cells
        cells = activated(raw_cells, scale)
        flat = cells.reshape(count * w_dev, channels)
        back = pltpu.roll(flat, 1, 0).reshape(cells.shape)
        ahead = pltpu.roll(flat, count * w_dev - 1, 0).reshape(cells.shape)
        lo = left_n[t, skip : skip + count].reshape(count, 1, channels)
        hi = right_n[t, skip : skip + count].reshape(count, 1, channels)
        to = taps.at[t, pl.ds(at, count)]
        to[:, :, :channels] = jnp.where(col == 0, lo, back).astype(jnp.bfloat16)
        to[:, :, channels : 2 * channels] = cells.astype(jnp.bfloat16)
        to[:, :, 2 * channels :] = jnp.where(col == w_dev - 1, hi, ahead).astype(jnp.bfloat16)

    for t in range(frames + 2):
        if t == 0:
            main, edge, lead = before, rim_before, 0
        elif t == frames + 1:
            main, edge, lead = after, rim_after, 0
        else:
            main, edge, lead = own, rim, t - 1
        inner = 0 < t <= frames
        for start in range(0, h_dev, 8):
            put(main, lead, t, start, 8, own_at + start, start, inner)
        put(edge, lead, t, 0, far, far_at, h_dev, inner)
        put(edge, lead, t, far, 1, near_at, h_dev + far, inner)

    half = rows // 2
    pieces = channels // LANES

    def convolve(t, start):
        parts = [
            taps[t + a, pl.ds(start + b, half)].reshape(half * w_dev, 3 * channels)
            for a in range(3)
            for b in range(3)
        ]
        total = jnp.dot(parts[0], w_ref[0], preferred_element_type=jnp.float32)
        for i in range(1, 9):
            total = total + jnp.dot(parts[i], w_ref[i], preferred_element_type=jnp.float32)
        return total

    for k, out in ((0, keep_ref), (1, give_ref)):
        t = frame ^ k

        def chunk(j, _):
            start = j * half
            total = convolve(t, start)
            base = raw[t, pl.ds(start + 1, half)].astype(jnp.float32)
            total = (total.reshape(half, w_dev, channels) + base).astype(jnp.bfloat16)
            block = total.astype(jnp.float32)
            for piece in range(pieces):
                sums[piece, pl.ds(start, half)] = block[:, :, piece * LANES : (piece + 1) * LANES]
            return 0

        lax.fori_loop(0, 2, chunk, 0)
        for piece in range(pieces):
            lanes = slice(piece * LANES, (piece + 1) * LANES)
            block_ref[t, :, :, lanes] = sums[piece, pl.ds(own_at - 1, h_dev)].astype(jnp.bfloat16)
            for dw in range(2):
                picked = sums[piece, :, pl.ds(dw, w_dev // 2, stride=2), :].astype(jnp.bfloat16)
                picked = picked.reshape(rows // 2, 2, w_dev // 2, LANES)
                for dh in range(2):
                    at = (2 * dh + dw) * channels + piece * LANES
                    out[:, :, at : at + LANES] = picked[:, dh]


def conv_block(place, own, before, after, rim, rim_before, rim_after, left, right, gain, weight):
    frames, h_dev, w_dev, channels = own.shape
    rows = h_dev + rim.shape[1] - 2
    vmem = pl.BlockSpec(memory_space=pltpu.VMEM)
    patch = jax.ShapeDtypeStruct((rows // 2, w_dev // 2, 4 * channels), jnp.bfloat16)
    return pl.pallas_call(
        conv_body,
        out_shape=(jax.ShapeDtypeStruct(own.shape, jnp.bfloat16), patch, patch),
        in_specs=[pl.BlockSpec(memory_space=pltpu.SMEM)] + [vmem] * 10,
        out_specs=(vmem, vmem, vmem),
        scratch_shapes=[
            pltpu.VMEM((frames + 2, rows + 2, w_dev, 3 * channels), jnp.bfloat16),
            pltpu.VMEM((frames, rows + 2, w_dev, channels), jnp.bfloat16),
            pltpu.VMEM(left.shape, jnp.float32),
            pltpu.VMEM(left.shape, jnp.float32),
            pltpu.VMEM((channels // LANES, rows, w_dev, LANES), jnp.float32),
        ],
        compiler_params=pltpu.CompilerParams(vmem_limit_bytes=40 * 2**20),
        cost_estimate=pl.CostEstimate(
            flops=2 * 27 * frames * rows * w_dev * channels * channels,
            bytes_accessed=8 * 2**20,
            transcendentals=2**20,
        ),
        name="conv",
    )(place, own, before, after, rim, rim_before, rim_after, left, right, gain, weight)


def ends(cells, axis, dim, width):
    count = lax.axis_size(axis)
    head = lax.slice_in_dim(cells, 0, width, axis=dim)
    tail = lax.slice_in_dim(cells, cells.shape[dim] - width, cells.shape[dim], axis=dim)
    return (
        lax.ppermute(tail, axis, [(i, i + 1) for i in range(count - 1)]),
        lax.ppermute(head, axis, [(i + 1, i) for i in range(count - 1)]),
    )


def block_and_attention(latents, norm_gain, conv_weight, qkv_weight):
    t_dev, h_dev, w_dev, channels = latents.shape
    n_ta, n_ha, n_wa = lax.axis_size("ta"), lax.axis_size("ha"), lax.axis_size("wa")
    a, h, w = lax.axis_index("ta"), lax.axis_index("ha"), lax.axis_index("wa")
    core, frame = h % 2, w % 2
    reach = 2 * WIN

    def everywhere(to):
        pairs = []
        for ta in range(n_ta):
            for ha in range(n_ha):
                for wa in range(n_wa):
                    dest = to(ta, ha, wa)
                    if dest is not None:
                        ta2, ha2, wa2 = dest
                        pairs.append(
                            ((ta * n_ha + ha) * n_wa + wa, (ta2 * n_ha + ha2) * n_wa + wa2)
                        )
        return pairs

    axes = ("ta", "ha", "wa")
    head, tail = latents[:, : reach + 1], latents[:, h_dev - reach - 1 :]
    first = core == 0
    odd = [(i, i + 1) for i in range(1, n_ha - 1, 2)]
    rim_far = lax.ppermute(jnp.where(first, head, tail), "ha", odd + [(j, i) for i, j in odd])
    before, after = ends(latents, "ta", 0, 1)
    rim_near = lax.ppermute(
        jnp.where(first, tail[:, reach:], head[:, :1]), "ha", [(i, i ^ 1) for i in range(n_ha)]
    )
    rim = jnp.concatenate([rim_far, rim_near], axis=1)
    rim_before, rim_after = ends(rim, "ta", 0, 1)
    last = w_dev - 1

    def side(at):
        return jnp.concatenate(
            [
                jnp.concatenate([x[:, :, at] for x in (before, latents, after)], axis=0),
                jnp.concatenate([x[:, :, at] for x in (rim_before, rim, rim_after)], axis=0),
            ],
            axis=1,
        )

    left = lax.ppermute(side(last), "wa", [(i, i + 1) for i in range(n_wa - 1)])
    right = lax.ppermute(side(0), "wa", [(i + 1, i) for i in range(n_wa - 1)])
    place = jnp.stack([core, w, frame]).astype(jnp.int32)

    mine = qkv_weight[:, 0].transpose(1, 0, 2)
    swapped = lax.ppermute(
        mine,
        axes,
        everywhere(lambda ta, ha, wa: (ta, ha, wa ^ 1) if (wa ^ 1) % 2 != ha % 2 else None),
    )
    mine = jnp.where(core == frame, mine, swapped)
    weights = [mine] + [
        lax.ppermute(mine, "ta", [(i, (i + d) % n_ta) for i in range(n_ta)])
        for d in range(1, n_ta)
    ]

    block_out, keep, give = conv_block(
        place, latents, before, after, rim, rim_before, rim_after, left, right,
        norm_gain[None], conv_weight.reshape(9, 3 * channels, channels),
    )
    own = [keep] + [
        lax.ppermute(give if d % 2 else keep, "wa", [(i, i ^ d) for i in range(n_wa)])
        for d in range(1, n_wa)
    ]
    other = [lax.ppermute(x, "ha", [(j, j ^ 1) for j in range(n_ha)]) for x in own]

    chip = h // 2
    bias = jnp.stack(
        [jnp.where(chip == 0, NEG, 0.0), jnp.where(chip == n_ha // 2 - 1, NEG, 0.0)]
    ).astype(jnp.float32)
    slots = [project(place, own[i], other[i], weights) for i in range(4)]
    result = None
    for d in range(n_ta - 1, -1, -1):
        out = one_head(d, qkv_weight.shape[3], place, bias, slots)
        for kind in range(2):
            moved = lax.ppermute(
                out[kind],
                axes,
                everywhere(
                    lambda ta, ha, wa: (
                        (ta - d) % n_ta,
                        ha - ha % 2 + (wa % 2) ^ kind,
                        wa - wa % 2 + ha % 2,
                    )
                ),
            )
            if result is None:
                result = jnp.zeros((n_ta * t_dev,) + moved.shape, moved.dtype)
            at = (a + d) % n_ta * t_dev + (core ^ kind)
            result = lax.dynamic_update_slice_in_dim(result, moved[None], at, 0)
    return block_out, result[:, :, :, None, :]


def solution(mesh):
    return jax.shard_map(
        block_and_attention,
        mesh=mesh,
        in_specs=(P("ta", "ha", "wa", None), P(), P(), P(None, ("ta", "wa"), None, None)),
        out_specs=(P("ta", "ha", "wa", None), P(None, "ha", None, ("ta", "wa"), None)),
        check_vma=False,
    )
```

time: 311 us -> 161 us (0.52)
  the two profiles are of different devices: /device:TPU:67 before, /device:TPU:3 now
where the time goes in v2:
time: 161 us; the launch traced here: 158 us
  starting transfers between devices  65.5 us (41%)
  waiting for transfers between devices  50.3 us (31%)
  Pallas kernels  29.3 us (18%)
  local copies, waits for them, and re-layouts  11.2 us (7%)
    ppermute x3, starting transfers between devices, block_and_attention(): lax.ppermute(give if d % 2 else keep, 'wa', [(i, i ^ d) for i in range(n_...  23.5 us
    ppermute x3, waiting for transfers between devices, block_and_attention(): lax.ppermute(give if d % 2 else keep, 'wa', [(i, i ^ d) for i in range(n_...  17 us
    ppermute x1, waiting for transfers between devices, block_and_attention(): lax.ppermute(jnp.where(first, head, tail), 'ha', odd + [(j, i) for i, j i...  13.1 us
    pallas_call x4, Pallas kernels, project(): pl.pallas_call(project_body, out_shape=jax.ShapeDtypeStruct((2 * rows, co...  11 us
    ppermute x8, waiting for transfers between devices, block_and_attention(): lax.ppermute(out[kind], axes, everywhere(lambda ta, ha, wa: ((ta - d) % n...  10.7 us
    ppermute x8, starting transfers between devices, block_and_attention(): lax.ppermute(out[kind], axes, everywhere(lambda ta, ha, wa: ((ta - d) % n...  10.4 us
    pallas_call x1, Pallas kernels, conv_block(): pl.pallas_call(conv_body, out_shape=(jax.ShapeDtypeStruct(own.shape, jnp....  10.2 us
    ppermute x1, starting transfers between devices, block_and_attention(): lax.ppermute(jnp.where(first, head, tail), 'ha', odd + [(j, i) for i, j i...  9.51 us
  transfers between devices with their start and end apart: 27, of which 12 were waited for; matrix products, arithmetic and copies ran while one was open for 4% of the time, Pallas kernels for 12%

profile of v2, /device:TPU:3, one launch (start us, length us, event | category | flops | bytes accessed | tf_op | source)
XLA Modules:
  0.0 158.4 jit_solution(3065221415062987655)
XLA Ops:
  2.2 9.5 %collective-permute-start.2 = (bf16[2,9,32,256]{3,1,2,0:T(8,128)(2,1)S(1)}, bf16[2,9,32,256]{3,1,2,0:T(8,128)(2,1)S(1)}, u32[]{:S(2)}, u32[]{:S(2)}) collective-permute-start(bf16[2,9,32,256]{3,1,2,0:T(8,128)(2,1)S(1)} %copy_select_fusion), channel_id=1, source_target_pairs={{4,8},{12,16},{20,24},{28,32},{36,40},{44,48},{52,56},{8,4},{16,12... | collective-permute-start | bytes 884744 | tf_op jit(solution)/shard_map/ppermute | solution.py:278
  12.8 3.2 %collective-permute-start = (bf16[1,16,32,256]{3,1,2,0:T(8,128)(2,1)}, bf16[1,16,32,256]{3,1,2,0:T(8,128)(2,1)S(1)}, u32[]{:S(2)}, u32[]{:S(2)}) collective-permute-start(bf16[1,16,32,256]{3,1,2,0:T(8,128)(2,1)} %copy.27), channel_id=1, source_target_pairs={{0,64},{64,128},{128,192},{1,65},{65,129},{129,193},{2,66},{66,130... | collective-permute-start | bytes 786440 | tf_op jit(solution)/shard_map/ppermute | solution.py:249
  18.2 1.3 collective-permute-start.9
  21.5 13.1 %collective-permute-done.2 = bf16[2,9,32,256]{3,1,2,0:T(8,128)(2,1)S(1)} collective-permute-done((bf16[2,9,32,256]{3,1,2,0:T(8,128)(2,1)S(1)}, bf16[2,9,32,256]{3,1,2,0:T(8,128)(2,1)S(1)}, u32[]{:S(2)}, u32[]{:S(2)}) %collective-permute-start.2) | collective-permute-done | bytes 294944 | tf_op jit(solution)/shard_map/ppermute | solution.py:278
  34.7 3.2 %collective-permute-start.4 = (bf16[1,10,32,256]{3,1,2,0:T(8,128)(2,1)S(1)}, bf16[1,10,32,256]{3,1,2,0:T(8,128)(2,1)S(1)}, u32[]{:S(2)}, u32[]{:S(2)}) collective-permute-start(bf16[1,10,32,256]{3,1,2,0:T(8,128)(2,1)S(1)} %get-tuple-element.11), channel_id=1, source_target_pairs={{0,64},{64,128},{128,192},{1,65},{65,129},{129,193},{2,66},{66,130... | collective-permute-start | bytes 491528 | tf_op jit(solution)/shard_map/ppermute | solution.py:249
  39.8 1.3 collective-permute-start.5
  41.1 2.2 %collective-permute-done.4 = bf16[1,10,32,256]{3,1,2,0:T(8,128)(2,1)S(1)} collective-permute-done((bf16[1,10,32,256]{3,1,2,0:T(8,128)(2,1)S(1)}, bf16[1,10,32,256]{3,1,2,0:T(8,128)(2,1)S(1)}, u32[]{:S(2)}, u32[]{:S(2)}) %collective-permute-start.4) | collective-permute-done | bytes 163872 | tf_op jit(solution)/shard_map/ppermute | solution.py:249
  43.4 5.7 %collective-permute-done.5 = bf16[1,10,32,256]{3,1,2,0:T(8,128)(2,1)S(1)} collective-permute-done((bf16[1,10,32,256]{3,1,2,0:T(8,128)(2,1)S(1)}, bf16[1,10,32,256]{3,1,2,0:T(8,128)(2,1)S(1)}, u32[]{:S(2)}, u32[]{:S(2)}) %collective-permute-start.5) | collective-permute-done | bytes 163872 | tf_op jit(solution)/shard_map/ppermute | solution.py:250
  50.4 4.1 %collective-permute-start.6 = (bf16[4,26,256]{2,1,0:T(8,128)(2,1)S(1)}, bf16[4,26,256]{2,1,0:T(8,128)(2,1)S(1)}, u32[]{:S(2)}, u32[]{:S(2)}) collective-permute-start(bf16[4,26,256]{2,1,0:T(8,128)(2,1)S(1)} %maximum_maximum_fusion), channel_id=1, source_target_pairs={{0,1},{1,2},{2,3},{4,5},{5,6},{6,7},{8,9},{9,10},{10,11},{12,13},{... | collective-permute-start | bytes 159752 | tf_op jit(solution)/shard_map/ppermute | solution.py:296
  55.8 10.2 %conv.1 = (bf16[2,16,32,256]{3,2,1,0:T(8,128)(2,1)}, bf16[12,16,1024]{2,1,0:T(8,128)(2,1)S(1)}, bf16[12,16,1024]{2,1,0:T(8,128)(2,1)S(1)}) custom-call(s32[3]{0:T(128)S(1)} %pad_add_fusion.place_ref.place, bf16[2,16,32,256]{3,2,1,0:T(8,128)(2,1)S(1)} %copy-done, bf16[1,16,32,256]{3,2,1,0:T(8,128)(2,1)S(1)} %copy.14.before, ...), custom_call_target="tpu_custom_call" | custom-call | flops 5435817984 | bytes 8388608 | tf_op jit(solution)/shard_map/conv/pallas_call | solution.py:222
  66.0 3.2 %collective-permute-start.17 = (bf16[12,16,1024]{2,1,0:T(8,128)(2,1)S(1)}, bf16[12,16,1024]{2,1,0:T(8,128)(2,1)S(1)}, u32[]{:S(2)}, u32[]{:S(2)}) collective-permute-start(bf16[12,16,1024]{2,1,0:T(8,128)(2,1)S(1)} %get-tuple-element.7), channel_id=1, source_target_pairs={{0,3},{1,2},{2,1},{3,0},{4,7},{5,6},{6,5},{7,4},{8,11},{9,10},{10,... | collective-permute-start | bytes 1179656 | tf_op jit(solution)/shard_map/ppermute | solution.py:317
  69.3 1.4 collective-permute-start.10
  70.7 1.4 collective-permute-start.11
  72.1 2.0 %collective-permute-start.12 = (bf16[3,1024,128]{2,1,0:T(8,128)(2,1)S(1)}, bf16[3,1024,128]{2,1,0:T(8,128)(2,1)S(1)}, u32[]{:S(2)}, u32[]{:S(2)}) collective-permute-start(bf16[3,1024,128]{2,1,0:T(8,128)(2,1)S(1)} %broadcast_select_fusion.w0), channel_id=1, source_target_pairs={{0,192},{64,0},{128,64},{192,128},{1,193},{65,1},{129,65},{193,129... | collective-permute-start | bytes 2359304 | tf_op jit(solution)/shard_map/ppermute | solution.py:308
  74.1 1.6 %collective-permute-done.17.own = bf16[12,16,1024]{2,1,0:T(8,128)(2,1)S(1)} collective-permute-done((bf16[12,16,1024]{2,1,0:T(8,128)(2,1)S(1)}, bf16[12,16,1024]{2,1,0:T(8,128)(2,1)S(1)}, u32[]{:S(2)}, u32[]{:S(2)}) %collective-permute-start.17) | collective-permute-done | bytes 393248 | tf_op jit(solution)/shard_map/ppermute | solution.py:317
  75.7 20.2 %collective-permute-start.13 = (bf16[12,16,1024]{2,1,0:T(8,128)(2,1)S(1)}, bf16[12,16,1024]{2,1,0:T(8,128)(2,1)}, u32[]{:S(2)}, u32[]{:S(2)}) collective-permute-start(bf16[12,16,1024]{2,1,0:T(8,128)(2,1)S(1)} %get-tuple-element.7), channel_id=1, source_target_pairs={{0,1},{1,0},{2,3},{3,2},{4,5},{5,4},{6,7},{7,6},{8,9},{9,8},{10,11... | collective-permute-start | bytes 1179656 | tf_op jit(solution)/shard_map/ppermute | solution.py:317
  95.9 8.3 %collective-permute-done.15.own = bf16[12,16,1024]{2,1,0:T(8,128)(2,1)} collective-permute-done((bf16[12,16,1024]{2,1,0:T(8,128)(2,1)S(1)}, bf16[12,16,1024]{2,1,0:T(8,128)(2,1)}, u32[]{:S(2)}, u32[]{:S(2)}) %collective-permute-start.15) | collective-permute-done | bytes 393248 | tf_op jit(solution)/shard_map/ppermute | solution.py:317
  105.5 7.1 %collective-permute-done.13.own = bf16[12,16,1024]{2,1,0:T(8,128)(2,1)} collective-permute-done((bf16[12,16,1024]{2,1,0:T(8,128)(2,1)S(1)}, bf16[12,16,1024]{2,1,0:T(8,128)(2,1)}, u32[]{:S(2)}, u32[]{:S(2)}) %collective-permute-start.13) | collective-permute-done | bytes 393248 | tf_op jit(solution)/shard_map/ppermute | solution.py:317
  116.5 2.3 %project.7.p3 = bf16[24,16,1536]{2,1,0:T(8,128)(2,1)S(1)} custom-call(s32[3]{0:T(128)S(1)} %pad_add_fusion.place_ref.place, bf16[12,16,1024]{2,1,0:T(8,128)(2,1)S(1)} %copy-done.2, bf16[12,16,1024]{2,1,0:T(8,128)(2,1)S(1)} %copy-done.4, bf16[3,1024,128]{2,1,0:T(8,128)(2,1)S(1)} %broadcast_select_fusion.w0, ...), custom_call_target="tpu_custom_call" | custom-call | flops 1207959552 | bytes 4194304 | tf_op jit(solution)/shard_map/project/pallas_call | solution.py:37
  118.8 2.9 %project.6.p2 = bf16[24,16,1536]{2,1,0:T(8,128)(2,1)S(1)} custom-call(s32[3]{0:T(128)S(1)} %pad_add_fusion.place_ref.place, bf16[12,16,1024]{2,1,0:T(8,128)(2,1)} %collective-permute-done.15.own, bf16[12,16,1024]{2,1,0:T(8,128)(2,1)} %collective-permute-done.16.other, bf16[3,1024,128]{2,1,0:T(8,128)(2,1)S(1)} %broadcast_select_fusion.w0, ...), custom_call_target="tpu_custom_call" | custom-call | flops 1207959552 | bytes 4194304 | tf_op jit(solution)/shard_map/project/pallas_call | solution.py:37
  121.7 2.9 %project.5.p1 = bf16[24,16,1536]{2,1,0:T(8,128)(2,1)S(1)} custom-call(s32[3]{0:T(128)S(1)} %pad_add_fusion.place_ref.place, bf16[12,16,1024]{2,1,0:T(8,128)(2,1)} %collective-permute-done.13.own, bf16[12,16,1024]{2,1,0:T(8,128)(2,1)} %collective-permute-done.14.other, bf16[3,1024,128]{2,1,0:T(8,128)(2,1)S(1)} %broadcast_select_fusion.w0, ...), custom_call_target="tpu_custom_call" | custom-call | flops 1207959552 | bytes 4194304 | tf_op jit(solution)/shard_map/project/pallas_call | solution.py:37
  124.7 2.8 %project.4.p0 = bf16[24,16,1536]{2,1,0:T(8,128)(2,1)S(1)} custom-call(s32[3]{0:T(128)S(1)} %pad_add_fusion.place_ref.place, bf16[12,16,1024]{2,1,0:T(8,128)(2,1)S(1)} %get-tuple-element.6.own, bf16[12,16,1024]{2,1,0:T(8,128)(2,1)} %collective-permute-done.8.other, bf16[3,1024,128]{2,1,0:T(8,128)(2,1)S(1)} %broadcast_select_fusion.w0, ...), custom_call_target="tpu_custom_call" | custom-call | flops 1207959552 | bytes 4194304 | tf_op jit(solution)/shard_map/project/pallas_call | solution.py:37
  127.5 2.0 %head.7 = bf16[2,8,64,128]{3,2,1,0:T(8,128)(2,1)S(1)} custom-call(s32[3]{0:T(128)S(1)} %pad_add_fusion.place_ref.place, f32[2]{0:T(128)S(1)} %pad_maximum_fusion.1.bias, bf16[24,16,1536]{2,1,0:T(8,128)(2,1)S(1)} %project.4.p0, bf16[24,16,1536]{2,1,0:T(8,128)(2,1)S(1)} %project.5.p1, bf16[24,16,1536]{2,1,0:T(8,128)(2,1)S(1)} %project.6.p2, ...), custom_call_target="tpu_custom_call" | custom-call | flops 603979776 | bytes 1048576 | tf_op jit(solution)/shard_map/head/pallas_call | solution.py:110
  129.5 2.0 %head.6 = bf16[2,8,64,128]{3,2,1,0:T(8,128)(2,1)S(1)} custom-call(s32[3]{0:T(128)S(1)} %pad_add_fusion.place_ref.place, f32[2]{0:T(128)S(1)} %pad_maximum_fusion.1.bias, bf16[24,16,1536]{2,1,0:T(8,128)(2,1)S(1)} %project.4.p0, bf16[24,16,1536]{2,1,0:T(8,128)(2,1)S(1)} %project.5.p1, bf16[24,16,1536]{2,1,0:T(8,128)(2,1)S(1)} %project.6.p2, ...), custom_call_target="tpu_custom_call" | custom-call | flops 603979776 | bytes 1048576 | tf_op jit(solution)/shard_map/head/pallas_call | solution.py:110
  131.6 2.0 %head.5 = bf16[2,8,64,128]{3,2,1,0:T(8,128)(2,1)S(1)} custom-call(s32[3]{0:T(128)S(1)} %pad_add_fusion.place_ref.place, f32[2]{0:T(128)S(1)} %pad_maximum_fusion.1.bias, bf16[24,16,1536]{2,1,0:T(8,128)(2,1)S(1)} %project.4.p0, bf16[24,16,1536]{2,1,0:T(8,128)(2,1)S(1)} %project.5.p1, bf16[24,16,1536]{2,1,0:T(8,128)(2,1)S(1)} %project.6.p2, ...), custom_call_target="tpu_custom_call" | custom-call | flops 603979776 | bytes 1048576 | tf_op jit(solution)/shard_map/head/pallas_call | solution.py:110
  133.6 2.0 %head.4 = bf16[2,8,64,128]{3,2,1,0:T(8,128)(2,1)S(1)} custom-call(s32[3]{0:T(128)S(1)} %pad_add_fusion.place_ref.place, f32[2]{0:T(128)S(1)} %pad_maximum_fusion.1.bias, bf16[24,16,1536]{2,1,0:T(8,128)(2,1)S(1)} %project.4.p0, bf16[24,16,1536]{2,1,0:T(8,128)(2,1)S(1)} %project.5.p1, bf16[24,16,1536]{2,1,0:T(8,128)(2,1)S(1)} %project.6.p2, ...), custom_call_target="tpu_custom_call" | custom-call | flops 603979776 | bytes 1048576 | tf_op jit(solution)/shard_map/head/pallas_call | solution.py:110
  135.7 1.9 %collective-permute-start.25 = (bf16[8,64,128]{2,1,0:T(8,128)(2,1)S(1)}, bf16[8,64,128]{2,1,0:T(8,128)(2,1)S(1)}, u32[]{:S(2)}, u32[]{:S(2)}) collective-permute-start(bf16[8,64,128]{2,1,0:T(8,128)(2,1)S(1)} %get-tuple-element.21), channel_id=1, source_target_pairs={{0,0},{1,4},{2,2},{3,6},{4,1},{5,5},{6,3},{7,7},{8,8},{9,12},{10,1... | collective-permute-start | bytes 393224 | tf_op jit(solution)/shard_map/ppermute | solution.py:331
  137.7 2.2 %collective-permute-start.23 = (bf16[8,64,128]{2,1,0:T(8,128)(2,1)S(1)}, bf16[8,64,128]{2,1,0:T(8,128)(2,1)S(1)}, u32[]{:S(2)}, u32[]{:S(2)}) collective-permute-start(bf16[8,64,128]{2,1,0:T(8,128)(2,1)S(1)} %get-tuple-element.23), channel_id=1, source_target_pairs={{0,192},{1,196},{2,194},{3,198},{4,193},{5,197},{6,195},{7,199},{8... | collective-permute-start | bytes 393224 | tf_op jit(solution)/shard_map/ppermute | solution.py:331
  140.6 4.3 %collective-permute-start.21 = (bf16[8,64,128]{2,1,0:T(8,128)(2,1)S(1)}, bf16[8,64,128]{2,1,0:T(8,128)(2,1)S(1)}, u32[]{:S(2)}, u32[]{:S(2)}) collective-permute-start(bf16[8,64,128]{2,1,0:T(8,128)(2,1)S(1)} %get-tuple-element.25), channel_id=1, source_target_pairs={{0,128},{1,132},{2,130},{3,134},{4,129},{5,133},{6,131},{7,135},{8... | collective-permute-start | bytes 393224 | tf_op jit(solution)/shard_map/ppermute | solution.py:331
  144.9 1.7 %collective-permute-done.19 = bf16[8,64,128]{2,1,0:T(8,128)(2,1)S(1)} collective-permute-done((bf16[8,64,128]{2,1,0:T(8,128)(2,1)S(1)}, bf16[8,64,128]{2,1,0:T(8,128)(2,1)S(1)}, u32[]{:S(2)}, u32[]{:S(2)}) %collective-permute-start.19) | collective-permute-done | bytes 131104 | tf_op jit(solution)/shard_map/ppermute | solution.py:331
  147.1 5.7 %collective-permute-done.20 = bf16[8,64,128]{2,1,0:T(8,128)(2,1)S(1)} collective-permute-done((bf16[8,64,128]{2,1,0:T(8,128)(2,1)S(1)}, bf16[8,64,128]{2,1,0:T(8,128)(2,1)S(1)}, u32[]{:S(2)}, u32[]{:S(2)}) %collective-permute-start.20) | collective-permute-done | bytes 131104 | tf_op jit(solution)/shard_map/ppermute | solution.py:331
  154.3 3.1 %collective-permute-done.24 = bf16[8,64,128]{2,1,0:T(8,128)(2,1)S(1)} collective-permute-done((bf16[8,64,128]{2,1,0:T(8,128)(2,1)S(1)}, bf16[8,64,128]{2,1,0:T(8,128)(2,1)S(1)}, u32[]{:S(2)}, u32[]{:S(2)}) %collective-permute-start.24) | collective-permute-done | bytes 131104 | tf_op jit(solution)/shard_map/ppermute | solution.py:331
  (93 shorter events, 20.3 us)
Async XLA Ops:
  0.6 11.0 %copy-start = (bf16[2,16,32,256]{3,2,1,0:T(8,128)(2,1)S(1)}, bf16[2,16,32,256]{3,2,1,0:T(8,128)(2,1)}, u32[]{:S(2)}) copy-start(bf16[2,16,32,256]{3,2,1,0:T(8,128)(2,1)} %own.1) | copy-start | bytes 1572868
  2.1 16.0 %copy-start.8 = (bf16[1024,1,3,128]{3,0,2,1:T(8,128)(2,1)S(1)}, bf16[1024,1,3,128]{3,0,2,1:T(8,128)(2,1)}, u32[]{:S(2)}) copy-start(bf16[1024,1,3,128]{3,0,2,1:T(8,128)(2,1)} %param.7) | copy-start | bytes 2359300
  2.2 32.4 %collective-permute-start.2 = (bf16[2,9,32,256]{3,1,2,0:T(8,128)(2,1)S(1)}, bf16[2,9,32,256]{3,1,2,0:T(8,128)(2,1)S(1)}, u32[]{:S(2)}, u32[]{:S(2)}) collective-permute-start(bf16[2,9,32,256]{3,1,2,0:T(8,128)(2,1)S(1)} %copy_select_fusion), channel_id=1, source_target_pairs={{4,8},{12,16},{20,24},{28,32},{36,40},{44,48},{52,56},{8,4},{16,12... | collective-permute-start | bytes 884744 | tf_op jit(solution)/shard_map/ppermute | solution.py:278
  11.8 9.7 %collective-permute-start.3 = (bf16[2,1,32,256]{3,1,2,0:T(2,128)(2,1)S(1)}, bf16[2,1,32,256]{3,1,2,0:T(2,128)(2,1)S(1)}, u32[]{:S(2)}, u32[]{:S(2)}) collective-permute-start(bf16[2,1,32,256]{3,1,2,0:T(2,128)(2,1)S(1)} %broadcast_select_fusion.1), channel_id=1, source_target_pairs={{0,4},{4,0},{8,12},{12,8},{16,20},{20,16},{24,28},{28,24},{32,36},... | collective-permute-start | bytes 98312 | tf_op jit(solution)/shard_map/ppermute | solution.py:280
  12.8 8.7 %collective-permute-start = (bf16[1,16,32,256]{3,1,2,0:T(8,128)(2,1)}, bf16[1,16,32,256]{3,1,2,0:T(8,128)(2,1)S(1)}, u32[]{:S(2)}, u32[]{:S(2)}) collective-permute-start(bf16[1,16,32,256]{3,1,2,0:T(8,128)(2,1)} %copy.27), channel_id=1, source_target_pairs={{0,64},{64,128},{128,192},{1,65},{65,129},{129,193},{2,66},{66,130... | collective-permute-start | bytes 786440 | tf_op jit(solution)/shard_map/ppermute | solution.py:249
  16.9 21.1 %collective-permute-start.1 = (bf16[1,16,32,256]{3,1,2,0:T(8,128)(2,1)}, bf16[1,16,32,256]{3,1,2,0:T(8,128)(2,1)}, u32[]{:S(2)}, u32[]{:S(2)}) collective-permute-start(bf16[1,16,32,256]{3,1,2,0:T(8,128)(2,1)} %copy.28), channel_id=1, source_target_pairs={{64,0},{128,64},{192,128},{65,1},{129,65},{193,129},{66,2},{130,66... | collective-permute-start | bytes 786440 | tf_op jit(solution)/shard_map/ppermute | solution.py:250
  18.2 51.1 %collective-permute-start.9 = (bf16[3,1024,128]{2,1,0:T(8,128)(2,1)S(1)}, bf16[3,1024,128]{2,1,0:T(8,128)(2,1)S(1)}, u32[]{:S(2)}, u32[]{:S(2)}) collective-permute-start(bf16[3,1024,128]{2,1,0:T(8,128)(2,1)S(1)} %bitcast.87), channel_id=1, source_target_pairs={{0,1},{2,3},{5,4},{7,6},{8,9},{10,11},{13,12},{15,14},{16,17},{18,... | collective-permute-start | bytes 2359304 | tf_op jit(solution)/shard_map/ppermute | solution.py:301
  21.5 27.6 %copy-start.10 = (bf16[2,16,1,256]{3,1,0,2:T(8,128)(2,1)S(1)}, bf16[2,16,1,256]{3,1,0,2:T(8,128)(2,1)}, u32[]{:S(2)}) copy-start(bf16[2,16,1,256]{3,1,0,2:T(8,128)(2,1)} %copy.41) | copy-start | bytes 49156
  34.7 15.7 %copy-start.9 = (bf16[2,16,1,256]{3,1,0,2:T(8,128)(2,1)S(1)}, bf16[2,16,1,256]{3,1,0,2:T(8,128)(2,1)}, u32[]{:S(2)}) copy-start(bf16[2,16,1,256]{3,1,0,2:T(8,128)(2,1)} %copy.42) | copy-start | bytes 49156
  34.7 8.6 %collective-permute-start.4 = (bf16[1,10,32,256]{3,1,2,0:T(8,128)(2,1)S(1)}, bf16[1,10,32,256]{3,1,2,0:T(8,128)(2,1)S(1)}, u32[]{:S(2)}, u32[]{:S(2)}) collective-permute-start(bf16[1,10,32,256]{3,1,2,0:T(8,128)(2,1)S(1)} %get-tuple-element.11), channel_id=1, source_target_pairs={{0,64},{64,128},{128,192},{1,65},{65,129},{129,193},{2,66},{66,130... | collective-permute-start | bytes 491528 | tf_op jit(solution)/shard_map/ppermute | solution.py:249
  39.8 9.3 %collective-permute-start.5 = (bf16[1,10,32,256]{3,1,2,0:T(8,128)(2,1)S(1)}, bf16[1,10,32,256]{3,1,2,0:T(8,128)(2,1)S(1)}, u32[]{:S(2)}, u32[]{:S(2)}) collective-permute-start(bf16[1,10,32,256]{3,1,2,0:T(8,128)(2,1)S(1)} %get-tuple-element.10), channel_id=1, source_target_pairs={{64,0},{128,64},{192,128},{65,1},{129,65},{193,129},{66,2},{130,66... | collective-permute-start | bytes 491528 | tf_op jit(solution)/shard_map/ppermute | solution.py:250
  41.1 14.7 %copy-start.5 = (bf16[3,3,3,256,256]{4,3,2,1,0:T(8,128)(2,1)S(1)}, bf16[3,3,3,256,256]{4,3,2,1,0:T(8,128)(2,1)}, u32[]{:S(2)}) copy-start(bf16[3,3,3,256,256]{4,3,2,1,0:T(8,128)(2,1)} %param.6) | copy-start | bytes 10616836
  49.1 5.8 %collective-permute-start.7 = (bf16[4,26,256]{2,1,0:T(8,128)(2,1)S(1)}, bf16[4,26,256]{2,1,0:T(8,128)(2,1)S(1)}, u32[]{:S(2)}, u32[]{:S(2)}) collective-permute-start(bf16[4,26,256]{2,1,0:T(8,128)(2,1)S(1)} %maximum_maximum_fusion.1), channel_id=1, source_target_pairs={{1,0},{2,1},{3,2},{5,4},{6,5},{7,6},{9,8},{10,9},{11,10},{13,12},{... | collective-permute-start | bytes 159752 | tf_op jit(solution)/shard_map/ppermute | solution.py:297
  50.4 5.4 %collective-permute-start.6 = (bf16[4,26,256]{2,1,0:T(8,128)(2,1)S(1)}, bf16[4,26,256]{2,1,0:T(8,128)(2,1)S(1)}, u32[]{:S(2)}, u32[]{:S(2)}) collective-permute-start(bf16[4,26,256]{2,1,0:T(8,128)(2,1)S(1)} %maximum_maximum_fusion), channel_id=1, source_target_pairs={{0,1},{1,2},{2,3},{4,5},{5,6},{6,7},{8,9},{9,10},{10,11},{12,13},{... | collective-permute-start | bytes 159752 | tf_op jit(solution)/shard_map/ppermute | solution.py:296
  66.0 9.7 %collective-permute-start.17 = (bf16[12,16,1024]{2,1,0:T(8,128)(2,1)S(1)}, bf16[12,16,1024]{2,1,0:T(8,128)(2,1)S(1)}, u32[]{:S(2)}, u32[]{:S(2)}) collective-permute-start(bf16[12,16,1024]{2,1,0:T(8,128)(2,1)S(1)} %get-tuple-element.7), channel_id=1, source_target_pairs={{0,3},{1,2},{2,1},{3,0},{4,7},{5,6},{6,5},{7,4},{8,11},{9,10},{10,... | collective-permute-start | bytes 1179656 | tf_op jit(solution)/shard_map/ppermute | solution.py:317
  69.2 35.1 %collective-permute-start.15 = (bf16[12,16,1024]{2,1,0:T(8,128)(2,1)S(1)}, bf16[12,16,1024]{2,1,0:T(8,128)(2,1)}, u32[]{:S(2)}, u32[]{:S(2)}) collective-permute-start(bf16[12,16,1024]{2,1,0:T(8,128)(2,1)S(1)} %get-tuple-element.6.own), channel_id=1, source_target_pairs={{0,2},{1,3},{2,0},{3,1},{4,6},{5,7},{6,4},{7,5},{8,10},{9,11},{10,... | collective-permute-start | bytes 1179656 | tf_op jit(solution)/shard_map/ppermute | solution.py:317
  69.3 44.6 %collective-permute-start.10 = (bf16[3,1024,128]{2,1,0:T(8,128)(2,1)S(1)}, bf16[3,1024,128]{2,1,0:T(8,128)(2,1)S(1)}, u32[]{:S(2)}, u32[]{:S(2)}) collective-permute-start(bf16[3,1024,128]{2,1,0:T(8,128)(2,1)S(1)} %broadcast_select_fusion.w0), channel_id=1, source_target_pairs={{0,64},{64,128},{128,192},{192,0},{1,65},{65,129},{129,193},{193,1... | collective-permute-start | bytes 2359304 | tf_op jit(solution)/shard_map/ppermute | solution.py:308
  70.7 43.8 %collective-permute-start.11 = (bf16[3,1024,128]{2,1,0:T(8,128)(2,1)S(1)}, bf16[3,1024,128]{2,1,0:T(8,128)(2,1)S(1)}, u32[]{:S(2)}, u32[]{:S(2)}) collective-permute-start(bf16[3,1024,128]{2,1,0:T(8,128)(2,1)S(1)} %broadcast_select_fusion.w0), channel_id=1, source_target_pairs={{0,128},{64,192},{128,0},{192,64},{1,129},{65,193},{129,1},{193,65... | collective-permute-start | bytes 2359304 | tf_op jit(solution)/shard_map/ppermute | solution.py:308
  72.1 42.4 %collective-permute-start.12 = (bf16[3,1024,128]{2,1,0:T(8,128)(2,1)S(1)}, bf16[3,1024,128]{2,1,0:T(8,128)(2,1)S(1)}, u32[]{:S(2)}, u32[]{:S(2)}) collective-permute-start(bf16[3,1024,128]{2,1,0:T(8,128)(2,1)S(1)} %broadcast_select_fusion.w0), channel_id=1, source_target_pairs={{0,192},{64,0},{128,64},{192,128},{1,193},{65,1},{129,65},{193,129... | collective-permute-start | bytes 2359304 | tf_op jit(solution)/shard_map/ppermute | solution.py:308
  75.7 36.9 %collective-permute-start.13 = (bf16[12,16,1024]{2,1,0:T(8,128)(2,1)S(1)}, bf16[12,16,1024]{2,1,0:T(8,128)(2,1)}, u32[]{:S(2)}, u32[]{:S(2)}) collective-permute-start(bf16[12,16,1024]{2,1,0:T(8,128)(2,1)S(1)} %get-tuple-element.7), channel_id=1, source_target_pairs={{0,1},{1,0},{2,3},{3,2},{4,5},{5,4},{6,7},{7,6},{8,9},{9,8},{10,11... | collective-permute-start | bytes 1179656 | tf_op jit(solution)/shard_map/ppermute | solution.py:317
  104.2 8.9 %collective-permute-start.18 = (bf16[12,16,1024]{2,1,0:T(8,128)(2,1)S(1)}, bf16[12,16,1024]{2,1,0:T(8,128)(2,1)S(1)}, u32[]{:S(2)}, u32[]{:S(2)}) collective-permute-start(bf16[12,16,1024]{2,1,0:T(8,128)(2,1)S(1)} %collective-permute-done.17.own), channel_id=1, source_target_pairs={{0,4},{4,0},{8,12},{12,8},{16,20},{20,16},{24,28},{28,24},{32,36},... | collective-permute-start | bytes 1179656 | tf_op jit(solution)/shard_map/ppermute | solution.py:320
  112.6 6.2 %collective-permute-start.16 = (bf16[12,16,1024]{2,1,0:T(8,128)(2,1)}, bf16[12,16,1024]{2,1,0:T(8,128)(2,1)}, u32[]{:S(2)}, u32[]{:S(2)}) collective-permute-start(bf16[12,16,1024]{2,1,0:T(8,128)(2,1)} %collective-permute-done.15.own), channel_id=1, source_target_pairs={{0,4},{4,0},{8,12},{12,8},{16,20},{20,16},{24,28},{28,24},{32,36},... | collective-permute-start | bytes 1179656 | tf_op jit(solution)/shard_map/ppermute | solution.py:320
  113.9 7.9 %collective-permute-start.14 = (bf16[12,16,1024]{2,1,0:T(8,128)(2,1)}, bf16[12,16,1024]{2,1,0:T(8,128)(2,1)}, u32[]{:S(2)}, u32[]{:S(2)}) collective-permute-start(bf16[12,16,1024]{2,1,0:T(8,128)(2,1)} %collective-permute-done.13.own), channel_id=1, source_target_pairs={{0,4},{4,0},{8,12},{12,8},{16,20},{20,16},{24,28},{28,24},{32,36},... | collective-permute-start | bytes 1179656 | tf_op jit(solution)/shard_map/ppermute | solution.py:320
  113.9 10.8 %collective-permute-start.8 = (bf16[12,16,1024]{2,1,0:T(8,128)(2,1)S(1)}, bf16[12,16,1024]{2,1,0:T(8,128)(2,1)}, u32[]{:S(2)}, u32[]{:S(2)}) collective-permute-start(bf16[12,16,1024]{2,1,0:T(8,128)(2,1)S(1)} %get-tuple-element.6.own), channel_id=1, source_target_pairs={{0,4},{4,0},{8,12},{12,8},{16,20},{20,16},{24,28},{28,24},{32,36},... | collective-permute-start | bytes 1179656 | tf_op jit(solution)/shard_map/ppermute | solution.py:320
  135.7 21.7 %collective-permute-start.25 = (bf16[8,64,128]{2,1,0:T(8,128)(2,1)S(1)}, bf16[8,64,128]{2,1,0:T(8,128)(2,1)S(1)}, u32[]{:S(2)}, u32[]{:S(2)}) collective-permute-start(bf16[8,64,128]{2,1,0:T(8,128)(2,1)S(1)} %get-tuple-element.21), channel_id=1, source_target_pairs={{0,0},{1,4},{2,2},{3,6},{4,1},{5,5},{6,3},{7,7},{8,8},{9,12},{10,1... | collective-permute-start | bytes 393224 | tf_op jit(solution)/shard_map/ppermute | solution.py:331
  137.7 16.6 %collective-permute-start.23 = (bf16[8,64,128]{2,1,0:T(8,128)(2,1)S(1)}, bf16[8,64,128]{2,1,0:T(8,128)(2,1)S(1)}, u32[]{:S(2)}, u32[]{:S(2)}) collective-permute-start(bf16[8,64,128]{2,1,0:T(8,128)(2,1)S(1)} %get-tuple-element.23), channel_id=1, source_target_pairs={{0,192},{1,196},{2,194},{3,198},{4,193},{5,197},{6,195},{7,199},{8... | collective-permute-start | bytes 393224 | tf_op jit(solution)/shard_map/ppermute | solution.py:331
  139.9 6.7 %collective-permute-start.19 = (bf16[8,64,128]{2,1,0:T(8,128)(2,1)S(1)}, bf16[8,64,128]{2,1,0:T(8,128)(2,1)S(1)}, u32[]{:S(2)}, u32[]{:S(2)}) collective-permute-start(bf16[8,64,128]{2,1,0:T(8,128)(2,1)S(1)} %get-tuple-element.27), channel_id=1, source_target_pairs={{0,64},{1,68},{2,66},{3,70},{4,65},{5,69},{6,67},{7,71},{8,72},{9,... | collective-permute-start | bytes 393224 | tf_op jit(solution)/shard_map/ppermute | solution.py:331
  140.6 12.2 %collective-permute-start.21 = (bf16[8,64,128]{2,1,0:T(8,128)(2,1)S(1)}, bf16[8,64,128]{2,1,0:T(8,128)(2,1)S(1)}, u32[]{:S(2)}, u32[]{:S(2)}) collective-permute-start(bf16[8,64,128]{2,1,0:T(8,128)(2,1)S(1)} %get-tuple-element.25), channel_id=1, source_target_pairs={{0,128},{1,132},{2,130},{3,134},{4,129},{5,133},{6,131},{7,135},{8... | collective-permute-start | bytes 393224 | tf_op jit(solution)/shard_map/ppermute | solution.py:331
  144.9 7.9 %collective-permute-start.20 = (bf16[8,64,128]{2,1,0:T(8,128)(2,1)S(1)}, bf16[8,64,128]{2,1,0:T(8,128)(2,1)S(1)}, u32[]{:S(2)}, u32[]{:S(2)}) collective-permute-start(bf16[8,64,128]{2,1,0:T(8,128)(2,1)S(1)} %get-tuple-element.26), channel_id=1, source_target_pairs={{0,68},{1,64},{2,70},{3,66},{4,69},{5,65},{6,71},{7,67},{8,76},{9,... | collective-permute-start | bytes 393224 | tf_op jit(solution)/shard_map/ppermute | solution.py:331
  146.6 7.6 %collective-permute-start.22 = (bf16[8,64,128]{2,1,0:T(8,128)(2,1)S(1)}, bf16[8,64,128]{2,1,0:T(8,128)(2,1)S(1)}, u32[]{:S(2)}, u32[]{:S(2)}) collective-permute-start(bf16[8,64,128]{2,1,0:T(8,128)(2,1)S(1)} %get-tuple-element.24), channel_id=1, source_target_pairs={{0,132},{1,128},{2,134},{3,130},{4,133},{5,129},{6,135},{7,131},{8... | collective-permute-start | bytes 393224 | tf_op jit(solution)/shard_map/ppermute | solution.py:331
  152.8 4.6 %collective-permute-start.24 = (bf16[8,64,128]{2,1,0:T(8,128)(2,1)S(1)}, bf16[8,64,128]{2,1,0:T(8,128)(2,1)S(1)}, u32[]{:S(2)}, u32[]{:S(2)}) collective-permute-start(bf16[8,64,128]{2,1,0:T(8,128)(2,1)S(1)} %get-tuple-element.22), channel_id=1, source_target_pairs={{0,196},{1,192},{2,198},{3,194},{4,197},{5,193},{6,199},{7,195},{8... | collective-permute-start | bytes 393224 | tf_op jit(solution)/shard_map/ppermute | solution.py:331
  152.8 4.6 %collective-permute-start.26 = (bf16[8,64,128]{2,1,0:T(8,128)(2,1)S(1)}, bf16[8,64,128]{2,1,0:T(8,128)(2,1)S(1)}, u32[]{:S(2)}, u32[]{:S(2)}) collective-permute-start(bf16[8,64,128]{2,1,0:T(8,128)(2,1)S(1)} %get-tuple-element.20), channel_id=1, source_target_pairs={{0,4},{1,0},{2,6},{3,2},{4,5},{5,1},{6,7},{7,3},{8,12},{9,8},{10,1... | collective-permute-start | bytes 393224 | tf_op jit(solution)/shard_map/ppermute | solution.py:331
  (6 other events, 9.9 us)

commit v3 on v2

v3 whole, which is shorter than its diff:
```python
import functools
import math

import jax
import jax.numpy as jnp
from jax import lax
from jax.experimental import pallas as pl
from jax.experimental.pallas import tpu as pltpu
from jax.sharding import PartitionSpec as P


WIN = 4
NEG = -1e30
LANES = 128


def where():
    a, h, w = lax.axis_index("ta"), lax.axis_index("ha"), lax.axis_index("wa")
    top = jnp.where(h < 2, 1, 0)
    bottom = jnp.where(h >= lax.axis_size("ha") - 2, 1, 0)
    return lax.rem(h, 2), w, lax.rem(w, 2), top, bottom, a


def faces_body(cells, far, near, first, last, sems):
    core = where()[0]
    end = cells.shape[1] - 1
    far_at = core * end
    moves = [(cells.at[0], first), (cells.at[1], last)]
    for t in range(2):
        moves += [(cells.at[t, far_at], far.at[t]), (cells.at[t, end - far_at], near.at[t])]
    copies = [pltpu.make_async_copy(x, y, sems.at[i]) for i, (x, y) in enumerate(moves)]
    for copy in copies:
        copy.start()
    for copy in copies:
        copy.wait()


def faces(cells):
    _, rows, cols, depth = cells.shape
    vmem = pl.BlockSpec(memory_space=pltpu.VMEM)
    row = jax.ShapeDtypeStruct((2, cols, depth), cells.dtype)
    face = jax.ShapeDtypeStruct((rows, cols, depth), cells.dtype)
    return pl.pallas_call(
        faces_body,
        out_shape=(row, row, face, face),
        in_specs=[pl.BlockSpec(memory_space=pltpu.HBM)],
        out_specs=(vmem,) * 4,
        scratch_shapes=[pltpu.SemaphoreType.DMA((6,))],
        compiler_params=pltpu.CompilerParams(vmem_limit_bytes=4 * 2**20),
        name="faces",
    )(cells)


def project_body(groups, *refs):
    place = where()
    outs = refs[-len(groups) :]
    weights = refs[-len(groups) - 4 : -len(groups)]
    core = place[0]
    sides, at = [], 0
    for first, count in groups:
        own, other = refs[at : at + count], refs[at + count : at + 2 * count]
        at += 2 * count
        rows, cols, depth = own[0].shape
        flat = [ref[...].reshape(rows * cols, depth) for ref in (*own, *other)]
        sides.append((jnp.concatenate(flat, axis=0), count, rows, cols))
    for d, w_ref in enumerate(weights):
        weight = jnp.concatenate([w_ref[i] for i in range(3)], axis=1)
        for (first, _), (cells, count, rows, cols), out in zip(groups, sides, outs):
            size = w_ref.shape[2]
            wide = (3 - first) * size
            got = jnp.dot(
                cells, weight[:, first * size :], preferred_element_type=jnp.float32
            ).astype(jnp.bfloat16)
            got = got.reshape(2, count, rows, cols, wide)
            lanes = slice(d * wide, (d + 1) * wide)
            for i in range(count):
                out[i, pl.ds(core * rows, rows), :, lanes] = got[0, i]
                out[i, pl.ds((1 - core) * rows, rows), :, lanes] = got[1, i]


def project(groups, weights):
    vmem = pl.BlockSpec(memory_space=pltpu.VMEM)
    shapes, cells, flops = [], [], 0
    for first, own, other in groups:
        rows, cols, depth = own[0].shape
        wide = (3 - first) * weights[0].shape[2] * len(weights)
        shapes.append(jax.ShapeDtypeStruct((len(own), 2 * rows, cols, wide), jnp.bfloat16))
        cells += [*own, *other]
        flops += 4 * len(own) * rows * cols * depth * wide
    return pl.pallas_call(
        functools.partial(project_body, [(first, len(own)) for first, own, _ in groups]),
        out_shape=tuple(shapes),
        in_specs=[vmem] * (len(cells) + 4),
        out_specs=(vmem,) * len(shapes),
        compiler_params=pltpu.CompilerParams(vmem_limit_bytes=12 * 2**20),
        cost_estimate=pl.CostEstimate(flops=flops, bytes_accessed=4 * 2**20, transcendentals=0),
        name="project",
    )(*cells, *weights)


def attend(scale, steps, r, place, load):
    size = load(1, 0).shape[1]
    span = load(1, 0).shape[0]
    cols = span // (4 * WIN)

    def row_of(dim):
        return (lax.broadcasted_iota(jnp.int32, (span, span), dim) // cols) % WIN

    query = load(r + 1, 0)
    parts = []
    for part in range(3):
        score = lax.dot_general(
            query,
            load(r + part, 1),
            (((1,), (1,)), ((), ())),
            preferred_element_type=jnp.float32,
        ) * scale
        if part == 0:
            score = score + jnp.where(row_of(1) >= row_of(0), 0.0, NEG)
            if r == 0:
                score = score + jnp.where(place[3] == 1, NEG, 0.0)
        if part == 2:
            score = score + jnp.where(row_of(1) <= row_of(0), 0.0, NEG)
            if r == steps - 1:
                score = score + jnp.where(place[4] == 1, NEG, 0.0)
        parts.append(score)
    peak = jnp.max(jnp.maximum(jnp.maximum(parts[0], parts[1]), parts[2]), axis=1, keepdims=True)
    total = None
    ones = jnp.ones((span, size), jnp.bfloat16)
    for part in range(3):
        prob = jnp.exp2(parts[part] - peak).astype(jnp.bfloat16)
        value = jnp.concatenate([load(r + part, 2), ones], axis=1)
        term = jnp.dot(prob, value, preferred_element_type=jnp.float32)
        total = term if total is None else total + term
    result = (total[:, :size] / total[:, size:]).astype(jnp.bfloat16)
    return result.reshape(4, WIN, cols, size)


def loader(d, size, slots, halo):
    _, rows, cols, _ = slots[0].shape
    groups = rows // WIN + 2

    def load(group, which):
        if 0 < group < groups - 1:
            at, lane = (group - 1) * WIN, (3 * d + which) * size
            parts = [p[0, at : at + WIN, :, lane : lane + size] for p in slots]
        else:
            at, lane = min(group, 1) * WIN, (2 * d + which - 1) * size
            parts = [halo[i, at : at + WIN, :, lane : lane + size] for i in range(4)]
        return jnp.concatenate([x.reshape(WIN * cols, size) for x in parts], axis=0)

    return load


def inner_body(scale, p0, p1, p2, p3, out_ref):
    place = where()
    slots = (p0, p1, p2, p3)
    heads, count, _, _, size = out_ref.shape
    cols = p0.shape[2]
    for d in range(heads):
        load = loader(d, size, slots, None)
        for i in range(count):
            result = attend(scale, count + 2, i + 1, place, load)
            for slot in range(4):
                out_ref[d, i, :, pl.ds((place[1] ^ slot) * cols, cols), :] = result[slot]


def outer_body(d, scale, p0, p1, p2, p3, halo, inner, out_ref):
    place = where()
    slots = (p0, p1, p2, p3)
    size = out_ref.shape[3]
    cols = p0.shape[2]
    load = loader(d, size, slots, halo)
    flip = place[2]
    steps = inner.shape[1] + 2
    half = steps // 2
    for r in range(steps):
        band, at = (r // half) ^ flip, (r % half) * WIN
        if 0 < r < steps - 1:
            out_ref[band, at : at + WIN] = inner[d, r - 1]
            continue
        result = attend(scale, steps, r, place, load)
        for slot in range(4):
            out_ref[band, at : at + WIN, pl.ds((place[1] ^ slot) * cols, cols), :] = result[slot]


def cost(queries, cols, size):
    keys = 12 * 4 * cols
    return pl.CostEstimate(
        flops=6 * queries * keys * size, bytes_accessed=2**20, transcendentals=queries * keys
    )


def inner_heads(heads, size, slots):
    _, rows, cols, _ = slots[0].shape
    count = rows // WIN - 2
    vmem = pl.BlockSpec(memory_space=pltpu.VMEM)
    return pl.pallas_call(
        functools.partial(inner_body, math.log2(math.e) * size**-0.5),
        out_shape=jax.ShapeDtypeStruct((heads, count, WIN, 4 * cols, size), jnp.bfloat16),
        in_specs=[vmem] * 4,
        out_specs=vmem,
        compiler_params=pltpu.CompilerParams(vmem_limit_bytes=12 * 2**20),
        cost_estimate=cost(heads * count * WIN * 4 * cols, cols, size),
        name="inner",
    )(*slots)


def one_head(d, size, slots, halo, inner):
    _, rows, cols, _ = slots[0].shape
    vmem = pl.BlockSpec(memory_space=pltpu.VMEM)
    return pl.pallas_call(
        functools.partial(outer_body, d, math.log2(math.e) * size**-0.5),
        out_shape=jax.ShapeDtypeStruct((2, rows // 2, 4 * cols, size), jnp.bfloat16),
        in_specs=[vmem] * 6,
        out_specs=vmem,
        compiler_params=pltpu.CompilerParams(vmem_limit_bytes=12 * 2**20),
        cost_estimate=cost(2 * WIN * 4 * cols, cols, size),
        name="head",
    )(*slots, halo, inner)


def activated(cells, gain):
    cells = cells.astype(jnp.float32)
    rms = lax.rsqrt(jnp.mean(cells * cells, axis=-1, keepdims=True) + 1e-06)
    scaled = cells * rms * gain
    return scaled / (1.0 + jnp.exp(-scaled))


def conv_body(
    own, before, after, rim, rim_before, rim_after, left, right, gain, w_ref,
    block_ref, keep_ref, give_ref, edge_ref, taps, raw, left_n, right_n, sums,
):
    core, frame = where()[0], where()[2]
    frames, h_dev, w_dev, channels = own.shape
    rim_rows = rim.shape[1]
    far = rim_rows - 1
    rows = h_dev + far - 1
    own_at = jnp.where(core == 0, far, 1)
    far_at = jnp.where(core == 0, 0, h_dev + 1)
    near_at = jnp.where(core == 0, h_dev + far, 0)
    scale = gain[...].reshape(1, 1, channels)

    for side_ref, to in ((left, left_n), (right, right_n)):
        to[...] = activated(side_ref[...], scale)
    col = lax.broadcasted_iota(jnp.int32, (1, w_dev, channels), 1)

    def put(source, lead, t, start, count, at, skip, keep_raw):
        raw_cells = source[lead, start : start + count]
        if keep_raw:
            raw[t - 1, pl.ds(at, count)] = raw_cells
        cells = activated(raw_cells, scale)
        flat = cells.reshape(count * w_dev, channels)
        back = pltpu.roll(flat, 1, 0).reshape(cells.shape)
        ahead = pltpu.roll(flat, count * w_dev - 1, 0).reshape(cells.shape)
        lo = left_n[t, skip : skip + count].reshape(count, 1, channels)
        hi = right_n[t, skip : skip + count].reshape(count, 1, channels)
        to = taps.at[t, pl.ds(at, count)]
        to[:, :, :channels] = jnp.where(col == 0, lo, back).astype(jnp.bfloat16)
        to[:, :, channels : 2 * channels] = cells.astype(jnp.bfloat16)
        to[:, :, 2 * channels :] = jnp.where(col == w_dev - 1, hi, ahead).astype(jnp.bfloat16)

    for t in range(frames + 2):
        if t == 0:
            main, edge, lead = before, rim_before, 0
        elif t == frames + 1:
            main, edge, lead = after, rim_after, 0
        else:
            main, edge, lead = own, rim, t - 1
        inner = 0 < t <= frames
        for start in range(0, h_dev, 8):
            put(main, lead, t, start, 8, own_at + start, start, inner)
        put(edge, lead, t, 0, far, far_at, h_dev, inner)
        put(edge, lead, t, far, 1, near_at, h_dev + far, inner)

    chunk_rows = rows
    pieces = channels // LANES

    def convolve(t, start):
        parts = [
            taps[t + a, pl.ds(start + b, chunk_rows)].reshape(chunk_rows * w_dev, 3 * channels)
            for a in range(3)
            for b in range(3)
        ]
        total = jnp.dot(parts[0], w_ref[0], preferred_element_type=jnp.float32)
        for i in range(1, 9):
            total = total + jnp.dot(parts[i], w_ref[i], preferred_element_type=jnp.float32)
        return total

    for k, out in ((0, keep_ref), (1, give_ref)):
        t = frame ^ k

        def chunk(j, _):
            start = j * chunk_rows
            total = convolve(t, start)
            base = raw[t, pl.ds(start + 1, chunk_rows)].astype(jnp.float32)
            total = (total.reshape(chunk_rows, w_dev, channels) + base).astype(jnp.bfloat16)
            block = total.astype(jnp.float32)
            for piece in range(pieces):
                sums[piece, pl.ds(start, chunk_rows)] = block[:, :, piece * LANES : (piece + 1) * LANES]
            return 0

        lax.fori_loop(0, rows // chunk_rows, chunk, 0)
        for piece in range(pieces):
            lanes = slice(piece * LANES, (piece + 1) * LANES)
            block_ref[t, :, :, lanes] = sums[piece, pl.ds(own_at - 1, h_dev)].astype(jnp.bfloat16)
            for dw in range(2):
                picked = sums[piece, :, pl.ds(dw, w_dev // 2, stride=2), :].astype(jnp.bfloat16)
                picked = picked.reshape(rows // 2, 2, w_dev // 2, LANES)
                for dh in range(2):
                    at = (2 * dh + dw) * channels + piece * LANES
                    out[:, :, at : at + LANES] = picked[:, dh]
        edge_ref[k] = out[pl.ds(core * (rows // 2 - WIN), WIN)]


def conv_block(own, before, after, rim, rim_before, rim_after, left, right, gain, weight):
    frames, h_dev, w_dev, channels = own.shape
    rows = h_dev + rim.shape[1] - 2
    vmem = pl.BlockSpec(memory_space=pltpu.VMEM)
    patch = jax.ShapeDtypeStruct((rows // 2, w_dev // 2, 4 * channels), jnp.bfloat16)
    edge = jax.ShapeDtypeStruct((2, WIN, w_dev // 2, 4 * channels), jnp.bfloat16)
    return pl.pallas_call(
        conv_body,
        out_shape=(jax.ShapeDtypeStruct(own.shape, jnp.bfloat16), patch, patch, edge),
        in_specs=[vmem] * 10,
        out_specs=(vmem,) * 4,
        scratch_shapes=[
            pltpu.VMEM((frames + 2, rows + 2, w_dev, 3 * channels), jnp.bfloat16),
            pltpu.VMEM((frames, rows + 2, w_dev, channels), jnp.bfloat16),
            pltpu.VMEM(left.shape, jnp.float32),
            pltpu.VMEM(left.shape, jnp.float32),
            pltpu.VMEM((channels // LANES, rows, w_dev, LANES), jnp.float32),
        ],
        compiler_params=pltpu.CompilerParams(vmem_limit_bytes=20 * 2**20),
        cost_estimate=pl.CostEstimate(
            flops=2 * 27 * frames * rows * w_dev * channels * channels,
            bytes_accessed=8 * 2**20,
            transcendentals=2**20,
        ),
        name="conv",
    )(own, before, after, rim, rim_before, rim_after, left, right, gain, weight)


def permute(cells, axis, pairs):
    if cells.shape[-2] % 16:
        return lax.ppermute(cells, axis, pairs)
    flat = cells.reshape(-1, cells.shape[-1])
    return lax.ppermute(flat, axis, pairs).reshape(cells.shape)


def ends(cells, axis, dim, width):
    count = lax.axis_size(axis)
    head = lax.slice_in_dim(cells, 0, width, axis=dim)
    tail = lax.slice_in_dim(cells, cells.shape[dim] - width, cells.shape[dim], axis=dim)
    return (
        permute(tail, axis, [(i, i + 1) for i in range(count - 1)]),
        permute(head, axis, [(i + 1, i) for i in range(count - 1)]),
    )


def choose_body(mine, swapped, out):
    place = where()

    @pl.when(place[0] == place[2])
    def _():
        out[...] = mine[...]

    @pl.when(place[0] != place[2])
    def _():
        out[...] = swapped[...]


def choose(mine, swapped):
    vmem = pl.BlockSpec(memory_space=pltpu.VMEM)
    return pl.pallas_call(
        choose_body,
        out_shape=jax.ShapeDtypeStruct(mine.shape, mine.dtype),
        in_specs=[vmem, vmem],
        out_specs=vmem,
        compiler_params=pltpu.CompilerParams(vmem_limit_bytes=4 * 2**20),
        name="choose",
    )(mine, swapped)


def assemble_body(count, order, *refs):
    place = where()
    pieces, out, sems = refs[: 2 * len(order)], refs[-2], refs[-1]
    copies = []
    for i, d in enumerate(order):
        for kind in range(2):
            at = (place[5] + d) % count * 2 + (place[0] ^ kind)
            n = 2 * i + kind
            copies.append(pltpu.make_async_copy(pieces[n], out.at[at], sems.at[n]))
            copies[-1].start()
    for copy in copies:
        copy.wait()


def assemble(count, order, pieces):
    vmem = pl.BlockSpec(memory_space=pltpu.VMEM)
    return pl.pallas_call(
        functools.partial(assemble_body, count, order),
        out_shape=jax.ShapeDtypeStruct((len(pieces),) + pieces[0].shape, jnp.bfloat16),
        in_specs=[vmem] * len(pieces),
        out_specs=pl.BlockSpec(memory_space=pl.ANY),
        scratch_shapes=[pltpu.SemaphoreType.DMA((len(pieces),))],
        compiler_params=pltpu.CompilerParams(vmem_limit_bytes=4 * 2**20),
        name="assemble",
    )(*pieces)


def block_and_attention(latents, norm_gain, conv_weight, qkv_weight):
    _, _, w_dev, channels = latents.shape
    n_ta, n_ha, n_wa = lax.axis_size("ta"), lax.axis_size("ha"), lax.axis_size("wa")

    def everywhere(to):
        pairs = []
        for ta in range(n_ta):
            for ha in range(n_ha):
                for wa in range(n_wa):
                    dest = to(ta, ha, wa)
                    if dest is not None:
                        ta2, ha2, wa2 = dest
                        pairs.append(
                            ((ta * n_ha + ha) * n_wa + wa, (ta2 * n_ha + ha2) * n_wa + wa2)
                        )
        return pairs

    axes = ("ta", "ha", "wa")
    far_row, near_row, first, last = faces(latents)
    odd = [(i, i + 1) for i in range(1, n_ha - 1, 2)]
    odd += [(j, i) for i, j in odd]
    rim_far = permute(far_row[:, None], "ha", odd)
    ups = [(i, i + 1) for i in range(n_ta - 1)]
    before = permute(last[None], "ta", ups)
    after = permute(first[None], "ta", [(j, i) for i, j in ups])
    rim_near = permute(near_row[:, None], "ha", [(i, i ^ 1) for i in range(n_ha)])
    rim = jnp.concatenate([rim_far, rim_near], axis=1)
    rim_before, rim_after = ends(rim, "ta", 0, 1)
    last = w_dev - 1

    def side(at):
        return jnp.concatenate(
            [
                jnp.concatenate([x[:, :, at] for x in (before, latents, after)], axis=0),
                jnp.concatenate([x[:, :, at] for x in (rim_before, rim, rim_after)], axis=0),
            ],
            axis=1,
        )

    left = permute(side(last), "wa", [(i, i + 1) for i in range(n_wa - 1)])
    right = permute(side(0), "wa", [(i + 1, i) for i in range(n_wa - 1)])
    mine = qkv_weight[:, 0].transpose(1, 0, 2)
    swapped = permute(
        mine,
        axes,
        everywhere(lambda ta, ha, wa: (ta, ha, wa ^ 1) if (wa ^ 1) % 2 != ha % 2 else None),
    )
    mine = choose(mine, swapped)
    weights = [mine] + [
        permute(mine, "ta", [(i, (i + d) % n_ta) for i in range(n_ta)])
        for d in range(1, n_ta)
    ]

    block_out, keep, give, edge = conv_block(
        latents, before, after, rim, rim_before, rim_after, left, right,
        norm_gain[None], conv_weight.reshape(9, 3 * channels, channels),
    )
    own = [keep] + [
        permute(give if d % 2 else keep, "wa", [(i, i ^ d) for i in range(n_wa)])
        for d in range(1, n_wa)
    ]
    other = [permute(x, "ha", [(j, j ^ 1) for j in range(n_ha)]) for x in own]

    edge = permute(edge, "ha", odd)
    rows_own = [edge[0]] + [
        permute(edge[d % 2], "wa", [(i, i ^ d) for i in range(n_wa)])
        for d in range(1, n_wa)
    ]
    rows_other = [permute(x, "ha", [(j, j ^ 1) for j in range(n_ha)]) for x in rows_own]
    slots = [project([(0, [own[i]], [other[i]])], weights)[0] for i in range(4)]
    heads, size = n_ta, qkv_weight.shape[3]
    inner = inner_heads(heads, size, slots)
    (halo,) = project([(1, rows_own, rows_other)], weights)
    pieces = []
    for d in range(heads - 1, -1, -1):
        out = one_head(d, size, slots, halo, inner)
        moved = permute(
            out,
            axes,
            everywhere(
                lambda ta, ha, wa: (
                    (ta - d) % n_ta,
                    ha - ha % 2 + wa % 2,
                    wa - wa % 2 + ha % 2,
                )
            ),
        )
        crossed = permute(moved[1], "ha", [(j, j ^ 1) for j in range(n_ha)])
        pieces += [moved[0], crossed]
    result = assemble(n_ta, list(range(heads - 1, -1, -1)), pieces)
    return block_out, result[:, :, :, None, :]


def solution(mesh):
    return jax.shard_map(
        block_and_attention,
        mesh=mesh,
        in_specs=(P("ta", "ha", "wa", None), P(), P(), P(None, ("ta", "wa"), None, None)),
        out_specs=(P("ta", "ha", "wa", None), P(None, "ha", None, ("ta", "wa"), None)),
        check_vma=False,
    )
```

time: 161 us -> 130 us (0.81); the launches traced: 158 us -> 129 us
  waiting for transfers between devices: 50.3 us -> 26.9 us
  Pallas kernels: 29.3 us -> 20 us
  starting transfers between devices: 65.5 us -> 74.4 us
  local copies, waits for them, and re-layouts: 11.2 us -> 6.12 us
    ppermute x27 -> x35, waiting for transfers between devices: 50.3 us -> 26.9 us  [the longest x33 25.9 us: permute(): return lax.ppermute(flat, axis, pairs).reshape(cells.shape)]
    ppermute x27 -> x35, starting transfers between devices: 65.5 us -> 74.4 us  [the longest x33 68.1 us: permute(): return lax.ppermute(flat, axis, pairs).reshape(cells.shape)]
    pallas_call x8 -> x13, Pallas kernels: 19.1 us -> 13.7 us  [the longest x5 6.25 us: project(): pl.pallas_call(functools.partial(project_body, [(first, len(own)) for fir...]
    pallas_call x1, Pallas kernels: 10.2 us -> 6.39 us  [conv_block(): pl.pallas_call(conv_body, out_shape=(jax.ShapeDtypeStruct(own.shape, jnp....]
    unnamed x26 -> x12, local copies, waits for them, and re-layouts: 7.41 us -> 4.77 us
  transfers between devices with their start and end apart: 27 -> 35, of which waited for: 12 -> 11; matrix products, arithmetic and copies ran while one was open for 4% -> 1% of each run, Pallas kernels for 12% -> 13%
where the time goes in v3:
time: 130 us; the launch traced here: 129 us
  starting transfers between devices  74.4 us (57%)
  waiting for transfers between devices  26.9 us (21%)
  Pallas kernels  20 us (15%)
  local copies, waits for them, and re-layouts  6.12 us (5%)
  between operations  1.3 us (1%)
    ppermute x33, starting transfers between devices, permute(): return lax.ppermute(flat, axis, pairs).reshape(cells.shape)  68.1 us
    ppermute x33, waiting for transfers between devices, permute(): return lax.ppermute(flat, axis, pairs).reshape(cells.shape)  25.9 us
    pallas_call x1, Pallas kernels, conv_block(): pl.pallas_call(conv_body, out_shape=(jax.ShapeDtypeStruct(own.shape, jnp....  6.39 us
    ppermute x2, starting transfers between devices, permute(): return lax.ppermute(cells, axis, pairs)  6.25 us
    pallas_call x5, Pallas kernels, project(): pl.pallas_call(functools.partial(project_body, [(first, len(own)) for fir...  6.25 us
    unnamed x12, local copies, waits for them, and re-layouts  4.77 us
    pallas_call x4, Pallas kernels, one_head(): pl.pallas_call(functools.partial(outer_body, d, math.log2(math.e) * size...  3.84 us
  transfers between devices with their start and end apart: 35, of which 11 were waited for; matrix products, arithmetic and copies ran while one was open for 1% of the time, Pallas kernels for 13%

profile of v3, /device:TPU:3, one launch (start us, length us, event | category | flops | bytes accessed | tf_op | source)
XLA Modules:
  0.0 129.1 jit_solution(11865463428432624882)
XLA Ops:
  1.9 9.4 %collective-permute-start.2 = (bf16[64,256]{1,0:T(8,128)(2,1)S(1)}, bf16[64,256]{1,0:T(8,128)(2,1)S(1)}, u32[]{:S(2)}, u32[]{:S(2)}) collective-permute-start(bf16[64,256]{1,0:T(8,128)(2,1)S(1)} %bitcast.148), channel_id=1, source_target_pairs={{4,8},{12,16},{20,24},{28,32},{36,40},{44,48},{52,56},{8,4},{16,12... | collective-permute-start | bytes 98312 | tf_op jit(solution)/shard_map/ppermute | solution.py:348
  11.3 1.3 %collective-permute-start.1 = (bf16[512,256]{1,0:T(8,128)(2,1)S(1)}, bf16[512,256]{1,0:T(8,128)(2,1)S(1)}, u32[]{:S(2)}, u32[]{:S(2)}) collective-permute-start(bf16[512,256]{1,0:T(8,128)(2,1)S(1)} %bitcast.143), channel_id=1, source_target_pairs={{64,0},{128,64},{192,128},{65,1},{129,65},{193,129},{66,2},{130,66... | collective-permute-start | bytes 786440 | tf_op jit(solution)/shard_map/ppermute | solution.py:348
  12.6 4.0 %collective-permute-start = (bf16[512,256]{1,0:T(8,128)(2,1)S(1)}, bf16[512,256]{1,0:T(8,128)(2,1)S(1)}, u32[]{:S(2)}, u32[]{:S(2)}) collective-permute-start(bf16[512,256]{1,0:T(8,128)(2,1)S(1)} %bitcast.142), channel_id=1, source_target_pairs={{0,64},{64,128},{128,192},{1,65},{65,129},{129,193},{2,66},{66,130... | collective-permute-start | bytes 786440 | tf_op jit(solution)/shard_map/ppermute | solution.py:348
  16.7 1.3 %collective-permute-start.9 = (bf16[3072,128]{1,0:T(8,128)(2,1)}, bf16[3072,128]{1,0:T(8,128)(2,1)S(1)}, u32[]{:S(2)}, u32[]{:S(2)}) collective-permute-start(bf16[3072,128]{1,0:T(8,128)(2,1)} %bitcast.101), channel_id=1, source_target_pairs={{0,1},{2,3},{5,4},{7,6},{8,9},{10,11},{13,12},{15,14},{16,17},{18,... | collective-permute-start | bytes 2359304 | tf_op jit(solution)/shard_map/ppermute | solution.py:348
  19.3 3.2 %collective-permute-start.4 = (bf16[64,256]{1,0:T(8,128)(2,1)S(1)}, bf16[64,256]{1,0:T(8,128)(2,1)S(1)}, u32[]{:S(2)}, u32[]{:S(2)}) collective-permute-start(bf16[64,256]{1,0:T(8,128)(2,1)S(1)} %bitcast.155), channel_id=1, source_target_pairs={{0,64},{64,128},{128,192},{1,65},{65,129},{129,193},{2,66},{66,130... | collective-permute-start | bytes 98312 | tf_op jit(solution)/shard_map/ppermute | solution.py:348
  22.6 1.3 %collective-permute-start.5 = (bf16[64,256]{1,0:T(8,128)(2,1)S(1)}, bf16[64,256]{1,0:T(8,128)(2,1)S(1)}, u32[]{:S(2)}, u32[]{:S(2)}) collective-permute-start(bf16[64,256]{1,0:T(8,128)(2,1)S(1)} %bitcast.156), channel_id=1, source_target_pairs={{64,0},{128,64},{192,128},{65,1},{129,65},{193,129},{66,2},{130,66... | collective-permute-start | bytes 98312 | tf_op jit(solution)/shard_map/ppermute | solution.py:348
  23.9 3.3 %collective-permute-done.5 = bf16[64,256]{1,0:T(8,128)(2,1)S(1)} collective-permute-done((bf16[64,256]{1,0:T(8,128)(2,1)S(1)}, bf16[64,256]{1,0:T(8,128)(2,1)S(1)}, u32[]{:S(2)}, u32[]{:S(2)}) %collective-permute-start.5) | collective-permute-done | bytes 32800 | tf_op jit(solution)/shard_map/ppermute | solution.py:348
  27.4 1.3 %collective-permute-start.7 = (bf16[4,18,256]{2,1,0:T(8,128)(2,1)S(1)}, bf16[4,18,256]{2,1,0:T(8,128)(2,1)S(1)}, u32[]{:S(2)}, u32[]{:S(2)}) collective-permute-start(bf16[4,18,256]{2,1,0:T(8,128)(2,1)S(1)} %maximum_maximum_fusion.1), channel_id=1, source_target_pairs={{1,0},{2,1},{3,2},{5,4},{6,5},{7,6},{9,8},{10,9},{11,10},{13,12},{... | collective-permute-start | bytes 110600 | tf_op jit(solution)/shard_map/ppermute | solution.py:346
  28.7 5.0 %collective-permute-start.6 = (bf16[4,18,256]{2,1,0:T(8,128)(2,1)S(1)}, bf16[4,18,256]{2,1,0:T(8,128)(2,1)S(1)}, u32[]{:S(2)}, u32[]{:S(2)}) collective-permute-start(bf16[4,18,256]{2,1,0:T(8,128)(2,1)S(1)} %maximum_maximum_fusion), channel_id=1, source_target_pairs={{0,1},{1,2},{2,3},{4,5},{5,6},{6,7},{8,9},{9,10},{10,11},{12,13},{... | collective-permute-start | bytes 110600 | tf_op jit(solution)/shard_map/ppermute | solution.py:346
  35.9 2.0 %copy-done.3 = bf16[3,3,3,256,256]{4,3,2,1,0:T(8,128)(2,1)S(1)} copy-done((bf16[3,3,3,256,256]{4,3,2,1,0:T(8,128)(2,1)S(1)}, bf16[3,3,3,256,256]{4,3,2,1,0:T(8,128)(2,1)}, u32[]{:S(2)}) %copy-start.3) | copy-done | bytes 3538968
  38.6 6.4 %conv.1 = (bf16[2,16,32,256]{3,2,1,0:T(8,128)(2,1)}, bf16[8,16,1024]{2,1,0:T(8,128)(2,1)S(1)}, bf16[8,16,1024]{2,1,0:T(8,128)(2,1)S(1)}, bf16[2,4,16,1024]{3,2,1,0:T(8,128)(2,1)S(1)}) custom-call(bf16[2,16,32,256]{3,2,1,0:T(8,128)(2,1)S(1)} %copy-done.2, bf16[1,16,32,256]{3,2,1,0:T(8,128)(2,1)S(1)} %bitcast.136, bf16[1,16,32,256]{3,2,1,0:T(8,128)(2,1)S(1)} %bitcast.134, ...), custom_call_target="tpu_custom_call" | custom-call | flops 3623878656 | bytes 8388608 | tf_op jit(solution)/shard_map/conv/pallas_call | solution.py:322
  44.9 2.7 %collective-permute-start.17 = (bf16[128,1024]{1,0:T(8,128)(2,1)S(1)}, bf16[128,1024]{1,0:T(8,128)(2,1)S(1)}, u32[]{:S(2)}, u32[]{:S(2)}) collective-permute-start(bf16[128,1024]{1,0:T(8,128)(2,1)S(1)} %bitcast.145), channel_id=1, source_target_pairs={{0,3},{1,2},{2,1},{3,0},{4,7},{5,6},{6,5},{7,4},{8,11},{9,10},{10,... | collective-permute-start | bytes 786440 | tf_op jit(solution)/shard_map/ppermute | solution.py:348
  48.6 3.1 %collective-permute-start.11 = (bf16[3072,128]{1,0:T(8,128)(2,1)S(1)}, bf16[3072,128]{1,0:T(8,128)(2,1)S(1)}, u32[]{:S(2)}, u32[]{:S(2)}) collective-permute-start(bf16[3072,128]{1,0:T(8,128)(2,1)S(1)} %bitcast.84), channel_id=1, source_target_pairs={{0,128},{64,192},{128,0},{192,64},{1,129},{65,193},{129,1},{193,65... | collective-permute-start | bytes 2359304 | tf_op jit(solution)/shard_map/ppermute | solution.py:348
  52.2 8.7 %collective-permute-start.19 = (bf16[128,1024]{1,0:T(8,128)(2,1)S(1)}, bf16[128,1024]{1,0:T(8,128)(2,1)S(1)}, u32[]{:S(2)}, u32[]{:S(2)}) collective-permute-start(bf16[128,1024]{1,0:T(8,128)(2,1)S(1)} %bitcast.144), channel_id=1, source_target_pairs={{4,8},{12,16},{20,24},{28,32},{36,40},{44,48},{52,56},{8,4},{16,12... | collective-permute-start | bytes 786440 | tf_op jit(solution)/shard_map/ppermute | solution.py:348
  60.9 3.3 %collective-permute-start.15 = (bf16[128,1024]{1,0:T(8,128)(2,1)S(1)}, bf16[128,1024]{1,0:T(8,128)(2,1)S(1)}, u32[]{:S(2)}, u32[]{:S(2)}) collective-permute-start(bf16[128,1024]{1,0:T(8,128)(2,1)S(1)} %bitcast.110), channel_id=1, source_target_pairs={{0,2},{1,3},{2,0},{3,1},{4,6},{5,7},{6,4},{7,5},{8,10},{9,11},{10,... | collective-permute-start | bytes 786440 | tf_op jit(solution)/shard_map/ppermute | solution.py:348
  64.2 2.9 %collective-permute-done.19 = bf16[128,1024]{1,0:T(8,128)(2,1)S(1)} collective-permute-done((bf16[128,1024]{1,0:T(8,128)(2,1)S(1)}, bf16[128,1024]{1,0:T(8,128)(2,1)S(1)}, u32[]{:S(2)}, u32[]{:S(2)}) %collective-permute-start.19) | collective-permute-done | bytes 262176 | tf_op jit(solution)/shard_map/ppermute | solution.py:348
  67.1 7.1 %collective-permute-start.8 = (bf16[128,1024]{1,0:T(8,128)(2,1)S(1)}, bf16[128,1024]{1,0:T(8,128)(2,1)S(1)}, u32[]{:S(2)}, u32[]{:S(2)}) collective-permute-start(bf16[128,1024]{1,0:T(8,128)(2,1)S(1)} %bitcast.111), channel_id=1, source_target_pairs={{0,4},{4,0},{8,12},{12,8},{16,20},{20,16},{24,28},{28,24},{32,36},... | collective-permute-start | bytes 786440 | tf_op jit(solution)/shard_map/ppermute | solution.py:348
  74.2 12.7 %collective-permute-done.15 = bf16[128,1024]{1,0:T(8,128)(2,1)S(1)} collective-permute-done((bf16[128,1024]{1,0:T(8,128)(2,1)S(1)}, bf16[128,1024]{1,0:T(8,128)(2,1)S(1)}, u32[]{:S(2)}, u32[]{:S(2)}) %collective-permute-start.15) | collective-permute-done | bytes 262176 | tf_op jit(solution)/shard_map/ppermute | solution.py:348
  89.5 3.0 %collective-permute-start.21 = (bf16[64,1024]{1,0:T(8,128)(2,1)S(1)}, bf16[64,1024]{1,0:T(8,128)(2,1)S(1)}, u32[]{:S(2)}, u32[]{:S(2)}) collective-permute-start(bf16[64,1024]{1,0:T(8,128)(2,1)S(1)} %get-tuple-element.33), channel_id=1, source_target_pairs={{0,2},{1,3},{2,0},{3,1},{4,6},{5,7},{6,4},{7,5},{8,10},{9,11},{10,... | collective-permute-start | bytes 393224 | tf_op jit(solution)/shard_map/ppermute | solution.py:348
  92.5 1.2 project.5.p0
  93.8 1.3 project.8.p3
  95.8 1.6 %collective-permute-start.23 = (bf16[64,1024]{1,0:T(8,128)(2,1)S(1)}, bf16[64,1024]{1,0:T(8,128)(2,1)S(1)}, u32[]{:S(2)}, u32[]{:S(2)}) collective-permute-start(bf16[64,1024]{1,0:T(8,128)(2,1)S(1)} %get-tuple-element.33), channel_id=1, source_target_pairs={{0,4},{4,0},{8,12},{12,8},{16,20},{20,16},{24,28},{28,24},{32,36},... | collective-permute-start | bytes 393224 | tf_op jit(solution)/shard_map/ppermute | solution.py:348
  97.4 2.2 %collective-permute-done.20 = bf16[64,1024]{1,0:T(8,128)(2,1)S(1)} collective-permute-done((bf16[64,1024]{1,0:T(8,128)(2,1)S(1)}, bf16[64,1024]{1,0:T(8,128)(2,1)S(1)}, u32[]{:S(2)}, u32[]{:S(2)}) %collective-permute-start.20) | collective-permute-done | bytes 131104 | tf_op jit(solution)/shard_map/ppermute | solution.py:348
  99.7 1.4 %collective-permute-start.26 = (bf16[64,1024]{1,0:T(8,128)(2,1)S(1)}, bf16[64,1024]{1,0:T(8,128)(2,1)S(1)}, u32[]{:S(2)}, u32[]{:S(2)}) collective-permute-start(bf16[64,1024]{1,0:T(8,128)(2,1)S(1)} %collective-permute-done.22), channel_id=1, source_target_pairs={{0,4},{4,0},{8,12},{12,8},{16,20},{20,16},{24,28},{28,24},{32,36},... | collective-permute-start | bytes 393224 | tf_op jit(solution)/shard_map/ppermute | solution.py:348
  102.8 1.3 project.6.p1
  104.1 2.3 %inner.1 = bf16[4,2,4,64,128]{4,3,2,1,0:T(8,128)(2,1)S(1)} custom-call(bf16[1,16,16,1536]{3,2,1,0:T(8,128)(2,1)S(1)} %project.5.p0, bf16[1,16,16,1536]{3,2,1,0:T(8,128)(2,1)S(1)} %project.6.p1, bf16[1,16,16,1536]{3,2,1,0:T(8,128)(2,1)S(1)} %project.7.p2, bf16[1,16,16,1536]{3,2,1,0:T(8,128)(2,1)S(1)} %project.8.p3), custom_call_target="tpu_custom_call" | custom-call | flops 1207959552 | bytes 1048576 | tf_op jit(solution)/shard_map/inner/pallas_call | solution.py:198
  106.4 1.3 project.9.halo
  108.6 3.2 %collective-permute-start.29 = (bf16[1024,128]{1,0:T(8,128)(2,1)S(1)}, bf16[1024,128]{1,0:T(8,128)(2,1)S(1)}, u32[]{:S(2)}, u32[]{:S(2)}) collective-permute-start(bf16[1024,128]{1,0:T(8,128)(2,1)S(1)} %bitcast.121), channel_id=1, source_target_pairs={{0,128},{1,132},{2,130},{3,134},{4,129},{5,133},{6,131},{7,135},{8... | collective-permute-start | bytes 786440 | tf_op jit(solution)/shard_map/ppermute | solution.py:348
  113.9 3.9 %collective-permute-start.31 = (bf16[1024,128]{1,0:T(8,128)(2,1)S(1)}, bf16[1024,128]{1,0:T(8,128)(2,1)S(1)}, u32[]{:S(2)}, u32[]{:S(2)}) collective-permute-start(bf16[1024,128]{1,0:T(8,128)(2,1)S(1)} %bitcast.119), channel_id=1, source_target_pairs={{0,192},{1,196},{2,194},{3,198},{4,193},{5,197},{6,195},{7,199},{8... | collective-permute-start | bytes 786440 | tf_op jit(solution)/shard_map/ppermute | solution.py:348
  118.8 2.2 %collective-permute-start.33 = (bf16[1024,128]{1,0:T(8,128)(2,1)S(1)}, bf16[1024,128]{1,0:T(8,128)(2,1)S(1)}, u32[]{:S(2)}, u32[]{:S(2)}) collective-permute-start(bf16[1024,128]{1,0:T(8,128)(2,1)S(1)} %bitcast.117), channel_id=1, source_target_pairs={{0,0},{1,4},{2,2},{3,6},{4,1},{5,5},{6,3},{7,7},{8,8},{9,12},{10,1... | collective-permute-start | bytes 786440 | tf_op jit(solution)/shard_map/ppermute | solution.py:348
  121.0 1.5 %collective-permute-start.30 = (bf16[512,128]{1,0:T(8,128)(2,1)S(1)}, bf16[512,128]{1,0:T(8,128)(2,1)S(1)}, u32[]{:S(2)}, u32[]{:S(2)}) collective-permute-start(bf16[512,128]{1,0:T(8,128)(2,1)S(1)} %get-tuple-element.28), channel_id=1, source_target_pairs={{0,4},{4,0},{8,12},{12,8},{16,20},{20,16},{24,28},{28,24},{32,36},... | collective-permute-start | bytes 393224 | tf_op jit(solution)/shard_map/ppermute | solution.py:348
  122.6 2.7 %collective-permute-start.28 = (bf16[512,128]{1,0:T(8,128)(2,1)S(1)}, bf16[512,128]{1,0:T(8,128)(2,1)S(1)}, u32[]{:S(2)}, u32[]{:S(2)}) collective-permute-start(bf16[512,128]{1,0:T(8,128)(2,1)S(1)} %get-tuple-element.30), channel_id=1, source_target_pairs={{0,4},{4,0},{8,12},{12,8},{16,20},{20,16},{24,28},{28,24},{32,36},... | collective-permute-start | bytes 393224 | tf_op jit(solution)/shard_map/ppermute | solution.py:348
  (88 shorter events, 19.8 us)
Async XLA Ops:
  1.9 17.2 %collective-permute-start.2 = (bf16[64,256]{1,0:T(8,128)(2,1)S(1)}, bf16[64,256]{1,0:T(8,128)(2,1)S(1)}, u32[]{:S(2)}, u32[]{:S(2)}) collective-permute-start(bf16[64,256]{1,0:T(8,128)(2,1)S(1)} %bitcast.148), channel_id=1, source_target_pairs={{4,8},{12,16},{20,24},{28,32},{36,40},{44,48},{52,56},{8,4},{16,12... | collective-permute-start | bytes 98312 | tf_op jit(solution)/shard_map/ppermute | solution.py:348
  11.2 7.8 %collective-permute-start.3 = (bf16[64,256]{1,0:T(8,128)(2,1)S(1)}, bf16[64,256]{1,0:T(8,128)(2,1)S(1)}, u32[]{:S(2)}, u32[]{:S(2)}) collective-permute-start(bf16[64,256]{1,0:T(8,128)(2,1)S(1)} %bitcast.147), channel_id=1, source_target_pairs={{0,4},{4,0},{8,12},{12,8},{16,20},{20,16},{24,28},{28,24},{32,36},... | collective-permute-start | bytes 98312 | tf_op jit(solution)/shard_map/ppermute | solution.py:348
  11.3 15.9 %collective-permute-start.1 = (bf16[512,256]{1,0:T(8,128)(2,1)S(1)}, bf16[512,256]{1,0:T(8,128)(2,1)S(1)}, u32[]{:S(2)}, u32[]{:S(2)}) collective-permute-start(bf16[512,256]{1,0:T(8,128)(2,1)S(1)} %bitcast.143), channel_id=1, source_target_pairs={{64,0},{128,64},{192,128},{65,1},{129,65},{193,129},{66,2},{130,66... | collective-permute-start | bytes 786440 | tf_op jit(solution)/shard_map/ppermute | solution.py:348
  12.6 14.7 %collective-permute-start = (bf16[512,256]{1,0:T(8,128)(2,1)S(1)}, bf16[512,256]{1,0:T(8,128)(2,1)S(1)}, u32[]{:S(2)}, u32[]{:S(2)}) collective-permute-start(bf16[512,256]{1,0:T(8,128)(2,1)S(1)} %bitcast.142), channel_id=1, source_target_pairs={{0,64},{64,128},{128,192},{1,65},{65,129},{129,193},{2,66},{66,130... | collective-permute-start | bytes 786440 | tf_op jit(solution)/shard_map/ppermute | solution.py:348
  16.7 31.8 %collective-permute-start.9 = (bf16[3072,128]{1,0:T(8,128)(2,1)}, bf16[3072,128]{1,0:T(8,128)(2,1)S(1)}, u32[]{:S(2)}, u32[]{:S(2)}) collective-permute-start(bf16[3072,128]{1,0:T(8,128)(2,1)} %bitcast.101), channel_id=1, source_target_pairs={{0,1},{2,3},{5,4},{7,6},{8,9},{10,11},{13,12},{15,14},{16,17},{18,... | collective-permute-start | bytes 2359304 | tf_op jit(solution)/shard_map/ppermute | solution.py:348
  19.3 4.5 %collective-permute-start.4 = (bf16[64,256]{1,0:T(8,128)(2,1)S(1)}, bf16[64,256]{1,0:T(8,128)(2,1)S(1)}, u32[]{:S(2)}, u32[]{:S(2)}) collective-permute-start(bf16[64,256]{1,0:T(8,128)(2,1)S(1)} %bitcast.155), channel_id=1, source_target_pairs={{0,64},{64,128},{128,192},{1,65},{65,129},{129,193},{2,66},{66,130... | collective-permute-start | bytes 98312 | tf_op jit(solution)/shard_map/ppermute | solution.py:348
  22.6 4.7 %collective-permute-start.5 = (bf16[64,256]{1,0:T(8,128)(2,1)S(1)}, bf16[64,256]{1,0:T(8,128)(2,1)S(1)}, u32[]{:S(2)}, u32[]{:S(2)}) collective-permute-start(bf16[64,256]{1,0:T(8,128)(2,1)S(1)} %bitcast.156), channel_id=1, source_target_pairs={{64,0},{128,64},{192,128},{65,1},{129,65},{193,129},{66,2},{130,66... | collective-permute-start | bytes 98312 | tf_op jit(solution)/shard_map/ppermute | solution.py:348
  27.4 6.5 %collective-permute-start.7 = (bf16[4,18,256]{2,1,0:T(8,128)(2,1)S(1)}, bf16[4,18,256]{2,1,0:T(8,128)(2,1)S(1)}, u32[]{:S(2)}, u32[]{:S(2)}) collective-permute-start(bf16[4,18,256]{2,1,0:T(8,128)(2,1)S(1)} %maximum_maximum_fusion.1), channel_id=1, source_target_pairs={{1,0},{2,1},{3,2},{5,4},{6,5},{7,6},{9,8},{10,9},{11,10},{13,12},{... | collective-permute-start | bytes 110600 | tf_op jit(solution)/shard_map/ppermute | solution.py:346
  28.7 6.1 %collective-permute-start.6 = (bf16[4,18,256]{2,1,0:T(8,128)(2,1)S(1)}, bf16[4,18,256]{2,1,0:T(8,128)(2,1)S(1)}, u32[]{:S(2)}, u32[]{:S(2)}) collective-permute-start(bf16[4,18,256]{2,1,0:T(8,128)(2,1)S(1)} %maximum_maximum_fusion), channel_id=1, source_target_pairs={{0,1},{1,2},{2,3},{4,5},{5,6},{6,7},{8,9},{9,10},{10,11},{12,13},{... | collective-permute-start | bytes 110600 | tf_op jit(solution)/shard_map/ppermute | solution.py:346
  44.9 7.2 %collective-permute-start.17 = (bf16[128,1024]{1,0:T(8,128)(2,1)S(1)}, bf16[128,1024]{1,0:T(8,128)(2,1)S(1)}, u32[]{:S(2)}, u32[]{:S(2)}) collective-permute-start(bf16[128,1024]{1,0:T(8,128)(2,1)S(1)} %bitcast.145), channel_id=1, source_target_pairs={{0,3},{1,2},{2,1},{3,0},{4,7},{5,6},{6,5},{7,4},{8,11},{9,10},{10,... | collective-permute-start | bytes 786440 | tf_op jit(solution)/shard_map/ppermute | solution.py:348
  47.6 13.3 %collective-permute-start.13 = (bf16[128,1024]{1,0:T(8,128)(2,1)S(1)}, bf16[128,1024]{1,0:T(8,128)(2,1)S(1)}, u32[]{:S(2)}, u32[]{:S(2)}) collective-permute-start(bf16[128,1024]{1,0:T(8,128)(2,1)S(1)} %bitcast.146), channel_id=1, source_target_pairs={{0,1},{1,0},{2,3},{3,2},{4,5},{5,4},{6,7},{7,6},{8,9},{9,8},{10,11... | collective-permute-start | bytes 786440 | tf_op jit(solution)/shard_map/ppermute | solution.py:348
  48.5 40.3 %collective-permute-start.12 = (bf16[3072,128]{1,0:T(8,128)(2,1)S(1)}, bf16[3072,128]{1,0:T(8,128)(2,1)S(1)}, u32[]{:S(2)}, u32[]{:S(2)}) collective-permute-start(bf16[3072,128]{1,0:T(8,128)(2,1)S(1)} %bitcast.83), channel_id=1, source_target_pairs={{0,192},{64,0},{128,64},{192,128},{1,193},{65,1},{129,65},{193,129... | collective-permute-start | bytes 2359304 | tf_op jit(solution)/shard_map/ppermute | solution.py:348
  48.6 40.9 %collective-permute-start.11 = (bf16[3072,128]{1,0:T(8,128)(2,1)S(1)}, bf16[3072,128]{1,0:T(8,128)(2,1)S(1)}, u32[]{:S(2)}, u32[]{:S(2)}) collective-permute-start(bf16[3072,128]{1,0:T(8,128)(2,1)S(1)} %bitcast.84), channel_id=1, source_target_pairs={{0,128},{64,192},{128,0},{192,64},{1,129},{65,193},{129,1},{193,65... | collective-permute-start | bytes 2359304 | tf_op jit(solution)/shard_map/ppermute | solution.py:348
  51.7 37.8 %collective-permute-start.10 = (bf16[3072,128]{1,0:T(8,128)(2,1)S(1)}, bf16[3072,128]{1,0:T(8,128)(2,1)S(1)}, u32[]{:S(2)}, u32[]{:S(2)}) collective-permute-start(bf16[3072,128]{1,0:T(8,128)(2,1)S(1)} %bitcast.85), channel_id=1, source_target_pairs={{0,64},{64,128},{128,192},{192,0},{1,65},{65,129},{129,193},{193,1... | collective-permute-start | bytes 2359304 | tf_op jit(solution)/shard_map/ppermute | solution.py:348
  52.2 14.9 %collective-permute-start.19 = (bf16[128,1024]{1,0:T(8,128)(2,1)S(1)}, bf16[128,1024]{1,0:T(8,128)(2,1)S(1)}, u32[]{:S(2)}, u32[]{:S(2)}) collective-permute-start(bf16[128,1024]{1,0:T(8,128)(2,1)S(1)} %bitcast.144), channel_id=1, source_target_pairs={{4,8},{12,16},{20,24},{28,32},{36,40},{44,48},{52,56},{8,4},{16,12... | collective-permute-start | bytes 786440 | tf_op jit(solution)/shard_map/ppermute | solution.py:348
  60.9 25.9 %collective-permute-start.15 = (bf16[128,1024]{1,0:T(8,128)(2,1)S(1)}, bf16[128,1024]{1,0:T(8,128)(2,1)S(1)}, u32[]{:S(2)}, u32[]{:S(2)}) collective-permute-start(bf16[128,1024]{1,0:T(8,128)(2,1)S(1)} %bitcast.110), channel_id=1, source_target_pairs={{0,2},{1,3},{2,0},{3,1},{4,6},{5,7},{6,4},{7,5},{8,10},{9,11},{10,... | collective-permute-start | bytes 786440 | tf_op jit(solution)/shard_map/ppermute | solution.py:348
  67.1 20.2 %collective-permute-start.8 = (bf16[128,1024]{1,0:T(8,128)(2,1)S(1)}, bf16[128,1024]{1,0:T(8,128)(2,1)S(1)}, u32[]{:S(2)}, u32[]{:S(2)}) collective-permute-start(bf16[128,1024]{1,0:T(8,128)(2,1)S(1)} %bitcast.111), channel_id=1, source_target_pairs={{0,4},{4,0},{8,12},{12,8},{16,20},{20,16},{24,28},{28,24},{32,36},... | collective-permute-start | bytes 786440 | tf_op jit(solution)/shard_map/ppermute | solution.py:348
  87.3 15.5 %collective-permute-start.14 = (bf16[128,1024]{1,0:T(8,128)(2,1)S(1)}, bf16[128,1024]{1,0:T(8,128)(2,1)S(1)}, u32[]{:S(2)}, u32[]{:S(2)}) collective-permute-start(bf16[128,1024]{1,0:T(8,128)(2,1)S(1)} %collective-permute-done.13), channel_id=1, source_target_pairs={{0,4},{4,0},{8,12},{12,8},{16,20},{20,16},{24,28},{28,24},{32,36},... | collective-permute-start | bytes 786440 | tf_op jit(solution)/shard_map/ppermute | solution.py:348
  88.5 12.6 %collective-permute-start.16 = (bf16[128,1024]{1,0:T(8,128)(2,1)S(1)}, bf16[128,1024]{1,0:T(8,128)(2,1)S(1)}, u32[]{:S(2)}, u32[]{:S(2)}) collective-permute-start(bf16[128,1024]{1,0:T(8,128)(2,1)S(1)} %collective-permute-done.15), channel_id=1, source_target_pairs={{0,4},{4,0},{8,12},{12,8},{16,20},{20,16},{24,28},{28,24},{32,36},... | collective-permute-start | bytes 786440 | tf_op jit(solution)/shard_map/ppermute | solution.py:348
  88.9 6.9 %collective-permute-start.22 = (bf16[64,1024]{1,0:T(8,128)(2,1)S(1)}, bf16[64,1024]{1,0:T(8,128)(2,1)S(1)}, u32[]{:S(2)}, u32[]{:S(2)}) collective-permute-start(bf16[64,1024]{1,0:T(8,128)(2,1)S(1)} %get-tuple-element.32), channel_id=1, source_target_pairs={{0,3},{1,2},{2,1},{3,0},{4,7},{5,6},{6,5},{7,4},{8,11},{9,10},{10,... | collective-permute-start | bytes 393224 | tf_op jit(solution)/shard_map/ppermute | solution.py:348
  89.5 10.2 %collective-permute-start.20 = (bf16[64,1024]{1,0:T(8,128)(2,1)S(1)}, bf16[64,1024]{1,0:T(8,128)(2,1)S(1)}, u32[]{:S(2)}, u32[]{:S(2)}) collective-permute-start(bf16[64,1024]{1,0:T(8,128)(2,1)S(1)} %get-tuple-element.32), channel_id=1, source_target_pairs={{0,1},{1,0},{2,3},{3,2},{4,5},{5,4},{6,7},{7,6},{8,9},{9,8},{10,11... | collective-permute-start | bytes 393224 | tf_op jit(solution)/shard_map/ppermute | solution.py:348
  89.5 11.5 %collective-permute-start.21 = (bf16[64,1024]{1,0:T(8,128)(2,1)S(1)}, bf16[64,1024]{1,0:T(8,128)(2,1)S(1)}, u32[]{:S(2)}, u32[]{:S(2)}) collective-permute-start(bf16[64,1024]{1,0:T(8,128)(2,1)S(1)} %get-tuple-element.33), channel_id=1, source_target_pairs={{0,2},{1,3},{2,0},{3,1},{4,6},{5,7},{6,4},{7,5},{8,10},{9,11},{10,... | collective-permute-start | bytes 393224 | tf_op jit(solution)/shard_map/ppermute | solution.py:348
  95.8 10.6 %collective-permute-start.23 = (bf16[64,1024]{1,0:T(8,128)(2,1)S(1)}, bf16[64,1024]{1,0:T(8,128)(2,1)S(1)}, u32[]{:S(2)}, u32[]{:S(2)}) collective-permute-start(bf16[64,1024]{1,0:T(8,128)(2,1)S(1)} %get-tuple-element.33), channel_id=1, source_target_pairs={{0,4},{4,0},{8,12},{12,8},{16,20},{20,16},{24,28},{28,24},{32,36},... | collective-permute-start | bytes 393224 | tf_op jit(solution)/shard_map/ppermute | solution.py:348
  99.7 6.7 %collective-permute-start.26 = (bf16[64,1024]{1,0:T(8,128)(2,1)S(1)}, bf16[64,1024]{1,0:T(8,128)(2,1)S(1)}, u32[]{:S(2)}, u32[]{:S(2)}) collective-permute-start(bf16[64,1024]{1,0:T(8,128)(2,1)S(1)} %collective-permute-done.22), channel_id=1, source_target_pairs={{0,4},{4,0},{8,12},{12,8},{16,20},{20,16},{24,28},{28,24},{32,36},... | collective-permute-start | bytes 393224 | tf_op jit(solution)/shard_map/ppermute | solution.py:348
  101.0 5.4 %collective-permute-start.24 = (bf16[64,1024]{1,0:T(8,128)(2,1)S(1)}, bf16[64,1024]{1,0:T(8,128)(2,1)S(1)}, u32[]{:S(2)}, u32[]{:S(2)}) collective-permute-start(bf16[64,1024]{1,0:T(8,128)(2,1)S(1)} %collective-permute-done.20), channel_id=1, source_target_pairs={{0,4},{4,0},{8,12},{12,8},{16,20},{20,16},{24,28},{28,24},{32,36},... | collective-permute-start | bytes 393224 | tf_op jit(solution)/shard_map/ppermute | solution.py:348
  101.0 5.4 %collective-permute-start.25 = (bf16[64,1024]{1,0:T(8,128)(2,1)S(1)}, bf16[64,1024]{1,0:T(8,128)(2,1)S(1)}, u32[]{:S(2)}, u32[]{:S(2)}) collective-permute-start(bf16[64,1024]{1,0:T(8,128)(2,1)S(1)} %collective-permute-done.21), channel_id=1, source_target_pairs={{0,4},{4,0},{8,12},{12,8},{16,20},{20,16},{24,28},{28,24},{32,36},... | collective-permute-start | bytes 393224 | tf_op jit(solution)/shard_map/ppermute | solution.py:348
  108.6 12.3 %collective-permute-start.29 = (bf16[1024,128]{1,0:T(8,128)(2,1)S(1)}, bf16[1024,128]{1,0:T(8,128)(2,1)S(1)}, u32[]{:S(2)}, u32[]{:S(2)}) collective-permute-start(bf16[1024,128]{1,0:T(8,128)(2,1)S(1)} %bitcast.121), channel_id=1, source_target_pairs={{0,128},{1,132},{2,130},{3,134},{4,129},{5,133},{6,131},{7,135},{8... | collective-permute-start | bytes 786440 | tf_op jit(solution)/shard_map/ppermute | solution.py:348
  112.8 9.7 %collective-permute-start.27 = (bf16[1024,128]{1,0:T(8,128)(2,1)S(1)}, bf16[1024,128]{1,0:T(8,128)(2,1)S(1)}, u32[]{:S(2)}, u32[]{:S(2)}) collective-permute-start(bf16[1024,128]{1,0:T(8,128)(2,1)S(1)} %bitcast.120), channel_id=1, source_target_pairs={{0,64},{1,68},{2,66},{3,70},{4,65},{5,69},{6,67},{7,71},{8,72},{9,... | collective-permute-start | bytes 786440 | tf_op jit(solution)/shard_map/ppermute | solution.py:348
  113.9 11.4 %collective-permute-start.31 = (bf16[1024,128]{1,0:T(8,128)(2,1)S(1)}, bf16[1024,128]{1,0:T(8,128)(2,1)S(1)}, u32[]{:S(2)}, u32[]{:S(2)}) collective-permute-start(bf16[1024,128]{1,0:T(8,128)(2,1)S(1)} %bitcast.119), channel_id=1, source_target_pairs={{0,192},{1,196},{2,194},{3,198},{4,193},{5,197},{6,195},{7,199},{8... | collective-permute-start | bytes 786440 | tf_op jit(solution)/shard_map/ppermute | solution.py:348
  118.8 7.7 %collective-permute-start.33 = (bf16[1024,128]{1,0:T(8,128)(2,1)S(1)}, bf16[1024,128]{1,0:T(8,128)(2,1)S(1)}, u32[]{:S(2)}, u32[]{:S(2)}) collective-permute-start(bf16[1024,128]{1,0:T(8,128)(2,1)S(1)} %bitcast.117), channel_id=1, source_target_pairs={{0,0},{1,4},{2,2},{3,6},{4,1},{5,5},{6,3},{7,7},{8,8},{9,12},{10,1... | collective-permute-start | bytes 786440 | tf_op jit(solution)/shard_map/ppermute | solution.py:348
  121.0 5.6 %collective-permute-start.30 = (bf16[512,128]{1,0:T(8,128)(2,1)S(1)}, bf16[512,128]{1,0:T(8,128)(2,1)S(1)}, u32[]{:S(2)}, u32[]{:S(2)}) collective-permute-start(bf16[512,128]{1,0:T(8,128)(2,1)S(1)} %get-tuple-element.28), channel_id=1, source_target_pairs={{0,4},{4,0},{8,12},{12,8},{16,20},{20,16},{24,28},{28,24},{32,36},... | collective-permute-start | bytes 393224 | tf_op jit(solution)/shard_map/ppermute | solution.py:348
  122.6 4.0 %collective-permute-start.28 = (bf16[512,128]{1,0:T(8,128)(2,1)S(1)}, bf16[512,128]{1,0:T(8,128)(2,1)S(1)}, u32[]{:S(2)}, u32[]{:S(2)}) collective-permute-start(bf16[512,128]{1,0:T(8,128)(2,1)S(1)} %get-tuple-element.30), channel_id=1, source_target_pairs={{0,4},{4,0},{8,12},{12,8},{16,20},{20,16},{24,28},{28,24},{32,36},... | collective-permute-start | bytes 393224 | tf_op jit(solution)/shard_map/ppermute | solution.py:348
  (8 other events, 19.1 us)

commit v4 on v3

--- a/solution.py
+++ b/solution.py
@@ -21,7 +21,8 @@
     return lax.rem(h, 2), w, lax.rem(w, 2), top, bottom, a
 
 
-def faces_body(cells, far, near, first, last, sems):
+def faces_body(cells, gain, far, near, first, last, gain_out, sems):
+    gain_out[...] = gain[...]
     core = where()[0]
     end = cells.shape[1] - 1
     far_at = core * end
@@ -35,20 +36,20 @@
         copy.wait()
 
 
-def faces(cells):
+def faces(cells, gain):
     _, rows, cols, depth = cells.shape
     vmem = pl.BlockSpec(memory_space=pltpu.VMEM)
     row = jax.ShapeDtypeStruct((2, cols, depth), cells.dtype)
     face = jax.ShapeDtypeStruct((rows, cols, depth), cells.dtype)
     return pl.pallas_call(
         faces_body,
-        out_shape=(row, row, face, face),
-        in_specs=[pl.BlockSpec(memory_space=pltpu.HBM)],
-        out_specs=(vmem,) * 4,
+        out_shape=(row, row, face, face, jax.ShapeDtypeStruct(gain.shape, gain.dtype)),
+        in_specs=[pl.BlockSpec(memory_space=pltpu.HBM), vmem],
+        out_specs=(vmem,) * 5,
         scratch_shapes=[pltpu.SemaphoreType.DMA((6,))],
         compiler_params=pltpu.CompilerParams(vmem_limit_bytes=4 * 2**20),
         name="faces",
-    )(cells)
+    )(cells, gain)
 
 
 def project_body(groups, *refs):
@@ -228,11 +229,14 @@
 
 
 def conv_body(
-    own, before, after, rim, rim_before, rim_after, left, right, gain, w_ref,
+    own0, own1, before, after, rim, rim_before, rim_after, left, right, gain, w_hbm,
     block_ref, keep_ref, give_ref, edge_ref, taps, raw, left_n, right_n, sums,
+    w_ref, w_sem,
 ):
+    fetch = pltpu.make_async_copy(w_hbm, w_ref, w_sem)
+    fetch.start()
     core, frame = where()[0], where()[2]
-    frames, h_dev, w_dev, channels = own.shape
+    frames, h_dev, w_dev, channels = (2,) + own0.shape[1:]
     rim_rows = rim.shape[1]
     far = rim_rows - 1
     rows = h_dev + far - 1
@@ -266,15 +270,17 @@
         elif t == frames + 1:
             main, edge, lead = after, rim_after, 0
         else:
-            main, edge, lead = own, rim, t - 1
+            main, edge, lead = (own0, own1)[t - 1], rim, t - 1
         inner = 0 < t <= frames
         for start in range(0, h_dev, 8):
-            put(main, lead, t, start, 8, own_at + start, start, inner)
+            put(main, 0, t, start, 8, own_at + start, start, inner)
         put(edge, lead, t, 0, far, far_at, h_dev, inner)
         put(edge, lead, t, far, 1, near_at, h_dev + far, inner)
 
     chunk_rows = rows
     pieces = channels // LANES
+
+    fetch.wait()
 
     def convolve(t, start):
         parts = [
@@ -313,16 +319,16 @@
         edge_ref[k] = out[pl.ds(core * (rows // 2 - WIN), WIN)]
 
 
-def conv_block(own, before, after, rim, rim_before, rim_after, left, right, gain, weight):
-    frames, h_dev, w_dev, channels = own.shape
+def conv_block(own0, own1, before, after, rim, rim_before, rim_after, left, right, gain, weight):
+    frames, h_dev, w_dev, channels = (2,) + own0.shape[1:]
     rows = h_dev + rim.shape[1] - 2
     vmem = pl.BlockSpec(memory_space=pltpu.VMEM)
     patch = jax.ShapeDtypeStruct((rows // 2, w_dev // 2, 4 * channels), jnp.bfloat16)
     edge = jax.ShapeDtypeStruct((2, WIN, w_dev // 2, 4 * channels), jnp.bfloat16)
     return pl.pallas_call(
         conv_body,
-        out_shape=(jax.ShapeDtypeStruct(own.shape, jnp.bfloat16), patch, patch, edge),
-        in_specs=[vmem] * 10,
+        out_shape=(jax.ShapeDtypeStruct((2,) + own0.shape[1:], jnp.bfloat16), patch, patch, edge),
+        in_specs=[vmem] * 10 + [pl.BlockSpec(memory_space=pltpu.HBM)],
         out_specs=(vmem,) * 4,
         scratch_shapes=[
             pltpu.VMEM((frames + 2, rows + 2, w_dev, 3 * channels), jnp.bfloat16),
@@ -330,15 +336,17 @@
             pltpu.VMEM(left.shape, jnp.float32),
             pltpu.VMEM(left.shape, jnp.float32),
             pltpu.VMEM((channels // LANES, rows, w_dev, LANES), jnp.float32),
+            pltpu.VMEM(weight.shape, weight.dtype),
+            pltpu.SemaphoreType.DMA,
         ],
-        compiler_params=pltpu.CompilerParams(vmem_limit_bytes=20 * 2**20),
+        compiler_params=pltpu.CompilerParams(vmem_limit_bytes=50 * 2**20),
         cost_estimate=pl.CostEstimate(
             flops=2 * 27 * frames * rows * w_dev * channels * channels,
             bytes_accessed=8 * 2**20,
             transcendentals=2**20,
         ),
         name="conv",
-    )(own, before, after, rim, rim_before, rim_after, left, right, gain, weight)
+    )(own0, own1, before, after, rim, rim_before, rim_after, left, right, gain, weight)
 
 
 def permute(cells, axis, pairs):
@@ -356,30 +364,6 @@
         permute(tail, axis, [(i, i + 1) for i in range(count - 1)]),
         permute(head, axis, [(i + 1, i) for i in range(count - 1)]),
     )
-
-
-def choose_body(mine, swapped, out):
-    place = where()
-
-    @pl.when(place[0] == place[2])
-    def _():
-        out[...] = mine[...]
-
-    @pl.when(place[0] != place[2])
-    def _():
-        out[...] = swapped[...]
-
-
-def choose(mine, swapped):
-    vmem = pl.BlockSpec(memory_space=pltpu.VMEM)
-    return pl.pallas_call(
-        choose_body,
-        out_shape=jax.ShapeDtypeStruct(mine.shape, mine.dtype),
-        in_specs=[vmem, vmem],
-        out_specs=vmem,
-        compiler_params=pltpu.CompilerParams(vmem_limit_bytes=4 * 2**20),
-        name="choose",
-    )(mine, swapped)
 
 
 def assemble_body(count, order, *refs):
@@ -427,7 +411,7 @@
         return pairs
 
     axes = ("ta", "ha", "wa")
-    far_row, near_row, first, last = faces(latents)
+    far_row, near_row, first, last, gain = faces(latents, norm_gain[None])
     odd = [(i, i + 1) for i in range(1, n_ha - 1, 2)]
     odd += [(j, i) for i, j in odd]
     rim_far = permute(far_row[:, None], "ha", odd)
@@ -437,34 +421,34 @@
     rim_near = permute(near_row[:, None], "ha", [(i, i ^ 1) for i in range(n_ha)])
     rim = jnp.concatenate([rim_far, rim_near], axis=1)
     rim_before, rim_after = ends(rim, "ta", 0, 1)
-    last = w_dev - 1
 
     def side(at):
         return jnp.concatenate(
             [
-                jnp.concatenate([x[:, :, at] for x in (before, latents, after)], axis=0),
+                jnp.concatenate([x[:, :, at] for x in (before, first[None], last[None], after)], axis=0),
                 jnp.concatenate([x[:, :, at] for x in (rim_before, rim, rim_after)], axis=0),
             ],
             axis=1,
         )
 
-    left = permute(side(last), "wa", [(i, i + 1) for i in range(n_wa - 1)])
+    left = permute(side(w_dev - 1), "wa", [(i, i + 1) for i in range(n_wa - 1)])
     right = permute(side(0), "wa", [(i + 1, i) for i in range(n_wa - 1)])
     mine = qkv_weight[:, 0].transpose(1, 0, 2)
-    swapped = permute(
+    mine = permute(
         mine,
         axes,
-        everywhere(lambda ta, ha, wa: (ta, ha, wa ^ 1) if (wa ^ 1) % 2 != ha % 2 else None),
+        everywhere(
+            lambda ta, ha, wa: (ta, ha, wa) if ha % 2 == wa % 2 else (ta, ha ^ 1, wa ^ 1)
+        ),
     )
-    mine = choose(mine, swapped)
     weights = [mine] + [
         permute(mine, "ta", [(i, (i + d) % n_ta) for i in range(n_ta)])
         for d in range(1, n_ta)
     ]
 
     block_out, keep, give, edge = conv_block(
-        latents, before, after, rim, rim_before, rim_after, left, right,
-        norm_gain[None], conv_weight.reshape(9, 3 * channels, channels),
+        first[None], last[None], before, after, rim, rim_before, rim_after, left, right,
+        gain, conv_weight.reshape(9, 3 * channels, channels),
     )
     own = [keep] + [
         permute(give if d % 2 else keep, "wa", [(i, i ^ d) for i in range(n_wa)])

time: 130 us -> 129 us (level)
  waiting for transfers between devices: 26.9 us -> 31 us
  local copies, waits for them, and re-layouts: 6.12 us -> 2.5 us
  starting transfers between devices: 74.4 us -> 72 us
    ppermute x2, starting transfers between devices: 6.25 us -> 2.58 us  [permute(): return lax.ppermute(cells, axis, pairs)]
    unnamed x12 -> x4, local copies, waits for them, and re-layouts: 4.77 us -> 1.71 us
    ppermute x2, waiting for transfers between devices: 0.97 us -> 3.98 us  [permute(): return lax.ppermute(cells, axis, pairs)]
    pallas_call x3 -> x2, Pallas kernels: 6.62 us -> 7.43 us  [the longest x1 7.25 us: conv_block(): pl.pallas_call(conv_body, out_shape=(jax.ShapeDtypeStruct((2,) + own0.sha...]
  transfers between devices with their start and end apart: 35 -> 35, of which waited for: 11 -> 12; matrix products, arithmetic and copies ran while one was open for 1% -> 1% of each run, Pallas kernels for 13% -> 14%
where the time goes in v4:
time: 129 us; the launch traced here: 128 us
  starting transfers between devices  72 us (56%)
  waiting for transfers between devices  31 us (24%)
  Pallas kernels  20.9 us (16%)
  local copies, waits for them, and re-layouts  2.5 us (2%)
  between operations  1.29 us (1%)
    ppermute x33, starting transfers between devices, permute(): return lax.ppermute(flat, axis, pairs).reshape(cells.shape)  69.4 us
    ppermute x33, waiting for transfers between devices, permute(): return lax.ppermute(flat, axis, pairs).reshape(cells.shape)  27 us
    pallas_call x1, Pallas kernels, conv_block(): pl.pallas_call(conv_body, out_shape=(jax.ShapeDtypeStruct((2,) + own0.sha...  7.25 us
    pallas_call x5, Pallas kernels, project(): pl.pallas_call(functools.partial(project_body, [(first, len(own)) for fir...  6.26 us
    ppermute x2, waiting for transfers between devices, permute(): return lax.ppermute(cells, axis, pairs)  3.98 us
    pallas_call x4, Pallas kernels, one_head(): pl.pallas_call(functools.partial(outer_body, d, math.log2(math.e) * size...  3.84 us
    ppermute x2, starting transfers between devices, permute(): return lax.ppermute(cells, axis, pairs)  2.58 us
  transfers between devices with their start and end apart: 35, of which 12 were waited for; matrix products, arithmetic and copies ran while one was open for 1% of the time, Pallas kernels for 14%

profile of v4, /device:TPU:3, one launch (start us, length us, event | category | flops | bytes accessed | tf_op | source)
XLA Modules:
  0.0 127.9 jit_solution(13782572748210818603)
XLA Ops:
  3.3 8.7 %collective-permute-start.2 = (bf16[64,256]{1,0:T(8,128)(2,1)S(1)}, bf16[64,256]{1,0:T(8,128)(2,1)S(1)}, u32[]{:S(2)}, u32[]{:S(2)}) collective-permute-start(bf16[64,256]{1,0:T(8,128)(2,1)S(1)} %bitcast.151), channel_id=1, source_target_pairs={{4,8},{12,16},{20,24},{28,32},{36,40},{44,48},{52,56},{8,4},{16,12... | collective-permute-start | bytes 98312 | tf_op jit(solution)/shard_map/ppermute | solution.py:356
  12.0 3.2 %collective-permute-start = (bf16[512,256]{1,0:T(8,128)(2,1)S(1)}, bf16[512,256]{1,0:T(8,128)(2,1)S(1)}, u32[]{:S(2)}, u32[]{:S(2)}) collective-permute-start(bf16[512,256]{1,0:T(8,128)(2,1)S(1)} %bitcast.127), channel_id=1, source_target_pairs={{0,64},{64,128},{128,192},{1,65},{65,129},{129,193},{2,66},{66,130... | collective-permute-start | bytes 786440 | tf_op jit(solution)/shard_map/ppermute | solution.py:356
  15.3 1.3 %collective-permute-start.1 = (bf16[512,256]{1,0:T(8,128)(2,1)S(1)}, bf16[512,256]{1,0:T(8,128)(2,1)S(1)}, u32[]{:S(2)}, u32[]{:S(2)}) collective-permute-start(bf16[512,256]{1,0:T(8,128)(2,1)S(1)} %bitcast.126), channel_id=1, source_target_pairs={{64,0},{128,64},{192,128},{65,1},{129,65},{193,129},{66,2},{130,66... | collective-permute-start | bytes 786440 | tf_op jit(solution)/shard_map/ppermute | solution.py:356
  16.6 3.3 %collective-permute-start.9 = (bf16[3072,128]{1,0:T(8,128)(2,1)}, bf16[3072,128]{1,0:T(8,128)(2,1)S(1)}, u32[]{:S(2)}, u32[]{:S(2)}) collective-permute-start(bf16[3072,128]{1,0:T(8,128)(2,1)} %bitcast.159), channel_id=1, source_target_pairs={{0,0},{1,4},{2,2},{3,6},{4,1},{5,5},{6,3},{7,7},{8,8},{9,12},{10,1... | collective-permute-start | bytes 2359304 | tf_op jit(solution)/shard_map/ppermute | solution.py:356
  20.6 4.3 %collective-permute-start.4 = (bf16[64,256]{1,0:T(8,128)(2,1)S(1)}, bf16[64,256]{1,0:T(8,128)(2,1)S(1)}, u32[]{:S(2)}, u32[]{:S(2)}) collective-permute-start(bf16[64,256]{1,0:T(8,128)(2,1)S(1)} %bitcast.156), channel_id=1, source_target_pairs={{0,64},{64,128},{128,192},{1,65},{65,129},{129,193},{2,66},{66,130... | collective-permute-start | bytes 98312 | tf_op jit(solution)/shard_map/ppermute | solution.py:356
  25.0 1.3 %collective-permute-start.5 = (bf16[64,256]{1,0:T(8,128)(2,1)S(1)}, bf16[64,256]{1,0:T(8,128)(2,1)S(1)}, u32[]{:S(2)}, u32[]{:S(2)}) collective-permute-start(bf16[64,256]{1,0:T(8,128)(2,1)S(1)} %bitcast.157), channel_id=1, source_target_pairs={{64,0},{128,64},{192,128},{65,1},{129,65},{193,129},{66,2},{130,66... | collective-permute-start | bytes 98312 | tf_op jit(solution)/shard_map/ppermute | solution.py:356
  26.3 3.9 %collective-permute-done.5 = bf16[64,256]{1,0:T(8,128)(2,1)S(1)} collective-permute-done((bf16[64,256]{1,0:T(8,128)(2,1)S(1)}, bf16[64,256]{1,0:T(8,128)(2,1)S(1)}, u32[]{:S(2)}, u32[]{:S(2)}) %collective-permute-start.5) | collective-permute-done | bytes 32800 | tf_op jit(solution)/shard_map/ppermute | solution.py:356
  30.4 1.3 %collective-permute-start.6 = (bf16[4,18,256]{2,1,0:T(8,128)(2,1)S(1)}, bf16[4,18,256]{2,1,0:T(8,128)(2,1)S(1)}, u32[]{:S(2)}, u32[]{:S(2)}) collective-permute-start(bf16[4,18,256]{2,1,0:T(8,128)(2,1)S(1)} %maximum_maximum_fusion), channel_id=1, source_target_pairs={{0,1},{1,2},{2,3},{4,5},{5,6},{6,7},{8,9},{9,10},{10,11},{12,13},{... | collective-permute-start | bytes 110600 | tf_op jit(solution)/shard_map/ppermute | solution.py:354
  31.7 1.3 %collective-permute-start.7 = (bf16[4,18,256]{2,1,0:T(8,128)(2,1)S(1)}, bf16[4,18,256]{2,1,0:T(8,128)(2,1)S(1)}, u32[]{:S(2)}, u32[]{:S(2)}) collective-permute-start(bf16[4,18,256]{2,1,0:T(8,128)(2,1)S(1)} %maximum_maximum_fusion.1), channel_id=1, source_target_pairs={{1,0},{2,1},{3,2},{5,4},{6,5},{7,6},{9,8},{10,9},{11,10},{13,12},{... | collective-permute-start | bytes 110600 | tf_op jit(solution)/shard_map/ppermute | solution.py:354
  33.2 4.0 %collective-permute-done.7.right = bf16[4,18,256]{2,1,0:T(8,128)(2,1)S(1)} collective-permute-done((bf16[4,18,256]{2,1,0:T(8,128)(2,1)S(1)}, bf16[4,18,256]{2,1,0:T(8,128)(2,1)S(1)}, u32[]{:S(2)}, u32[]{:S(2)}) %collective-permute-start.7) | collective-permute-done | bytes 36896 | tf_op jit(solution)/shard_map/ppermute | solution.py:354
  37.2 7.2 %conv.1 = (bf16[2,16,32,256]{3,2,1,0:T(8,128)(2,1)}, bf16[8,16,1024]{2,1,0:T(8,128)(2,1)S(1)}, bf16[8,16,1024]{2,1,0:T(8,128)(2,1)S(1)}, bf16[2,4,16,1024]{3,2,1,0:T(8,128)(2,1)S(1)}) custom-call(bf16[1,16,32,256]{3,2,1,0:T(8,128)(2,1)S(1)} %copy.30.own0, bf16[1,16,32,256]{3,2,1,0:T(8,128)(2,1)S(1)} %copy.31.own1, bf16[1,16,32,256]{3,2,1,0:T(8,128)(2,1)S(1)} %bitcast.140, ...), custom_call_target="tpu_custom_call" | custom-call | flops 3623878656 | bytes 8388608 | tf_op jit(solution)/shard_map/conv/pallas_call | solution.py:328
  46.8 2.3 %collective-permute-start.11 = (bf16[3072,128]{1,0:T(8,128)(2,1)S(1)}, bf16[3072,128]{1,0:T(8,128)(2,1)S(1)}, u32[]{:S(2)}, u32[]{:S(2)}) collective-permute-start(bf16[3072,128]{1,0:T(8,128)(2,1)S(1)} %collective-permute-done.9), channel_id=1, source_target_pairs={{0,128},{64,192},{128,0},{192,64},{1,129},{65,193},{129,1},{193,65... | collective-permute-start | bytes 2359304 | tf_op jit(solution)/shard_map/ppermute | solution.py:356
  49.6 2.1 %collective-permute-done.17 = bf16[128,1024]{1,0:T(8,128)(2,1)S(1)} collective-permute-done((bf16[128,1024]{1,0:T(8,128)(2,1)S(1)}, bf16[128,1024]{1,0:T(8,128)(2,1)S(1)}, u32[]{:S(2)}, u32[]{:S(2)}) %collective-permute-start.17) | collective-permute-done | bytes 262176 | tf_op jit(solution)/shard_map/ppermute | solution.py:356
  51.7 8.2 %collective-permute-start.19 = (bf16[128,1024]{1,0:T(8,128)(2,1)S(1)}, bf16[128,1024]{1,0:T(8,128)(2,1)S(1)}, u32[]{:S(2)}, u32[]{:S(2)}) collective-permute-start(bf16[128,1024]{1,0:T(8,128)(2,1)S(1)} %bitcast.148), channel_id=1, source_target_pairs={{4,8},{12,16},{20,24},{28,32},{36,40},{44,48},{52,56},{8,4},{16,12... | collective-permute-start | bytes 786440 | tf_op jit(solution)/shard_map/ppermute | solution.py:356
  59.9 2.8 %collective-permute-start.15 = (bf16[128,1024]{1,0:T(8,128)(2,1)S(1)}, bf16[128,1024]{1,0:T(8,128)(2,1)S(1)}, u32[]{:S(2)}, u32[]{:S(2)}) collective-permute-start(bf16[128,1024]{1,0:T(8,128)(2,1)S(1)} %bitcast.114), channel_id=1, source_target_pairs={{0,2},{1,3},{2,0},{3,1},{4,6},{5,7},{6,4},{7,5},{8,10},{9,11},{10,... | collective-permute-start | bytes 786440 | tf_op jit(solution)/shard_map/ppermute | solution.py:356
  62.7 4.2 %collective-permute-done.19 = bf16[128,1024]{1,0:T(8,128)(2,1)S(1)} collective-permute-done((bf16[128,1024]{1,0:T(8,128)(2,1)S(1)}, bf16[128,1024]{1,0:T(8,128)(2,1)S(1)}, u32[]{:S(2)}, u32[]{:S(2)}) %collective-permute-start.19) | collective-permute-done | bytes 262176 | tf_op jit(solution)/shard_map/ppermute | solution.py:356
  66.9 8.3 %collective-permute-start.8 = (bf16[128,1024]{1,0:T(8,128)(2,1)S(1)}, bf16[128,1024]{1,0:T(8,128)(2,1)S(1)}, u32[]{:S(2)}, u32[]{:S(2)}) collective-permute-start(bf16[128,1024]{1,0:T(8,128)(2,1)S(1)} %bitcast.115), channel_id=1, source_target_pairs={{0,4},{4,0},{8,12},{12,8},{16,20},{20,16},{24,28},{28,24},{32,36},... | collective-permute-start | bytes 786440 | tf_op jit(solution)/shard_map/ppermute | solution.py:356
  75.2 8.9 %collective-permute-done.15 = bf16[128,1024]{1,0:T(8,128)(2,1)S(1)} collective-permute-done((bf16[128,1024]{1,0:T(8,128)(2,1)S(1)}, bf16[128,1024]{1,0:T(8,128)(2,1)S(1)}, u32[]{:S(2)}, u32[]{:S(2)}) %collective-permute-start.15) | collective-permute-done | bytes 262176 | tf_op jit(solution)/shard_map/ppermute | solution.py:356
  86.1 2.8 %collective-permute-start.22 = (bf16[64,1024]{1,0:T(8,128)(2,1)S(1)}, bf16[64,1024]{1,0:T(8,128)(2,1)S(1)}, u32[]{:S(2)}, u32[]{:S(2)}) collective-permute-start(bf16[64,1024]{1,0:T(8,128)(2,1)S(1)} %get-tuple-element.32), channel_id=1, source_target_pairs={{0,3},{1,2},{2,1},{3,0},{4,7},{5,6},{6,5},{7,4},{8,11},{9,10},{10,... | collective-permute-start | bytes 393224 | tf_op jit(solution)/shard_map/ppermute | solution.py:356
  89.7 1.2 project.5.p0
  91.0 1.3 project.8.p3
  92.9 1.6 %collective-permute-start.23 = (bf16[64,1024]{1,0:T(8,128)(2,1)S(1)}, bf16[64,1024]{1,0:T(8,128)(2,1)S(1)}, u32[]{:S(2)}, u32[]{:S(2)}) collective-permute-start(bf16[64,1024]{1,0:T(8,128)(2,1)S(1)} %get-tuple-element.33), channel_id=1, source_target_pairs={{0,4},{4,0},{8,12},{12,8},{16,20},{20,16},{24,28},{28,24},{32,36},... | collective-permute-start | bytes 393224 | tf_op jit(solution)/shard_map/ppermute | solution.py:356
  94.5 4.1 %collective-permute-done.20 = bf16[64,1024]{1,0:T(8,128)(2,1)S(1)} collective-permute-done((bf16[64,1024]{1,0:T(8,128)(2,1)S(1)}, bf16[64,1024]{1,0:T(8,128)(2,1)S(1)}, u32[]{:S(2)}, u32[]{:S(2)}) %collective-permute-start.20) | collective-permute-done | bytes 131104 | tf_op jit(solution)/shard_map/ppermute | solution.py:356
  100.1 1.2 project.7.p2
  101.4 1.3 project.6.p1
  102.6 2.3 %inner.1 = bf16[4,2,4,64,128]{4,3,2,1,0:T(8,128)(2,1)S(1)} custom-call(bf16[1,16,16,1536]{3,2,1,0:T(8,128)(2,1)S(1)} %project.5.p0, bf16[1,16,16,1536]{3,2,1,0:T(8,128)(2,1)S(1)} %project.6.p1, bf16[1,16,16,1536]{3,2,1,0:T(8,128)(2,1)S(1)} %project.7.p2, bf16[1,16,16,1536]{3,2,1,0:T(8,128)(2,1)S(1)} %project.8.p3), custom_call_target="tpu_custom_call" | custom-call | flops 1207959552 | bytes 1048576 | tf_op jit(solution)/shard_map/inner/pallas_call | solution.py:199
  105.0 1.3 project.9.halo
  107.2 2.6 %collective-permute-start.29 = (bf16[1024,128]{1,0:T(8,128)(2,1)S(1)}, bf16[1024,128]{1,0:T(8,128)(2,1)S(1)}, u32[]{:S(2)}, u32[]{:S(2)}) collective-permute-start(bf16[1024,128]{1,0:T(8,128)(2,1)S(1)} %bitcast.125), channel_id=1, source_target_pairs={{0,128},{1,132},{2,130},{3,134},{4,129},{5,133},{6,131},{7,135},{8... | collective-permute-start | bytes 786440 | tf_op jit(solution)/shard_map/ppermute | solution.py:356
  112.0 3.8 %collective-permute-start.31 = (bf16[1024,128]{1,0:T(8,128)(2,1)S(1)}, bf16[1024,128]{1,0:T(8,128)(2,1)S(1)}, u32[]{:S(2)}, u32[]{:S(2)}) collective-permute-start(bf16[1024,128]{1,0:T(8,128)(2,1)S(1)} %bitcast.123), channel_id=1, source_target_pairs={{0,192},{1,196},{2,194},{3,198},{4,193},{5,197},{6,195},{7,199},{8... | collective-permute-start | bytes 786440 | tf_op jit(solution)/shard_map/ppermute | solution.py:356
  116.8 3.5 %collective-permute-start.33 = (bf16[1024,128]{1,0:T(8,128)(2,1)S(1)}, bf16[1024,128]{1,0:T(8,128)(2,1)S(1)}, u32[]{:S(2)}, u32[]{:S(2)}) collective-permute-start(bf16[1024,128]{1,0:T(8,128)(2,1)S(1)} %bitcast.121), channel_id=1, source_target_pairs={{0,0},{1,4},{2,2},{3,6},{4,1},{5,5},{6,3},{7,7},{8,8},{9,12},{10,1... | collective-permute-start | bytes 786440 | tf_op jit(solution)/shard_map/ppermute | solution.py:356
  120.3 1.9 %collective-permute-start.30 = (bf16[512,128]{1,0:T(8,128)(2,1)S(1)}, bf16[512,128]{1,0:T(8,128)(2,1)S(1)}, u32[]{:S(2)}, u32[]{:S(2)}) collective-permute-start(bf16[512,128]{1,0:T(8,128)(2,1)S(1)} %get-tuple-element.28), channel_id=1, source_target_pairs={{0,4},{4,0},{8,12},{12,8},{16,20},{20,16},{24,28},{28,24},{32,36},... | collective-permute-start | bytes 393224 | tf_op jit(solution)/shard_map/ppermute | solution.py:356
  122.2 2.3 %collective-permute-start.28 = (bf16[512,128]{1,0:T(8,128)(2,1)S(1)}, bf16[512,128]{1,0:T(8,128)(2,1)S(1)}, u32[]{:S(2)}, u32[]{:S(2)}) collective-permute-start(bf16[512,128]{1,0:T(8,128)(2,1)S(1)} %get-tuple-element.30), channel_id=1, source_target_pairs={{0,4},{4,0},{8,12},{12,8},{16,20},{20,16},{24,28},{28,24},{32,36},... | collective-permute-start | bytes 393224 | tf_op jit(solution)/shard_map/ppermute | solution.py:356
  (83 shorter events, 18.8 us)
Async XLA Ops:
  2.5 17.8 %collective-permute-start.3 = (bf16[64,256]{1,0:T(8,128)(2,1)S(1)}, bf16[64,256]{1,0:T(8,128)(2,1)S(1)}, u32[]{:S(2)}, u32[]{:S(2)}) collective-permute-start(bf16[64,256]{1,0:T(8,128)(2,1)S(1)} %bitcast.152), channel_id=1, source_target_pairs={{0,4},{4,0},{8,12},{12,8},{16,20},{20,16},{24,28},{28,24},{32,36},... | collective-permute-start | bytes 98312 | tf_op jit(solution)/shard_map/ppermute | solution.py:356
  3.3 17.1 %collective-permute-start.2 = (bf16[64,256]{1,0:T(8,128)(2,1)S(1)}, bf16[64,256]{1,0:T(8,128)(2,1)S(1)}, u32[]{:S(2)}, u32[]{:S(2)}) collective-permute-start(bf16[64,256]{1,0:T(8,128)(2,1)S(1)} %bitcast.151), channel_id=1, source_target_pairs={{4,8},{12,16},{20,24},{28,32},{36,40},{44,48},{52,56},{8,4},{16,12... | collective-permute-start | bytes 98312 | tf_op jit(solution)/shard_map/ppermute | solution.py:356
  12.0 18.2 %collective-permute-start = (bf16[512,256]{1,0:T(8,128)(2,1)S(1)}, bf16[512,256]{1,0:T(8,128)(2,1)S(1)}, u32[]{:S(2)}, u32[]{:S(2)}) collective-permute-start(bf16[512,256]{1,0:T(8,128)(2,1)S(1)} %bitcast.127), channel_id=1, source_target_pairs={{0,64},{64,128},{128,192},{1,65},{65,129},{129,193},{2,66},{66,130... | collective-permute-start | bytes 786440 | tf_op jit(solution)/shard_map/ppermute | solution.py:356
  15.3 15.1 %collective-permute-start.1 = (bf16[512,256]{1,0:T(8,128)(2,1)S(1)}, bf16[512,256]{1,0:T(8,128)(2,1)S(1)}, u32[]{:S(2)}, u32[]{:S(2)}) collective-permute-start(bf16[512,256]{1,0:T(8,128)(2,1)S(1)} %bitcast.126), channel_id=1, source_target_pairs={{64,0},{128,64},{192,128},{65,1},{129,65},{193,129},{66,2},{130,66... | collective-permute-start | bytes 786440 | tf_op jit(solution)/shard_map/ppermute | solution.py:356
  16.6 29.5 %collective-permute-start.9 = (bf16[3072,128]{1,0:T(8,128)(2,1)}, bf16[3072,128]{1,0:T(8,128)(2,1)S(1)}, u32[]{:S(2)}, u32[]{:S(2)}) collective-permute-start(bf16[3072,128]{1,0:T(8,128)(2,1)} %bitcast.159), channel_id=1, source_target_pairs={{0,0},{1,4},{2,2},{3,6},{4,1},{5,5},{6,3},{7,7},{8,8},{9,12},{10,1... | collective-permute-start | bytes 2359304 | tf_op jit(solution)/shard_map/ppermute | solution.py:356
  20.6 5.6 %collective-permute-start.4 = (bf16[64,256]{1,0:T(8,128)(2,1)S(1)}, bf16[64,256]{1,0:T(8,128)(2,1)S(1)}, u32[]{:S(2)}, u32[]{:S(2)}) collective-permute-start(bf16[64,256]{1,0:T(8,128)(2,1)S(1)} %bitcast.156), channel_id=1, source_target_pairs={{0,64},{64,128},{128,192},{1,65},{65,129},{129,193},{2,66},{66,130... | collective-permute-start | bytes 98312 | tf_op jit(solution)/shard_map/ppermute | solution.py:356
  25.0 5.3 %collective-permute-start.5 = (bf16[64,256]{1,0:T(8,128)(2,1)S(1)}, bf16[64,256]{1,0:T(8,128)(2,1)S(1)}, u32[]{:S(2)}, u32[]{:S(2)}) collective-permute-start(bf16[64,256]{1,0:T(8,128)(2,1)S(1)} %bitcast.157), channel_id=1, source_target_pairs={{64,0},{128,64},{192,128},{65,1},{129,65},{193,129},{66,2},{130,66... | collective-permute-start | bytes 98312 | tf_op jit(solution)/shard_map/ppermute | solution.py:356
  30.4 2.8 %collective-permute-start.6 = (bf16[4,18,256]{2,1,0:T(8,128)(2,1)S(1)}, bf16[4,18,256]{2,1,0:T(8,128)(2,1)S(1)}, u32[]{:S(2)}, u32[]{:S(2)}) collective-permute-start(bf16[4,18,256]{2,1,0:T(8,128)(2,1)S(1)} %maximum_maximum_fusion), channel_id=1, source_target_pairs={{0,1},{1,2},{2,3},{4,5},{5,6},{6,7},{8,9},{9,10},{10,11},{12,13},{... | collective-permute-start | bytes 110600 | tf_op jit(solution)/shard_map/ppermute | solution.py:354
  31.7 5.5 %collective-permute-start.7 = (bf16[4,18,256]{2,1,0:T(8,128)(2,1)S(1)}, bf16[4,18,256]{2,1,0:T(8,128)(2,1)S(1)}, u32[]{:S(2)}, u32[]{:S(2)}) collective-permute-start(bf16[4,18,256]{2,1,0:T(8,128)(2,1)S(1)} %maximum_maximum_fusion.1), channel_id=1, source_target_pairs={{1,0},{2,1},{3,2},{5,4},{6,5},{7,6},{9,8},{10,9},{11,10},{13,12},{... | collective-permute-start | bytes 110600 | tf_op jit(solution)/shard_map/ppermute | solution.py:354
  44.4 7.2 %collective-permute-start.17 = (bf16[128,1024]{1,0:T(8,128)(2,1)S(1)}, bf16[128,1024]{1,0:T(8,128)(2,1)S(1)}, u32[]{:S(2)}, u32[]{:S(2)}) collective-permute-start(bf16[128,1024]{1,0:T(8,128)(2,1)S(1)} %bitcast.149), channel_id=1, source_target_pairs={{0,3},{1,2},{2,1},{3,0},{4,7},{5,6},{6,5},{7,4},{8,11},{9,10},{10,... | collective-permute-start | bytes 786440 | tf_op jit(solution)/shard_map/ppermute | solution.py:356
  45.1 14.7 %collective-permute-start.13 = (bf16[128,1024]{1,0:T(8,128)(2,1)S(1)}, bf16[128,1024]{1,0:T(8,128)(2,1)S(1)}, u32[]{:S(2)}, u32[]{:S(2)}) collective-permute-start(bf16[128,1024]{1,0:T(8,128)(2,1)S(1)} %bitcast.150), channel_id=1, source_target_pairs={{0,1},{1,0},{2,3},{3,2},{4,5},{5,4},{6,7},{7,6},{8,9},{9,8},{10,11... | collective-permute-start | bytes 786440 | tf_op jit(solution)/shard_map/ppermute | solution.py:356
  46.1 40.0 %collective-permute-start.12 = (bf16[3072,128]{1,0:T(8,128)(2,1)S(1)}, bf16[3072,128]{1,0:T(8,128)(2,1)S(1)}, u32[]{:S(2)}, u32[]{:S(2)}) collective-permute-start(bf16[3072,128]{1,0:T(8,128)(2,1)S(1)} %collective-permute-done.9), channel_id=1, source_target_pairs={{0,192},{64,0},{128,64},{192,128},{1,193},{65,1},{129,65},{193,129... | collective-permute-start | bytes 2359304 | tf_op jit(solution)/shard_map/ppermute | solution.py:356
  46.8 42.1 %collective-permute-start.11 = (bf16[3072,128]{1,0:T(8,128)(2,1)S(1)}, bf16[3072,128]{1,0:T(8,128)(2,1)S(1)}, u32[]{:S(2)}, u32[]{:S(2)}) collective-permute-start(bf16[3072,128]{1,0:T(8,128)(2,1)S(1)} %collective-permute-done.9), channel_id=1, source_target_pairs={{0,128},{64,192},{128,0},{192,64},{1,129},{65,193},{129,1},{193,65... | collective-permute-start | bytes 2359304 | tf_op jit(solution)/shard_map/ppermute | solution.py:356
  49.2 39.7 %collective-permute-start.10 = (bf16[3072,128]{1,0:T(8,128)(2,1)S(1)}, bf16[3072,128]{1,0:T(8,128)(2,1)S(1)}, u32[]{:S(2)}, u32[]{:S(2)}) collective-permute-start(bf16[3072,128]{1,0:T(8,128)(2,1)S(1)} %collective-permute-done.9), channel_id=1, source_target_pairs={{0,64},{64,128},{128,192},{192,0},{1,65},{65,129},{129,193},{193,1... | collective-permute-start | bytes 2359304 | tf_op jit(solution)/shard_map/ppermute | solution.py:356
  51.7 15.2 %collective-permute-start.19 = (bf16[128,1024]{1,0:T(8,128)(2,1)S(1)}, bf16[128,1024]{1,0:T(8,128)(2,1)S(1)}, u32[]{:S(2)}, u32[]{:S(2)}) collective-permute-start(bf16[128,1024]{1,0:T(8,128)(2,1)S(1)} %bitcast.148), channel_id=1, source_target_pairs={{4,8},{12,16},{20,24},{28,32},{36,40},{44,48},{52,56},{8,4},{16,12... | collective-permute-start | bytes 786440 | tf_op jit(solution)/shard_map/ppermute | solution.py:356
  59.9 24.2 %collective-permute-start.15 = (bf16[128,1024]{1,0:T(8,128)(2,1)S(1)}, bf16[128,1024]{1,0:T(8,128)(2,1)S(1)}, u32[]{:S(2)}, u32[]{:S(2)}) collective-permute-start(bf16[128,1024]{1,0:T(8,128)(2,1)S(1)} %bitcast.114), channel_id=1, source_target_pairs={{0,2},{1,3},{2,0},{3,1},{4,6},{5,7},{6,4},{7,5},{8,10},{9,11},{10,... | collective-permute-start | bytes 786440 | tf_op jit(solution)/shard_map/ppermute | solution.py:356
  66.9 17.6 %collective-permute-start.8 = (bf16[128,1024]{1,0:T(8,128)(2,1)S(1)}, bf16[128,1024]{1,0:T(8,128)(2,1)S(1)}, u32[]{:S(2)}, u32[]{:S(2)}) collective-permute-start(bf16[128,1024]{1,0:T(8,128)(2,1)S(1)} %bitcast.115), channel_id=1, source_target_pairs={{0,4},{4,0},{8,12},{12,8},{16,20},{20,16},{24,28},{28,24},{32,36},... | collective-permute-start | bytes 786440 | tf_op jit(solution)/shard_map/ppermute | solution.py:356
  84.5 16.9 %collective-permute-start.14 = (bf16[128,1024]{1,0:T(8,128)(2,1)S(1)}, bf16[128,1024]{1,0:T(8,128)(2,1)S(1)}, u32[]{:S(2)}, u32[]{:S(2)}) collective-permute-start(bf16[128,1024]{1,0:T(8,128)(2,1)S(1)} %collective-permute-done.13), channel_id=1, source_target_pairs={{0,4},{4,0},{8,12},{12,8},{16,20},{20,16},{24,28},{28,24},{32,36},... | collective-permute-start | bytes 786440 | tf_op jit(solution)/shard_map/ppermute | solution.py:356
  85.7 14.5 %collective-permute-start.16 = (bf16[128,1024]{1,0:T(8,128)(2,1)S(1)}, bf16[128,1024]{1,0:T(8,128)(2,1)S(1)}, u32[]{:S(2)}, u32[]{:S(2)}) collective-permute-start(bf16[128,1024]{1,0:T(8,128)(2,1)S(1)} %collective-permute-done.15), channel_id=1, source_target_pairs={{0,4},{4,0},{8,12},{12,8},{16,20},{20,16},{24,28},{28,24},{32,36},... | collective-permute-start | bytes 786440 | tf_op jit(solution)/shard_map/ppermute | solution.py:356
  86.1 6.8 %collective-permute-start.22 = (bf16[64,1024]{1,0:T(8,128)(2,1)S(1)}, bf16[64,1024]{1,0:T(8,128)(2,1)S(1)}, u32[]{:S(2)}, u32[]{:S(2)}) collective-permute-start(bf16[64,1024]{1,0:T(8,128)(2,1)S(1)} %get-tuple-element.32), channel_id=1, source_target_pairs={{0,3},{1,2},{2,1},{3,0},{4,7},{5,6},{6,5},{7,4},{8,11},{9,10},{10,... | collective-permute-start | bytes 393224 | tf_op jit(solution)/shard_map/ppermute | solution.py:356
  88.9 9.7 %collective-permute-start.20 = (bf16[64,1024]{1,0:T(8,128)(2,1)S(1)}, bf16[64,1024]{1,0:T(8,128)(2,1)S(1)}, u32[]{:S(2)}, u32[]{:S(2)}) collective-permute-start(bf16[64,1024]{1,0:T(8,128)(2,1)S(1)} %get-tuple-element.32), channel_id=1, source_target_pairs={{0,1},{1,0},{2,3},{3,2},{4,5},{5,4},{6,7},{7,6},{8,9},{9,8},{10,11... | collective-permute-start | bytes 393224 | tf_op jit(solution)/shard_map/ppermute | solution.py:356
  88.9 10.2 %collective-permute-start.21 = (bf16[64,1024]{1,0:T(8,128)(2,1)S(1)}, bf16[64,1024]{1,0:T(8,128)(2,1)S(1)}, u32[]{:S(2)}, u32[]{:S(2)}) collective-permute-start(bf16[64,1024]{1,0:T(8,128)(2,1)S(1)} %get-tuple-element.33), channel_id=1, source_target_pairs={{0,2},{1,3},{2,0},{3,1},{4,6},{5,7},{6,4},{7,5},{8,10},{9,11},{10,... | collective-permute-start | bytes 393224 | tf_op jit(solution)/shard_map/ppermute | solution.py:356
  92.9 12.1 %collective-permute-start.23 = (bf16[64,1024]{1,0:T(8,128)(2,1)S(1)}, bf16[64,1024]{1,0:T(8,128)(2,1)S(1)}, u32[]{:S(2)}, u32[]{:S(2)}) collective-permute-start(bf16[64,1024]{1,0:T(8,128)(2,1)S(1)} %get-tuple-element.33), channel_id=1, source_target_pairs={{0,4},{4,0},{8,12},{12,8},{16,20},{20,16},{24,28},{28,24},{32,36},... | collective-permute-start | bytes 393224 | tf_op jit(solution)/shard_map/ppermute | solution.py:356
  98.6 6.4 %collective-permute-start.26 = (bf16[64,1024]{1,0:T(8,128)(2,1)S(1)}, bf16[64,1024]{1,0:T(8,128)(2,1)S(1)}, u32[]{:S(2)}, u32[]{:S(2)}) collective-permute-start(bf16[64,1024]{1,0:T(8,128)(2,1)S(1)} %collective-permute-done.22), channel_id=1, source_target_pairs={{0,4},{4,0},{8,12},{12,8},{16,20},{20,16},{24,28},{28,24},{32,36},... | collective-permute-start | bytes 393224 | tf_op jit(solution)/shard_map/ppermute | solution.py:356
  99.1 5.9 %collective-permute-start.24 = (bf16[64,1024]{1,0:T(8,128)(2,1)S(1)}, bf16[64,1024]{1,0:T(8,128)(2,1)S(1)}, u32[]{:S(2)}, u32[]{:S(2)}) collective-permute-start(bf16[64,1024]{1,0:T(8,128)(2,1)S(1)} %collective-permute-done.20), channel_id=1, source_target_pairs={{0,4},{4,0},{8,12},{12,8},{16,20},{20,16},{24,28},{28,24},{32,36},... | collective-permute-start | bytes 393224 | tf_op jit(solution)/shard_map/ppermute | solution.py:356
  100.1 4.9 %collective-permute-start.25 = (bf16[64,1024]{1,0:T(8,128)(2,1)S(1)}, bf16[64,1024]{1,0:T(8,128)(2,1)S(1)}, u32[]{:S(2)}, u32[]{:S(2)}) collective-permute-start(bf16[64,1024]{1,0:T(8,128)(2,1)S(1)} %collective-permute-done.21), channel_id=1, source_target_pairs={{0,4},{4,0},{8,12},{12,8},{16,20},{20,16},{24,28},{28,24},{32,36},... | collective-permute-start | bytes 393224 | tf_op jit(solution)/shard_map/ppermute | solution.py:356
  107.2 13.0 %collective-permute-start.29 = (bf16[1024,128]{1,0:T(8,128)(2,1)S(1)}, bf16[1024,128]{1,0:T(8,128)(2,1)S(1)}, u32[]{:S(2)}, u32[]{:S(2)}) collective-permute-start(bf16[1024,128]{1,0:T(8,128)(2,1)S(1)} %bitcast.125), channel_id=1, source_target_pairs={{0,128},{1,132},{2,130},{3,134},{4,129},{5,133},{6,131},{7,135},{8... | collective-permute-start | bytes 786440 | tf_op jit(solution)/shard_map/ppermute | solution.py:356
  110.8 11.4 %collective-permute-start.27 = (bf16[1024,128]{1,0:T(8,128)(2,1)S(1)}, bf16[1024,128]{1,0:T(8,128)(2,1)S(1)}, u32[]{:S(2)}, u32[]{:S(2)}) collective-permute-start(bf16[1024,128]{1,0:T(8,128)(2,1)S(1)} %bitcast.124), channel_id=1, source_target_pairs={{0,64},{1,68},{2,66},{3,70},{4,65},{5,69},{6,67},{7,71},{8,72},{9,... | collective-permute-start | bytes 786440 | tf_op jit(solution)/shard_map/ppermute | solution.py:356
  112.0 12.5 %collective-permute-start.31 = (bf16[1024,128]{1,0:T(8,128)(2,1)S(1)}, bf16[1024,128]{1,0:T(8,128)(2,1)S(1)}, u32[]{:S(2)}, u32[]{:S(2)}) collective-permute-start(bf16[1024,128]{1,0:T(8,128)(2,1)S(1)} %bitcast.123), channel_id=1, source_target_pairs={{0,192},{1,196},{2,194},{3,198},{4,193},{5,197},{6,195},{7,199},{8... | collective-permute-start | bytes 786440 | tf_op jit(solution)/shard_map/ppermute | solution.py:356
  116.8 8.5 %collective-permute-start.33 = (bf16[1024,128]{1,0:T(8,128)(2,1)S(1)}, bf16[1024,128]{1,0:T(8,128)(2,1)S(1)}, u32[]{:S(2)}, u32[]{:S(2)}) collective-permute-start(bf16[1024,128]{1,0:T(8,128)(2,1)S(1)} %bitcast.121), channel_id=1, source_target_pairs={{0,0},{1,4},{2,2},{3,6},{4,1},{5,5},{6,3},{7,7},{8,8},{9,12},{10,1... | collective-permute-start | bytes 786440 | tf_op jit(solution)/shard_map/ppermute | solution.py:356
  120.3 5.1 %collective-permute-start.30 = (bf16[512,128]{1,0:T(8,128)(2,1)S(1)}, bf16[512,128]{1,0:T(8,128)(2,1)S(1)}, u32[]{:S(2)}, u32[]{:S(2)}) collective-permute-start(bf16[512,128]{1,0:T(8,128)(2,1)S(1)} %get-tuple-element.28), channel_id=1, source_target_pairs={{0,4},{4,0},{8,12},{12,8},{16,20},{20,16},{24,28},{28,24},{32,36},... | collective-permute-start | bytes 393224 | tf_op jit(solution)/shard_map/ppermute | solution.py:356
  122.2 3.3 %collective-permute-start.28 = (bf16[512,128]{1,0:T(8,128)(2,1)S(1)}, bf16[512,128]{1,0:T(8,128)(2,1)S(1)}, u32[]{:S(2)}, u32[]{:S(2)}) collective-permute-start(bf16[512,128]{1,0:T(8,128)(2,1)S(1)} %get-tuple-element.30), channel_id=1, source_target_pairs={{0,4},{4,0},{8,12},{12,8},{16,20},{20,16},{24,28},{28,24},{32,36},... | collective-permute-start | bytes 393224 | tf_op jit(solution)/shard_map/ppermute | solution.py:356
  (5 other events, 6.2 us)
